TPU v7x, 128 devices: a whole 4x4x4 slice. The times are simulated.
128 devices in a mesh: row: 4 (over y), col: 16 (over x_hi, z, core), rep: 2 (over x_lo).
Axes of the slice: x: 4 (x_hi: 2, x_lo: 2; x = x_hi * 2 + x_lo), y: 4, z: 4, core: 2. Of those that a mesh axis runs over, the one named last changes fastest.
Arguments:
- features: bfloat16 [2, 128, 512, 512], P('rep', 'row', 'col'), may hold values from -6 to 6
- cotangent: bfloat16 [2, 128, 512, 512], P('rep', 'row', 'col'), may hold values from -6 to 6
- depthwise_filters: float32 [2, 7, 7, 512], replicated, may hold values from -0.875 to 0.875
- depthwise_bias_vector: float32 [2, 512], replicated, may hold values from -1.5 to 1.5
- layernorm_gain: float32 [2, 512], replicated, may hold values from 0.5 to 1.5
- layernorm_shift: float32 [2, 512], replicated, may hold values from -1.5 to 1.5
- inner_frozen_weight: bfloat16 [2, 512, 2048], replicated, may hold values from -0.25 to 0.25
- outer_frozen_weight: bfloat16 [2, 2048, 512], replicated, may hold values from -0.125 to 0.125
- inner_down_factor: bfloat16 [2, 512, 16], replicated, may hold values from -0.25 to 0.25
- inner_up_factor: bfloat16 [2, 16, 2048], replicated, may hold values from -0.75 to 0.75
- outer_down_factor: bfloat16 [2, 2048, 16], replicated, may hold values from -0.125 to 0.125
- outer_up_factor: bfloat16 [2, 16, 512], replicated, may hold values from -0.75 to 0.75
- branch_channel_scale: float32 [2, 512], replicated, may hold values from 0.2 to 1
Outputs:
- features_out: bfloat16 [2, 128, 512, 512], P('rep', 'row', 'col')
- step_a_in: float32 [2, 512, 16], replicated
- step_b_in: float32 [2, 16, 2048], replicated
- step_a_out: float32 [2, 2048, 16], replicated
- step_b_out: float32 [2, 16, 512], replicated
All inputs are finite; a program needn't handle non-finite values.
Results may differ from a plain program's by a relative error of at most 0.013.
Values may be sent and summed in bfloat16 or wider, within the bound.
No kernel may reach another device: no remote copies, remote signals or barrier semaphores. Data moves between devices by JAX's collectives and lax.ppermute only.
A program may use at most 128 MiB of HBM per device.

v0:
```python
import jax
import jax.numpy as jnp
from jax import lax
from jax.experimental import pallas as pl
from jax.experimental.pallas import tpu as pltpu
from jax.sharding import PartitionSpec as P

BLOCK_COUNT = 2
ROWS, COLS, CHANS, HIDDEN, RANK = 32, 32, 512, 2048, 16
PIXELS = ROWS * COLS
GROUPS = CHANS // 128
HALF = COLS // 2
SPAN = 32
OFFSET = 5
TILE = 256
CHUNK = 512

adapter_scale = 2.0
norm_eps = 1e-06
step_eps = 1e-06
gelu_coef = 0.7978845608
f32, bf16 = jnp.float32, jnp.bfloat16


def dot(a, b):
    return jnp.dot(a, b, preferred_element_type=f32)


def dot_t(a, b):
    return lax.dot_general(a, b, (((1,), (1,)), ((), ())), preferred_element_type=f32)


def t_dot(a, b):
    return lax.dot_general(a, b, (((0,), (0,)), ((), ())), preferred_element_type=f32)


def spread(xs, row, values, blocks):
    for k, g, half, at in blocks:
        start = (row * SPAN + at) * 8 + half * GROUPS + g
        xs[pl.ds(start, 8, stride=8), :] = values[8 * k : 8 * k + 8, 128 * g : 128 * g + 128]


CENTRE = [(k, g, 0, 8 * k + 8) for k in (0, 1, 2) for g in range(GROUPS)] + [
    (k, g, 1, 8 * k - 8) for k in (1, 2, 3) for g in range(GROUPS)
]


def fill(xs, x_ref, n_ref, s_ref, w_ref, e_ref):
    def centre(i, c):
        spread(xs, i + 3, x_ref[i].astype(f32), CENTRE)
        return c

    lax.fori_loop(0, ROWS, centre, 0)
    for i in range(3):
        spread(xs, i, n_ref[i].astype(f32), CENTRE)
        spread(xs, ROWS + 3 + i, s_ref[i].astype(f32), CENTRE)
    for side, half, at in ((w_ref, 0, OFFSET), (e_ref, 1, 3 + 16 + OFFSET)):
        for c in range(3):
            v = side[c].astype(f32)
            for r in range(0, 40, 8):
                for g in range(GROUPS):
                    start = (r * SPAN + at + c) * 8 + half * GROUPS + g
                    xs[pl.ds(start, 8, stride=8 * SPAN), :] = v[r : r + 8, 128 * g : 128 * g + 128]


def conv_row(xs, cv, taps, first, i):
    totals = [first] * HALF
    for a in range(7):
        base = pl.multiple_of((i + a) * (SPAN * 8), SPAN * 8)
        line = [xs[pl.ds(base + (OFFSET + c) * 8, 8), :] for c in range(HALF + 6)]
        for b in range(7):
            tap = taps[a * 7 + b]
            for c in range(HALF):
                totals[c] = totals[c] + line[c + b] * tap
    base = pl.multiple_of(i * (HALF * 8), HALF * 8)
    for c in range(HALF):
        cv[pl.ds(base + c * 8, 8), :] = totals[c]
    parts = []
    for k in range(4):
        start = base + (k % 2) * 64 + (k // 2) * GROUPS
        parts.append(
            jnp.concatenate([cv[pl.ds(start + g, 8, stride=8), :] for g in range(GROUPS)], axis=1)
        )
    return jnp.concatenate(parts, axis=0)


def gelu_parts(v):
    square = v * v
    t = jnp.tanh(v * (gelu_coef + (gelu_coef * 0.044715) * square))
    h = 0.5 * t + 0.5
    value = v * h
    slope = h + value * (1.0 - t) * (gelu_coef + (3.0 * 0.044715 * gelu_coef) * square)
    return value, slope


def row_of(i):
    return pl.ds(pl.multiple_of(i * COLS, COLS), COLS)


def norm_rows(xs, cv, taps, bias, gain, shift, nrm, xh=None, rs=None):
    def body(i, c):
        conv = conv_row(xs, cv, taps, bias[...], i)
        centred = conv - jnp.mean(conv, -1, keepdims=True)
        inverse = lax.rsqrt(jnp.mean(centred * centred, -1, keepdims=True) + norm_eps)
        standard = centred * inverse
        nrm[row_of(i), :] = (standard * gain[...] + shift[...]).astype(bf16)
        if xh is not None:
            xh[row_of(i), :] = standard
            rs[row_of(i), :] = jnp.broadcast_to(inverse, (COLS, 128))
        return c

    lax.fori_loop(0, ROWS, body, 0)


def tiles(body):
    def step(t, c):
        body(pl.ds(pl.multiple_of(t * TILE, TILE), TILE))
        return c

    lax.fori_loop(0, PIXELS // TILE, step, 0)


def fold_kernel(win, ain, bin_, wout, aout, bout, win_out, wout_out):
    win_out[0] = (win[0].astype(f32) + adapter_scale * dot(ain[0], bin_[0])).astype(bf16)
    wout_out[0] = (wout[0].astype(f32) + adapter_scale * dot(aout[0], bout[0])).astype(bf16)


def first_kernel(
    x, n, s, w, e, taps, bias, gain, shift, win, wout, ain, aout, scale,
    y, nrm, hid, slope, mid_in, mid_out, xs, cv,
):
    fill(xs, x, n, s, w, e)
    norm_rows(xs, cv, taps, bias, gain, shift, nrm)
    xf = x.reshape(PIXELS, CHANS)
    yf = y.reshape(PIXELS, CHANS)

    def body(at):
        nb = nrm[at, :]
        mid_in[at, :] = dot(nb, ain[...]).astype(bf16)
        out = jnp.zeros((TILE, CHANS), f32)
        mid = jnp.zeros((TILE, RANK), f32)
        for c in range(0, HIDDEN, CHUNK):
            cs = slice(c, c + CHUNK)
            value, sl = gelu_parts(dot(nb, win[:, cs]))
            h = value.astype(bf16)
            hid[at, cs] = h
            slope[at, cs] = sl.astype(bf16)
            out = out + dot(h, wout[cs, :])
            mid = mid + dot(h, aout[cs, :])
        mid_out[at, :] = mid.astype(bf16)
        yf[at, :] = (xf[at, :].astype(f32) + scale[...] * out).astype(bf16)

    tiles(body)


def second_kernel(
    x, n, s, w, e, cot, taps, bias, gain, shift, win, wout, ain, bin_, aout, bout, scale,
    y, gc, grads, xs, cv, nrm, xh, rs,
):
    fill(xs, x, n, s, w, e)
    norm_rows(xs, cv, taps, bias, gain, shift, nrm, xh, rs)
    xf = x.reshape(PIXELS, CHANS)
    yf = y.reshape(PIXELS, CHANS)
    cf = cot.reshape(PIXELS, CHANS)
    gf = gc.reshape(PIXELS, CHANS)
    grads[...] = jnp.zeros_like(grads)

    def body(at):
        nb = nrm[at, :]
        go = (cf[at, :].astype(f32) * scale[...]).astype(bf16)
        mid_in = dot(nb, ain[...]).astype(bf16)
        gm_out = (adapter_scale * dot_t(go, bout[...])).astype(bf16)
        out = jnp.zeros((TILE, CHANS), f32)
        gn = jnp.zeros((TILE, CHANS), f32)
        mid = jnp.zeros((TILE, RANK), f32)
        gm_in = jnp.zeros((TILE, RANK), f32)
        for c in range(0, HIDDEN, CHUNK):
            cs = slice(c, c + CHUNK)
            value, sl = gelu_parts(dot(nb, win[:, cs]))
            h = value.astype(bf16)
            gpre = (dot_t(go, wout[cs, :]) * sl).astype(bf16)
            out = out + dot(h, wout[cs, :])
            mid = mid + dot(h, aout[cs, :])
            gn = gn + dot_t(gpre, win[:, cs])
            gm_in = gm_in + dot_t(gpre, bin_[:, cs])
            grads[:, 512 + c : 512 + c + CHUNK] += t_dot(mid_in, gpre)
            grads[:, 2560 + c : 2560 + c + CHUNK] += t_dot(gm_out, h)
        gm_in = (adapter_scale * gm_in).astype(bf16)
        grads[:, 0:512] += t_dot(gm_in, nb)
        grads[:, 4608:5120] += t_dot(mid.astype(bf16), go)
        yf[at, :] = (xf[at, :].astype(f32) + scale[...] * out).astype(bf16)
        u = gn * gain[...]
        standard = xh[at, :]
        m1 = jnp.mean(u, -1, keepdims=True)
        m2 = jnp.mean(u * standard, -1, keepdims=True)
        inverse = jnp.concatenate([rs[at, :]] * GROUPS, axis=1)
        gf[at, :] = (inverse * (u - m1 - standard * m2)).astype(bf16)

    tiles(body)


def third_kernel(
    x, n, s, w, e, cot, taps, scale, wout, bin_, bout, nrm, hid, slope, mid_in, mid_out,
    grads, xs, cv, gos,
):
    fill(xs, x, n, s, w, e)
    zero = jnp.zeros((8, 128), f32)

    def rows(i, c):
        g = cot[i].astype(f32) + conv_row(xs, cv, taps, zero, i)
        gos[row_of(i), :] = (g * scale[...]).astype(bf16)
        return c

    lax.fori_loop(0, ROWS, rows, 0)
    grads[...] = jnp.zeros_like(grads)

    def body(at):
        nb = nrm[at, :]
        go = gos[at, :]
        mi = mid_in[at, :]
        gm_out = (adapter_scale * dot_t(go, bout[...])).astype(bf16)
        gm_in = jnp.zeros((TILE, RANK), f32)
        for c in range(0, HIDDEN, CHUNK):
            cs = slice(c, c + CHUNK)
            gpre = (dot_t(go, wout[cs, :]) * slope[at, cs].astype(f32)).astype(bf16)
            gm_in = gm_in + dot_t(gpre, bin_[:, cs])
            grads[:, 512 + c : 512 + c + CHUNK] += t_dot(mi, gpre)
            grads[:, 2560 + c : 2560 + c + CHUNK] += t_dot(gm_out, hid[at, cs])
        gm_in = (adapter_scale * gm_in).astype(bf16)
        grads[:, 0:512] += t_dot(gm_in, nb)
        grads[:, 4608:5120] += t_dot(mid_out[at, :], go)

    tiles(body)


VMEM = pl.BlockSpec(memory_space=pltpu.VMEM)
PARAMS = dict(compiler_params=pltpu.CompilerParams(vmem_limit_bytes=60 * 2**20))
XS = pltpu.VMEM((40 * SPAN * 8, 128), f32)
CV = pltpu.VMEM((ROWS * HALF * 8, 128), f32)


def call(kernel, outs, scratch, args, name):
    return pl.pallas_call(
        kernel,
        out_shape=[jax.ShapeDtypeStruct(shape, dtype) for shape, dtype in outs],
        in_specs=[VMEM] * len(args),
        out_specs=[VMEM] * len(outs),
        scratch_shapes=scratch,
        name=name,
        **PARAMS,
    )(*args)


def halo(x):
    def shift(v, axis):
        devices = lax.axis_size(axis)
        up = [(i, i + 1) for i in range(devices - 1)]
        return lambda first, last: (
            lax.ppermute(last, axis, up),
            lax.ppermute(first, axis, [(j, i) for i, j in up]),
        )

    north, south = shift(x, "row")(x[:3], x[-3:])
    zeros = jnp.zeros((2, 3, CHANS), x.dtype)

    def strip(cut):
        parts = [north[:, cut], x[:, cut], south[:, cut], zeros]
        return jnp.concatenate(parts, axis=0).transpose(1, 0, 2)

    west, east = shift(x, "col")(strip(slice(0, 3)), strip(slice(COLS - 3, COLS)))
    return x, north, south, west, east


def pair_swap(v, axis, mask):
    n = lax.axis_size(axis)
    return lax.ppermute(v, axis, [(i, i ^ mask) for i in range(n)])


def total(first, second):
    core = lax.axis_index("col") % 2
    mine = jnp.where(core == 0, first, second)
    other = jnp.where(core == 0, second, first).astype(bf16)
    part = (mine + pair_swap(other, "col", 1).astype(f32)).astype(bf16)
    for axis, mask in (("row", 1), ("row", 2), ("col", 2), ("col", 4), ("rep", 1), ("col", 8)):
        part = (part.astype(f32) + pair_swap(part, axis, mask).astype(f32)).astype(bf16)
    back = pair_swap(part, "col", 1)
    return jnp.stack([jnp.where(core == 0, part, back), jnp.where(core == 0, back, part)]).astype(f32)


def normalize(stacked):
    mean = jnp.mean(stacked * stacked, axis=(1, 2), keepdims=True)
    return stacked * lax.rsqrt(mean + step_eps)


def body(
    features,
    cotangent,
    depthwise_filters,
    depthwise_bias_vector,
    layernorm_gain,
    layernorm_shift,
    inner_frozen_weight,
    outer_frozen_weight,
    inner_down_factor,
    inner_up_factor,
    outer_down_factor,
    outer_up_factor,
    branch_channel_scale,
):
    x0 = features.reshape(ROWS, COLS, CHANS)
    cot = cotangent.reshape(ROWS, COLS, CHANS)
    taps = depthwise_filters.reshape(2, 49, GROUPS, 128)
    taps = jnp.concatenate([taps, taps], axis=2)
    bias = depthwise_bias_vector.reshape(2, GROUPS, 128)
    bias = jnp.concatenate([bias, bias], axis=1)
    gain, shift, scale = (
        v.reshape(2, 1, CHANS) for v in (layernorm_gain, layernorm_shift, branch_channel_scale)
    )
    halo0 = halo(x0)

    def whole(*shape):
        return pl.BlockSpec((1,) + shape, lambda i: (i, 0, 0))

    win, wout = pl.pallas_call(
        fold_kernel,
        grid=(2,),
        out_shape=[
            jax.ShapeDtypeStruct((2, CHANS, HIDDEN), bf16),
            jax.ShapeDtypeStruct((2, HIDDEN, CHANS), bf16),
        ],
        in_specs=[
            whole(CHANS, HIDDEN), whole(CHANS, RANK), whole(RANK, HIDDEN),
            whole(HIDDEN, CHANS), whole(HIDDEN, RANK), whole(RANK, CHANS),
        ],
        out_specs=[whole(CHANS, HIDDEN), whole(HIDDEN, CHANS)],
        name="fold",
        **PARAMS,
    )(
        inner_frozen_weight, inner_down_factor, inner_up_factor,
        outer_frozen_weight, outer_down_factor, outer_up_factor,
    )
    ain, bin_, aout, bout = inner_down_factor, inner_up_factor, outer_down_factor, outer_up_factor

    x1, nrm, hid, slope, mid_in, mid_out = call(
        first_kernel,
        [
            ((ROWS, COLS, CHANS), bf16),
            ((PIXELS, CHANS), bf16),
            ((PIXELS, HIDDEN), bf16),
            ((PIXELS, HIDDEN), bf16),
            ((PIXELS, RANK), bf16),
            ((PIXELS, RANK), bf16),
        ],
        [XS, CV],
        [*halo0, taps[0], bias[0], gain[0], shift[0], win[0], wout[0], ain[0], aout[0], scale[0]],
        "first",
    )
    out, gconv, grads1 = call(
        second_kernel,
        [((ROWS, COLS, CHANS), bf16), ((ROWS, COLS, CHANS), bf16), ((RANK, 5120), f32)],
        [
            XS,
            CV,
            pltpu.VMEM((PIXELS, CHANS), bf16),
            pltpu.VMEM((PIXELS, CHANS), f32),
            pltpu.VMEM((PIXELS, 128), f32),
        ],
        [
            *halo(x1), cot, taps[1], bias[1], gain[1], shift[1], win[1], wout[1],
            ain[1], bin_[1], aout[1], bout[1], scale[1],
        ],
        "second",
    )
    (grads0,) = call(
        third_kernel,
        [((RANK, 5120), f32)],
        [XS, CV, pltpu.VMEM((PIXELS, CHANS), bf16)],
        [
            *halo(gconv), cot, taps[1, ::-1], scale[0], wout[0], bin_[0], bout[0],
            nrm, hid, slope, mid_in, mid_out,
        ],
        "third",
    )
    sums = total(grads0, grads1)
    return (
        out[None],
        normalize(sums[:, :, 0:512].transpose(0, 2, 1)),
        normalize(adapter_scale * sums[:, :, 512:2560]),
        normalize(sums[:, :, 2560:4608].transpose(0, 2, 1)),
        normalize(adapter_scale * sums[:, :, 4608:5120]),
    )


def solution(mesh):
    tile = P("rep", "row", "col", None)
    return jax.shard_map(
        body,
        mesh=mesh,
        in_specs=(tile, tile) + (P(),) * 11,
        out_specs=(tile, P(), P(), P(), P()),
        check_vma=False,
    )
```

profile of v0, /device:TPU:1, one launch (start us, length us, event | category | flops | bytes accessed | tf_op | source)
XLA Modules:
  0.0 223.3 jit_solution(16353664566830967407)
XLA Ops:
  0.7 1.8 copy.75
  2.6 4.0 %collective-permute-start = (bf16[3,32,512]{2,0,1:T(4,128)(2,1)S(1)}, bf16[3,32,512]{2,0,1:T(4,128)(2,1)S(1)}, u32[]{:S(2)}, u32[]{:S(2)}) collective-permute-start(bf16[3,32,512]{2,0,1:T(4,128)(2,1)S(1)} %get-tuple-element.52), channel_id=1, source_target_pairs={{0,32},{32,64},{64,96},{1,33},{33,65},{65,97},{2,34},{34,66},{66,9... | collective-permute-start | bytes 294920 | tf_op jit(solution)/shard_map/ppermute | solution.py:259
  12.2 6.6 %fold.1 = (bf16[2,512,2048]{2,1,0:T(8,128)(2,1)}, bf16[2,2048,512]{2,1,0:T(8,128)(2,1)}) custom-call(bf16[2,512,2048]{2,1,0:T(8,128)(2,1)} %win.1, bf16[2,512,16]{2,1,0:T(8,128)(2,1)} %copy-done.2, bf16[2,16,2048]{2,1,0:T(8,128)(2,1)} %bin_.1, bf16[2,2048,512]{2,1,0:T(8,128)(2,1)} %wout.1, bf16[2,2048,16]{2,1,0:T(8,128)(2,1)} %copy-done, ...), custom_call_target="tpu_custom_call" | custom-call | tf_op jit(solution)/shard_map/fold/pallas_call | solution.py:324
  18.8 4.6 %slice_bitcast_fusion = (bf16[2048,512]{1,0:T(8,128)(2,1)}, bf16[2048,512]{1,0:T(8,128)(2,1)}) fusion(bf16[2,2048,512]{2,1,0:T(8,128)(2,1)} %get-tuple-element.17), kind=kLoop, calls=%fused_computation | loop fusion | bytes 8388608 | tf_op jit(solution)/shard_map/squeeze | solution.py:369
  23.4 2.5 %slice_bitcast_fusion.1 = (bf16[512,2048]{1,0:T(8,128)(2,1)}, bf16[512,2048]{1,0:T(8,128)(2,1)}) fusion(bf16[2,512,2048]{2,1,0:T(8,128)(2,1)S(1)} %copy-done.1), kind=kLoop, calls=%fused_computation.1 | loop fusion | bytes 8388608 | tf_op jit(solution)/shard_map/squeeze | solution.py:369
  27.3 4.4 %collective-permute-start.2 = (bf16[3,40,512]{2,1,0:T(8,128)(2,1)S(1)}, bf16[3,40,512]{2,1,0:T(8,128)(2,1)S(1)}, u32[]{:S(2)}, u32[]{:S(2)}) collective-permute-start(bf16[3,40,512]{2,1,0:T(8,128)(2,1)S(1)} %get-tuple-element.93), channel_id=1, source_target_pairs={{0,2},{2,4},{4,6},{6,8},{8,10},{10,12},{12,14},{14,16},{16,18},{18... | collective-permute-start | bytes 368648 | tf_op jit(solution)/shard_map/ppermute | solution.py:259
  31.7 1.9 collective-permute-start.3
  38.6 29.4 %first.1 = (bf16[32,32,512]{2,1,0:T(8,128)(2,1)}, bf16[1024,512]{1,0:T(8,128)(2,1)}, bf16[1024,2048]{1,0:T(8,128)(2,1)}, bf16[1024,2048]{1,0:T(8,128)(2,1)}, bf1...) custom-call(bf16[32,32,512]{2,1,0:T(8,128)(2,1)} %bitcast.73, bf16[3,32,512]{2,1,0:T(8,128)(2,1)} %copy.53.n, ...), custom_call_target="tpu_custom_call" | custom-call | tf_op jit(solution)/shard_map/first/pallas_call | solution.py:243
  68.0 1.8 copy.55
  69.9 4.3 %collective-permute-start.4 = (bf16[3,32,512]{2,0,1:T(4,128)(2,1)S(1)}, bf16[3,32,512]{2,0,1:T(4,128)(2,1)S(1)}, u32[]{:S(2)}, u32[]{:S(2)}) collective-permute-start(bf16[3,32,512]{2,0,1:T(4,128)(2,1)S(1)} %get-tuple-element.46), channel_id=1, source_target_pairs={{0,32},{32,64},{64,96},{1,33},{33,65},{65,97},{2,34},{34,66},{66,9... | collective-permute-start | bytes 294920 | tf_op jit(solution)/shard_map/ppermute | solution.py:259
  76.1 3.8 %collective-permute-done.5 = bf16[3,32,512]{2,0,1:T(4,128)(2,1)S(1)} collective-permute-done((bf16[3,32,512]{2,0,1:T(4,128)(2,1)S(1)}, bf16[3,32,512]{2,0,1:T(4,128)(2,1)S(1)}, u32[]{:S(2)}, u32[]{:S(2)}) %collective-permute-start.5) | collective-permute-done | bytes 98336 | tf_op jit(solution)/shard_map/ppermute | solution.py:260
  80.0 4.9 %collective-permute-start.6 = (bf16[3,40,512]{2,1,0:T(8,128)(2,1)S(1)}, bf16[3,40,512]{2,1,0:T(8,128)(2,1)S(1)}, u32[]{:S(2)}, u32[]{:S(2)}) collective-permute-start(bf16[3,40,512]{2,1,0:T(8,128)(2,1)S(1)} %get-tuple-element.91), channel_id=1, source_target_pairs={{0,2},{2,4},{4,6},{6,8},{8,10},{10,12},{12,14},{14,16},{16,18},{18... | collective-permute-start | bytes 368648 | tf_op jit(solution)/shard_map/ppermute | solution.py:259
  84.9 2.1 collective-permute-start.7
  89.0 2.2 collective-permute-done.7.e
  91.8 33.1 %second.1 = (bf16[32,32,512]{2,1,0:T(8,128)(2,1)}, bf16[32,32,512]{2,1,0:T(8,128)(2,1)}, f32[16,5120]{1,0:T(8,128)}) custom-call(bf16[32,32,512]{2,1,0:T(8,128)(2,1)} %get-tuple-element.18.x, bf16[3,32,512]{2,1,0:T(8,128)(2,1)} %copy.61.n, bf16[3,32,512]{2,1,0:T(8,128)(2,1)} %copy.62.s, bf16[3,40,512]{2,1,0:T(8,128)(2,1)} %copy-done.9, ...), custom_call_target="tpu_custom_call" | custom-call | tf_op jit(solution)/shard_map/second/pallas_call | solution.py:243
  124.9 1.8 copy.63
  126.8 3.3 %collective-permute-start.8 = (bf16[3,32,512]{2,0,1:T(4,128)(2,1)S(1)}, bf16[3,32,512]{2,0,1:T(4,128)(2,1)S(1)}, u32[]{:S(2)}, u32[]{:S(2)}) collective-permute-start(bf16[3,32,512]{2,0,1:T(4,128)(2,1)S(1)} %get-tuple-element.40), channel_id=1, source_target_pairs={{0,32},{32,64},{64,96},{1,33},{33,65},{65,97},{2,34},{34,66},{66,9... | collective-permute-start | bytes 294920 | tf_op jit(solution)/shard_map/ppermute | solution.py:259
  132.0 3.8 %collective-permute-done.9 = bf16[3,32,512]{2,0,1:T(4,128)(2,1)S(1)} collective-permute-done((bf16[3,32,512]{2,0,1:T(4,128)(2,1)S(1)}, bf16[3,32,512]{2,0,1:T(4,128)(2,1)S(1)}, u32[]{:S(2)}, u32[]{:S(2)}) %collective-permute-start.9) | collective-permute-done | bytes 98336 | tf_op jit(solution)/shard_map/ppermute | solution.py:260
  135.9 3.4 %collective-permute-start.10 = (bf16[3,40,512]{2,1,0:T(8,128)(2,1)S(1)}, bf16[3,40,512]{2,1,0:T(8,128)(2,1)S(1)}, u32[]{:S(2)}, u32[]{:S(2)}) collective-permute-start(bf16[3,40,512]{2,1,0:T(8,128)(2,1)S(1)} %get-tuple-element.89), channel_id=1, source_target_pairs={{0,2},{2,4},{4,6},{6,8},{8,10},{10,12},{12,14},{14,16},{16,18},{18... | collective-permute-start | bytes 368648 | tf_op jit(solution)/shard_map/ppermute | solution.py:259
  139.3 1.9 collective-permute-start.11
  143.3 2.2 %collective-permute-done.11.e = bf16[3,40,512]{2,1,0:T(8,128)(2,1)S(1)} collective-permute-done((bf16[3,40,512]{2,1,0:T(8,128)(2,1)S(1)}, bf16[3,40,512]{2,1,0:T(8,128)(2,1)S(1)}, u32[]{:S(2)}, u32[]{:S(2)}) %collective-permute-start.11) | collective-permute-done | bytes 122912 | tf_op jit(solution)/shard_map/ppermute | solution.py:260
  146.2 22.3 %third.1 = f32[16,5120]{1,0:T(8,128)} custom-call(bf16[32,32,512]{2,1,0:T(8,128)(2,1)} %get-tuple-element.20.x, bf16[3,32,512]{2,1,0:T(8,128)(2,1)} %copy.67.n, bf16[3,32,512]{2,1,0:T(8,128)(2,1)} %copy.68.s, bf16[3,40,512]{2,1,0:T(8,128)(2,1)} %copy-done.7, bf16[3,40,512]{2,1,0:T(8,128)(2,1)} %copy-done.8, bf16[32,32,512]{2,1,0:T(8,128)(2,1)} %bitcast.72, ...), custom_call_target="tpu_custom_call" | custom-call | tf_op jit(solution)/shard_map/third/pallas_call | solution.py:243
  169.6 1.4 collective-permute-done.12
  172.1 3.6 %collective-permute-done.13 = bf16[16,5120]{1,0:T(8,128)(2,1)S(1)} collective-permute-done((bf16[16,5120]{1,0:T(8,128)(2,1)S(1)}, bf16[16,5120]{1,0:T(8,128)(2,1)S(1)}, u32[]{:S(2)}, u32[]{:S(2)}) %collective-permute-start.13) | collective-permute-done | bytes 163872 | tf_op jit(solution)/shard_map/ppermute | solution.py:276
  176.7 4.9 %collective-permute-done.14 = bf16[16,5120]{1,0:T(8,128)(2,1)S(1)} collective-permute-done((bf16[16,5120]{1,0:T(8,128)(2,1)S(1)}, bf16[16,5120]{1,0:T(8,128)(2,1)S(1)}, u32[]{:S(2)}, u32[]{:S(2)}) %collective-permute-start.14) | collective-permute-done | bytes 163872 | tf_op jit(solution)/shard_map/ppermute | solution.py:276
  181.6 2.2 collective-permute-start.15
  183.8 2.7 %collective-permute-done.15 = bf16[16,5120]{1,0:T(8,128)(2,1)S(1)} collective-permute-done((bf16[16,5120]{1,0:T(8,128)(2,1)S(1)}, bf16[16,5120]{1,0:T(8,128)(2,1)S(1)}, u32[]{:S(2)}, u32[]{:S(2)}) %collective-permute-start.15) | collective-permute-done | bytes 163872 | tf_op jit(solution)/shard_map/ppermute | solution.py:276
  186.5 12.1 %collective-permute-start.16 = (bf16[16,5120]{1,0:T(8,128)(2,1)S(1)}, bf16[16,5120]{1,0:T(8,128)(2,1)S(1)}, u32[]{:S(2)}, u32[]{:S(2)}) collective-permute-start(bf16[16,5120]{1,0:T(8,128)(2,1)S(1)} %add_convert_fusion.3), channel_id=1, source_target_pairs={{0,8},{2,10},{4,12},{6,14},{8,0},{10,2},{12,4},{14,6},{16,24},{18,... | collective-permute-start | bytes 491528 | tf_op jit(solution)/shard_map/ppermute | solution.py:276
  198.6 3.7 %collective-permute-done.16 = bf16[16,5120]{1,0:T(8,128)(2,1)S(1)} collective-permute-done((bf16[16,5120]{1,0:T(8,128)(2,1)S(1)}, bf16[16,5120]{1,0:T(8,128)(2,1)S(1)}, u32[]{:S(2)}, u32[]{:S(2)}) %collective-permute-start.16) | collective-permute-done | bytes 163872 | tf_op jit(solution)/shard_map/ppermute | solution.py:276
  202.8 4.0 %collective-permute-done.17 = bf16[16,5120]{1,0:T(8,128)(2,1)S(1)} collective-permute-done((bf16[16,5120]{1,0:T(8,128)(2,1)S(1)}, bf16[16,5120]{1,0:T(8,128)(2,1)S(1)}, u32[]{:S(2)}, u32[]{:S(2)}) %collective-permute-start.17) | collective-permute-done | bytes 163872 | tf_op jit(solution)/shard_map/ppermute | solution.py:276
  206.9 6.0 %collective-permute-done.18 = bf16[16,5120]{1,0:T(8,128)(2,1)S(1)} collective-permute-done((bf16[16,5120]{1,0:T(8,128)(2,1)S(1)}, bf16[16,5120]{1,0:T(8,128)(2,1)S(1)}, u32[]{:S(2)}, u32[]{:S(2)}) %collective-permute-start.18) | collective-permute-done | bytes 163872 | tf_op jit(solution)/shard_map/ppermute | solution.py:276
  212.9 6.7 %collective-permute-start.19 = (bf16[16,5120]{1,0:T(8,128)(2,1)S(1)}, bf16[16,5120]{1,0:T(8,128)(2,1)S(1)}, u32[]{:S(2)}, u32[]{:S(2)}) collective-permute-start(bf16[16,5120]{1,0:T(8,128)(2,1)S(1)} %add_convert_fusion), channel_id=1, source_target_pairs={{0,2},{2,0},{4,6},{6,4},{8,10},{10,8},{12,14},{14,12},{16,18},{18,... | collective-permute-start | bytes 491528 | tf_op jit(solution)/shard_map/ppermute | solution.py:276
  (108 shorter events, 29.0 us)
Async XLA Ops:
  0.6 8.7 %copy-start.13 = (bf16[2,512,16]{1,2,0:T(8,128)(2,1)S(1)}, bf16[2,512,16]{1,2,0:T(8,128)(2,1)}, u32[]{:S(2)}) copy-start(bf16[2,512,16]{1,2,0:T(8,128)(2,1)} %param.21) | copy-start | bytes 98308
  0.6 10.9 %copy-start.4 = (bf16[2,16,2048]{2,1,0:T(8,128)(2,1)S(1)}, bf16[2,16,2048]{2,1,0:T(8,128)(2,1)}, u32[]{:S(2)}) copy-start(bf16[2,16,2048]{2,1,0:T(8,128)(2,1)} %bin_.1) | copy-start | bytes 393220
  2.6 24.6 %collective-permute-start = (bf16[3,32,512]{2,0,1:T(4,128)(2,1)S(1)}, bf16[3,32,512]{2,0,1:T(4,128)(2,1)S(1)}, u32[]{:S(2)}, u32[]{:S(2)}) collective-permute-start(bf16[3,32,512]{2,0,1:T(4,128)(2,1)S(1)} %get-tuple-element.52), channel_id=1, source_target_pairs={{0,32},{32,64},{64,96},{1,33},{33,65},{65,97},{2,34},{34,66},{66,9... | collective-permute-start | bytes 294920 | tf_op jit(solution)/shard_map/ppermute | solution.py:259
  6.7 20.5 %collective-permute-start.1 = (bf16[3,32,512]{2,0,1:T(4,128)(2,1)S(1)}, bf16[3,32,512]{2,0,1:T(4,128)(2,1)S(1)}, u32[]{:S(2)}, u32[]{:S(2)}) collective-permute-start(bf16[3,32,512]{2,0,1:T(4,128)(2,1)S(1)} %get-tuple-element.51), channel_id=1, source_target_pairs={{32,0},{64,32},{96,64},{33,1},{65,33},{97,65},{34,2},{66,34},{98,6... | collective-permute-start | bytes 294920 | tf_op jit(solution)/shard_map/ppermute | solution.py:260
  9.4 2.8 %copy-start = (bf16[2,2048,16]{2,1,0:T(8,128)(2,1)}, bf16[2,2048,16]{2,1,0:T(8,128)(2,1)S(1)}, u32[]{:S(2)}) copy-start(bf16[2,2048,16]{2,1,0:T(8,128)(2,1)S(1)} %copy.49.aout) | copy-start | bytes 393220
  9.6 2.6 %copy-start.2 = (bf16[2,512,16]{2,1,0:T(8,128)(2,1)}, bf16[2,512,16]{2,1,0:T(8,128)(2,1)S(1)}, u32[]{:S(2)}) copy-start(bf16[2,512,16]{2,1,0:T(8,128)(2,1)S(1)} %copy.48.ain) | copy-start | bytes 98308
  18.8 4.6 %copy-start.1 = (bf16[2,512,2048]{2,1,0:T(8,128)(2,1)S(1)}, bf16[2,512,2048]{2,1,0:T(8,128)(2,1)}, u32[]{:S(2)}) copy-start(bf16[2,512,2048]{2,1,0:T(8,128)(2,1)} %get-tuple-element.16) | copy-start | bytes 12582916
  23.4 2.5 %copy-start.16 = (f32[2,512]{1,0:T(2,128)S(1)}, f32[2,512]{1,0:T(2,128)}, u32[]{:S(2)}) copy-start(f32[2,512]{1,0:T(2,128)} %param.25) | copy-start | bytes 12292
  23.4 2.5 %copy-start.17 = (f32[2,512]{1,0:T(2,128)S(1)}, f32[2,512]{1,0:T(2,128)}, u32[]{:S(2)}) copy-start(f32[2,512]{1,0:T(2,128)} %param.18) | copy-start | bytes 12292
  23.4 3.1 %copy-start.14 = (f32[2,512]{1,0:T(2,128)S(1)}, f32[2,512]{1,0:T(2,128)}, u32[]{:S(2)}) copy-start(f32[2,512]{1,0:T(2,128)} %param.17) | copy-start | bytes 12292
  23.4 3.7 %copy-start.15 = (f32[2,512]{1,0:T(2,128)S(1)}, f32[2,512]{1,0:T(2,128)}, u32[]{:S(2)}) copy-start(f32[2,512]{1,0:T(2,128)} %param.16) | copy-start | bytes 12292
  23.4 10.9 %copy-start.5 = (f32[2,7,7,512]{3,0,2,1:T(2,128)S(1)}, f32[2,7,7,512]{3,0,2,1:T(2,128)}, u32[]{:S(2)}) copy-start(f32[2,7,7,512]{3,0,2,1:T(2,128)} %param.15) | copy-start | bytes 602116
  27.3 9.3 %collective-permute-start.2 = (bf16[3,40,512]{2,1,0:T(8,128)(2,1)S(1)}, bf16[3,40,512]{2,1,0:T(8,128)(2,1)S(1)}, u32[]{:S(2)}, u32[]{:S(2)}) collective-permute-start(bf16[3,40,512]{2,1,0:T(8,128)(2,1)S(1)} %get-tuple-element.93), channel_id=1, source_target_pairs={{0,2},{2,4},{4,6},{6,8},{8,10},{10,12},{12,14},{14,16},{16,18},{18... | collective-permute-start | bytes 368648 | tf_op jit(solution)/shard_map/ppermute | solution.py:259
  31.7 6.2 %collective-permute-start.3 = (bf16[3,40,512]{2,1,0:T(8,128)(2,1)S(1)}, bf16[3,40,512]{2,1,0:T(8,128)(2,1)S(1)}, u32[]{:S(2)}, u32[]{:S(2)}) collective-permute-start(bf16[3,40,512]{2,1,0:T(8,128)(2,1)S(1)} %get-tuple-element.92), channel_id=1, source_target_pairs={{2,0},{4,2},{6,4},{8,6},{10,8},{12,10},{14,12},{16,14},{18,16},{20... | collective-permute-start | bytes 368648 | tf_op jit(solution)/shard_map/ppermute | solution.py:260
  38.6 48.4 %copy-start.6 = (bf16[2,16,512]{2,1,0:T(8,128)(2,1)S(1)}, bf16[2,16,512]{2,1,0:T(8,128)(2,1)}, u32[]{:S(2)}) copy-start(bf16[2,16,512]{2,1,0:T(8,128)(2,1)} %bout.1) | copy-start | bytes 98308
  69.9 6.2 %collective-permute-start.4 = (bf16[3,32,512]{2,0,1:T(4,128)(2,1)S(1)}, bf16[3,32,512]{2,0,1:T(4,128)(2,1)S(1)}, u32[]{:S(2)}, u32[]{:S(2)}) collective-permute-start(bf16[3,32,512]{2,0,1:T(4,128)(2,1)S(1)} %get-tuple-element.46), channel_id=1, source_target_pairs={{0,32},{32,64},{64,96},{1,33},{33,65},{65,97},{2,34},{34,66},{66,9... | collective-permute-start | bytes 294920 | tf_op jit(solution)/shard_map/ppermute | solution.py:259
  74.2 5.7 %collective-permute-start.5 = (bf16[3,32,512]{2,0,1:T(4,128)(2,1)S(1)}, bf16[3,32,512]{2,0,1:T(4,128)(2,1)S(1)}, u32[]{:S(2)}, u32[]{:S(2)}) collective-permute-start(bf16[3,32,512]{2,0,1:T(4,128)(2,1)S(1)} %get-tuple-element.45), channel_id=1, source_target_pairs={{32,0},{64,32},{96,64},{33,1},{65,33},{97,65},{34,2},{66,34},{98,6... | collective-permute-start | bytes 294920 | tf_op jit(solution)/shard_map/ppermute | solution.py:260
  80.0 8.9 %collective-permute-start.6 = (bf16[3,40,512]{2,1,0:T(8,128)(2,1)S(1)}, bf16[3,40,512]{2,1,0:T(8,128)(2,1)S(1)}, u32[]{:S(2)}, u32[]{:S(2)}) collective-permute-start(bf16[3,40,512]{2,1,0:T(8,128)(2,1)S(1)} %get-tuple-element.91), channel_id=1, source_target_pairs={{0,2},{2,4},{4,6},{6,8},{8,10},{10,12},{12,14},{14,16},{16,18},{18... | collective-permute-start | bytes 368648 | tf_op jit(solution)/shard_map/ppermute | solution.py:259
  84.9 6.2 %collective-permute-start.7 = (bf16[3,40,512]{2,1,0:T(8,128)(2,1)S(1)}, bf16[3,40,512]{2,1,0:T(8,128)(2,1)S(1)}, u32[]{:S(2)}, u32[]{:S(2)}) collective-permute-start(bf16[3,40,512]{2,1,0:T(8,128)(2,1)S(1)} %get-tuple-element.90), channel_id=1, source_target_pairs={{2,0},{4,2},{6,4},{8,6},{10,8},{12,10},{14,12},{16,14},{18,16},{20... | collective-permute-start | bytes 368648 | tf_op jit(solution)/shard_map/ppermute | solution.py:260
  126.8 5.2 %collective-permute-start.8 = (bf16[3,32,512]{2,0,1:T(4,128)(2,1)S(1)}, bf16[3,32,512]{2,0,1:T(4,128)(2,1)S(1)}, u32[]{:S(2)}, u32[]{:S(2)}) collective-permute-start(bf16[3,32,512]{2,0,1:T(4,128)(2,1)S(1)} %get-tuple-element.40), channel_id=1, source_target_pairs={{0,32},{32,64},{64,96},{1,33},{33,65},{65,97},{2,34},{34,66},{66,9... | collective-permute-start | bytes 294920 | tf_op jit(solution)/shard_map/ppermute | solution.py:259
  130.1 5.7 %collective-permute-start.9 = (bf16[3,32,512]{2,0,1:T(4,128)(2,1)S(1)}, bf16[3,32,512]{2,0,1:T(4,128)(2,1)S(1)}, u32[]{:S(2)}, u32[]{:S(2)}) collective-permute-start(bf16[3,32,512]{2,0,1:T(4,128)(2,1)S(1)} %get-tuple-element.39), channel_id=1, source_target_pairs={{32,0},{64,32},{96,64},{33,1},{65,33},{97,65},{34,2},{66,34},{98,6... | collective-permute-start | bytes 294920 | tf_op jit(solution)/shard_map/ppermute | solution.py:260
  135.9 7.4 %collective-permute-start.10 = (bf16[3,40,512]{2,1,0:T(8,128)(2,1)S(1)}, bf16[3,40,512]{2,1,0:T(8,128)(2,1)S(1)}, u32[]{:S(2)}, u32[]{:S(2)}) collective-permute-start(bf16[3,40,512]{2,1,0:T(8,128)(2,1)S(1)} %get-tuple-element.89), channel_id=1, source_target_pairs={{0,2},{2,4},{4,6},{6,8},{8,10},{10,12},{12,14},{14,16},{16,18},{18... | collective-permute-start | bytes 368648 | tf_op jit(solution)/shard_map/ppermute | solution.py:259
  139.3 6.2 %collective-permute-start.11 = (bf16[3,40,512]{2,1,0:T(8,128)(2,1)S(1)}, bf16[3,40,512]{2,1,0:T(8,128)(2,1)S(1)}, u32[]{:S(2)}, u32[]{:S(2)}) collective-permute-start(bf16[3,40,512]{2,1,0:T(8,128)(2,1)S(1)} %get-tuple-element.88), channel_id=1, source_target_pairs={{2,0},{4,2},{6,4},{8,6},{10,8},{12,10},{14,12},{16,14},{18,16},{20... | collective-permute-start | bytes 368648 | tf_op jit(solution)/shard_map/ppermute | solution.py:260
  146.2 22.3 %copy-start.3 = (f32[16,5120]{1,0:T(8,128)S(1)}, f32[16,5120]{1,0:T(8,128)}, u32[]{:S(2)}) copy-start(f32[16,5120]{1,0:T(8,128)} %get-tuple-element.26) | copy-start | bytes 983044
  169.5 1.5 collective-permute-start.12
  171.1 4.7 %collective-permute-start.13 = (bf16[16,5120]{1,0:T(8,128)(2,1)S(1)}, bf16[16,5120]{1,0:T(8,128)(2,1)S(1)}, u32[]{:S(2)}, u32[]{:S(2)}) collective-permute-start(bf16[16,5120]{1,0:T(8,128)(2,1)S(1)} %add_convert_fusion.6), channel_id=1, source_target_pairs={{0,32},{32,0},{64,96},{96,64},{1,33},{33,1},{65,97},{97,65},{2,34}... | collective-permute-start | bytes 491528 | tf_op jit(solution)/shard_map/ppermute | solution.py:276
  175.8 5.8 %collective-permute-start.14 = (bf16[16,5120]{1,0:T(8,128)(2,1)S(1)}, bf16[16,5120]{1,0:T(8,128)(2,1)S(1)}, u32[]{:S(2)}, u32[]{:S(2)}) collective-permute-start(bf16[16,5120]{1,0:T(8,128)(2,1)S(1)} %add_convert_fusion.5), channel_id=1, source_target_pairs={{0,64},{32,96},{64,0},{96,32},{1,65},{33,97},{65,1},{97,33},{2,66}... | collective-permute-start | bytes 491528 | tf_op jit(solution)/shard_map/ppermute | solution.py:276
  181.6 4.9 %collective-permute-start.15 = (bf16[16,5120]{1,0:T(8,128)(2,1)S(1)}, bf16[16,5120]{1,0:T(8,128)(2,1)S(1)}, u32[]{:S(2)}, u32[]{:S(2)}) collective-permute-start(bf16[16,5120]{1,0:T(8,128)(2,1)S(1)} %add_convert_fusion.4), channel_id=1, source_target_pairs={{0,4},{2,6},{4,0},{6,2},{8,12},{10,14},{12,8},{14,10},{16,20},{18,... | collective-permute-start | bytes 491528 | tf_op jit(solution)/shard_map/ppermute | solution.py:276
  186.5 15.8 %collective-permute-start.16 = (bf16[16,5120]{1,0:T(8,128)(2,1)S(1)}, bf16[16,5120]{1,0:T(8,128)(2,1)S(1)}, u32[]{:S(2)}, u32[]{:S(2)}) collective-permute-start(bf16[16,5120]{1,0:T(8,128)(2,1)S(1)} %add_convert_fusion.3), channel_id=1, source_target_pairs={{0,8},{2,10},{4,12},{6,14},{8,0},{10,2},{12,4},{14,6},{16,24},{18,... | collective-permute-start | bytes 491528 | tf_op jit(solution)/shard_map/ppermute | solution.py:276
  202.4 4.3 %collective-permute-start.17 = (bf16[16,5120]{1,0:T(8,128)(2,1)S(1)}, bf16[16,5120]{1,0:T(8,128)(2,1)S(1)}, u32[]{:S(2)}, u32[]{:S(2)}) collective-permute-start(bf16[16,5120]{1,0:T(8,128)(2,1)S(1)} %add_convert_fusion.2), channel_id=1, source_target_pairs={{0,1},{1,0},{2,3},{3,2},{4,5},{5,4},{6,7},{7,6},{8,9},{9,8},{10,11... | collective-permute-start | bytes 491528 | tf_op jit(solution)/shard_map/ppermute | solution.py:276
  206.8 6.1 %collective-permute-start.18 = (bf16[16,5120]{1,0:T(8,128)(2,1)S(1)}, bf16[16,5120]{1,0:T(8,128)(2,1)S(1)}, u32[]{:S(2)}, u32[]{:S(2)}) collective-permute-start(bf16[16,5120]{1,0:T(8,128)(2,1)S(1)} %add_convert_fusion.1), channel_id=1, source_target_pairs={{0,16},{2,18},{4,20},{6,22},{8,24},{10,26},{12,28},{14,30},{16,0},... | collective-permute-start | bytes 491528 | tf_op jit(solution)/shard_map/ppermute | solution.py:276
  212.9 7.8 %collective-permute-start.19 = (bf16[16,5120]{1,0:T(8,128)(2,1)S(1)}, bf16[16,5120]{1,0:T(8,128)(2,1)S(1)}, u32[]{:S(2)}, u32[]{:S(2)}) collective-permute-start(bf16[16,5120]{1,0:T(8,128)(2,1)S(1)} %add_convert_fusion), channel_id=1, source_target_pairs={{0,2},{2,0},{4,6},{6,4},{8,10},{10,8},{12,14},{14,12},{16,18},{18,... | collective-permute-start | bytes 491528 | tf_op jit(solution)/shard_map/ppermute | solution.py:276
  (6 other events, 7.7 us)
where the time goes:
time: 224 us; the launch traced here: 223 us
  Pallas kernels  91.4 us (41%)
  starting transfers between devices  57.7 us (26%)
  waiting for transfers between devices  41.7 us (19%)
  local copies, waits for them, and re-layouts  25.8 us (12%)
  other arithmetic  5.72 us (3%)
    pallas_call x3, Pallas kernels, call(): pl.pallas_call(kernel, out_shape=[jax.ShapeDtypeStruct(shape, dtype) for...  84.8 us
    ppermute x8, waiting for transfers between devices, pair_swap(): return lax.ppermute(v, axis, [(i, i ^ mask) for i in range(n)])  27.2 us
    ppermute x6, starting transfers between devices, shift(): lax.ppermute(last, axis, up)  24.3 us
    ppermute x8, starting transfers between devices, pair_swap(): return lax.ppermute(v, axis, [(i, i ^ mask) for i in range(n)])  23.6 us
    ppermute x6, waiting for transfers between devices, shift(): lax.ppermute(first, axis, [(j, i) for i, j in up])  13.3 us
    ppermute x6, starting transfers between devices, shift(): lax.ppermute(first, axis, [(j, i) for i, j in up])  9.82 us
    pallas_call x1, Pallas kernels, body(): pl.pallas_call(fold_kernel, grid=(2,), out_shape=[jax.ShapeDtypeStruct((2...  6.58 us
    unnamed x39, local copies, waits for them, and re-layouts  5.4 us
  transfers between devices with their start and end apart: 20, of which 15 were waited for; matrix products, arithmetic and copies ran while one was open for 9% of the time, Pallas kernels for 3%

commit v1 on v0

v1 whole, which is shorter than its diff:
```python
import functools

import jax
import jax.numpy as jnp
from jax import lax
from jax.experimental import pallas as pl
from jax.experimental.pallas import tpu as pltpu
from jax.sharding import PartitionSpec as P

BLOCK_COUNT = 2
ROWS, COLS, CHANS, HIDDEN, RANK = 32, 32, 512, 2048, 16
PIXELS = ROWS * COLS
GROUPS = CHANS // 128
HALF = COLS // 2
SPAN = 32
OFFSET = 5
TROWS = 8
TILE = TROWS * COLS
CHUNK = 512
STRIP = 48
GRADS = 2 * (CHANS + HIDDEN)

adapter_scale = 2.0
norm_eps = 1e-06
step_eps = 1e-06
gelu_coef = 0.7978845608
f32, bf16 = jnp.float32, jnp.bfloat16


def dot(a, b):
    return jnp.dot(a, b, preferred_element_type=f32)


def dot_t(a, b):
    return lax.dot_general(a, b, (((1,), (1,)), ((), ())), preferred_element_type=f32)


def t_dot(a, b):
    return lax.dot_general(a, b, (((0,), (0,)), ((), ())), preferred_element_type=f32)


CENTRE = [(k, g, 0, 8 * k + 8) for k in (0, 1, 2) for g in range(GROUPS)] + [
    (k, g, 1, 8 * k - 8) for k in (1, 2, 3) for g in range(GROUPS)
]


def spread(xs, row, values):
    for k, g, half, at in CENTRE:
        start = (row * SPAN + at) * 8 + half * GROUPS + g
        xs[pl.ds(start, 8, stride=8), :] = values[8 * k : 8 * k + 8, 128 * g : 128 * g + 128]


def conv_kernel(sources, flip, flags, *refs):
    xrefs, (n, s, taps, bias, cv, xs) = refs[: len(sources)], refs[len(sources) :]
    step = pl.program_id(0)

    @pl.when(step == 0)
    def _():
        zero = jnp.zeros((8, 128), f32)
        for ref, pieces in zip(xrefs, sources):
            for at, row, count in pieces:

                def centre(i, c, ref=ref, at=at, row=row):
                    spread(xs, row + 3 + i, ref[at + i].astype(f32))
                    return c

                lax.fori_loop(0, count, centre, 0)
        for i in range(3):
            spread(xs, i, n[i].astype(f32) * flags[0])
            spread(xs, ROWS + 3 + i, s[i].astype(f32) * flags[1])
        left = lax.broadcasted_iota(jnp.int32, (8, 128), 0) < GROUPS

        def edge(r, c):
            for k in (5, 6, 7):
                at = pl.ds(pl.multiple_of((r * SPAN + k) * 8, 8), 8)
                xs[at, :] = jnp.where(left, zero, xs[at, :])
            for k in (24, 25, 26):
                at = pl.ds(pl.multiple_of((r * SPAN + k) * 8, 8), 8)
                xs[at, :] = jnp.where(left, xs[at, :], zero)
            return c

        lax.fori_loop(0, ROWS + 6, edge, 0)

    def row(i, c):
        first = jnp.zeros((8, 128), f32) if flip else bias[...]
        totals = [first] * HALF
        for a in range(7):
            base = pl.multiple_of((step * TROWS + i + a) * (SPAN * 8), SPAN * 8)
            line = [xs[pl.ds(base + (OFFSET + k) * 8, 8), :] for k in range(HALF + 6)]
            for b in range(7):
                tap = taps[48 - (a * 7 + b) if flip else a * 7 + b]
                for k in range(HALF):
                    totals[k] = totals[k] + line[k + b] * tap
        base = pl.multiple_of(i * (HALF * 8), HALF * 8)
        for k in range(HALF):
            cv[pl.ds(base + k * 8, 8), :] = totals[k]
        return c

    lax.fori_loop(0, TROWS, row, 0)


def hold_strips(he, w, e, flags):
    he[...] = jnp.zeros_like(he)
    for side, ref in ((0, w), (1, e)):
        for c in range(3):
            for block, row in ((4, 0), (5, 35), (0, 3), (2, 11), (3, 19), (1, 27)):
                v = ref[c, 8 * block : 8 * block + 8, :].astype(f32) * flags[2 + side]
                if block >= 4:
                    v = v * flags[block - 4]
                if block == 5:
                    v = v[0:3]
                for g in range(GROUPS):
                    start = (row * 6 + side * 3 + c) * 8 + side * GROUPS + g
                    he[pl.ds(start, v.shape[0], stride=48), :] = v[:, 128 * g : 128 * g + 128]


def whole_row(cv, he, taps, flip, line, tile, i):
    base = pl.multiple_of(i * (HALF * 8), HALF * 8)
    totals = [cv[pl.ds(base + k * 8, 8), :] for k in range(HALF)]
    for a in range(7):
        at = pl.multiple_of((tile * TROWS + i + a) * 48, 48)
        edge = [he[pl.ds(at + 8 * k, 8), :] for k in range(6)]
        pairs = [(k, h, h - k) for k in range(3) for h in range(k, 3)]
        pairs += [(k, 3 + h, 19 + h - k) for k in (13, 14, 15) for h in range(k - 12)]
        for k, h, b in pairs:
            totals[k] = totals[k] + edge[h] * taps[48 - (a * 7 + b) if flip else a * 7 + b]
    for k in range(HALF):
        line[k * 8 : k * 8 + 8, :] = totals[k]
    parts = []
    for k in range(4):
        start = (k % 2) * 64 + (k // 2) * GROUPS
        parts.append(
            jnp.concatenate([line[pl.ds(start + g, 8, stride=8), :] for g in range(GROUPS)], axis=1)
        )
    return jnp.concatenate(parts, axis=0)


def gelu_parts(v):
    square = v * v
    t = jnp.tanh(v * (gelu_coef + (gelu_coef * 0.044715) * square))
    h = 0.5 * t + 0.5
    value = v * h
    slope = h + value * (1.0 - t) * (gelu_coef + (3.0 * 0.044715 * gelu_coef) * square)
    return value, slope


def row_of(i):
    return pl.ds(pl.multiple_of(i * COLS, COLS), COLS)


def norm_rows(cv, he, taps, line, tile, gain, shift, nrm, xh=None, rs=None):
    def body(i, c):
        conv = whole_row(cv, he, taps, False, line, tile, i)
        centred = conv - jnp.mean(conv, -1, keepdims=True)
        inverse = lax.rsqrt(jnp.mean(centred * centred, -1, keepdims=True) + norm_eps)
        standard = centred * inverse
        nrm[row_of(i), :] = (standard * gain[...] + shift[...]).astype(bf16)
        if xh is not None:
            xh[row_of(i), :] = standard
            rs[row_of(i), :] = jnp.broadcast_to(inverse, (COLS, 128))
        return c

    lax.fori_loop(0, TROWS, body, 0)


def put_edges(edge, value, refs, step, inner):
    west, east = refs[-2:]
    if not inner:
        top, bottom = refs[:2]

        @pl.when(step == 0)
        def _():
            top[...] = value[: 3 * COLS].reshape(3, COLS, CHANS).astype(bf16)

        @pl.when(step == 1)
        def _():
            bottom[...] = value[5 * COLS :].reshape(3, COLS, CHANS).astype(bf16)

    for g in range(GROUPS):
        cs = slice(128 * g, 128 * g + 128)
        edge[...] = value[:, cs]
        for c in range(3):
            at = pl.ds(pl.multiple_of(step * 8, 8), 8)
            west[c, at, cs] = edge[pl.ds(c, 8, stride=COLS), :].astype(bf16)
            east[c, at, cs] = edge[pl.ds(COLS - 3 + c, 8, stride=COLS), :].astype(bf16)


def fold_kernel(win, ain, bin_, wout, aout, bout, win_out, wout_out):
    win_out[...] = (win[...].astype(f32) + adapter_scale * dot(ain[...], bin_[...])).astype(bf16)
    wout_out[...] = (wout[...].astype(f32) + adapter_scale * dot(aout[...], bout[...])).astype(bf16)


def first_kernel(inner, flags, x, cv, w, e, taps, gain, shift, win, wout, ain, aout, scale, *refs):
    refs = refs[5 if inner else 0 :]
    nrm, hid, slope, mid_in, mid_out, y = refs[:6]
    edges, (he, line, edge) = refs[6:-3], refs[-3:]
    step = pl.program_id(0)
    tile = step + 1 if inner else 3 * step

    @pl.when(step == 0)
    def _():
        hold_strips(he, w, e, flags)

    norm_rows(cv, he, taps, line, tile, gain, shift, nrm)
    nb = nrm[...]
    mid_in[...] = dot(nb, ain[...]).astype(bf16)
    out = jnp.zeros((TILE, CHANS), f32)
    mid = jnp.zeros((TILE, RANK), f32)
    for c in range(0, HIDDEN, CHUNK):
        cs = slice(c, c + CHUNK)
        value, sl = gelu_parts(dot(nb, win[:, cs]))
        h = value.astype(bf16)
        hid[:, cs] = h
        slope[:, cs] = sl.astype(bf16)
        out = out + dot(h, wout[cs, :])
        mid = mid + dot(h, aout[cs, :])
    mid_out[...] = mid.astype(bf16)
    result = x[...].reshape(TILE, CHANS).astype(f32) + scale[...] * out
    y[...] = result.reshape(TROWS, COLS, CHANS).astype(bf16)
    put_edges(edge, result, edges, step, inner)


def second_kernel(
    inner, flags, x, cv, w, e, taps, gain, shift, win, wout, ain, bin_, aout, bout, scale, cot, *refs
):
    if inner:
        before, refs = refs[1], refs[2:]
    out_ref, grads, gc = refs[:3]
    edges, (he, line, edge, nrm, xh, rs) = refs[3:-6], refs[-6:]
    step = pl.program_id(0)
    tile = step + 1 if inner else 3 * step

    @pl.when(step == 0)
    def _():
        hold_strips(he, w, e, flags)
        grads[...] = before[...] if inner else jnp.zeros_like(grads)

    norm_rows(cv, he, taps, line, tile, gain, shift, nrm, xh, rs)
    nb = nrm[...]
    go = (cot[...].reshape(TILE, CHANS).astype(f32) * scale[...]).astype(bf16)
    mid_in = dot(nb, ain[...]).astype(bf16)
    gm_out = (adapter_scale * dot_t(go, bout[...])).astype(bf16)
    out = jnp.zeros((TILE, CHANS), f32)
    gn = jnp.zeros((TILE, CHANS), f32)
    mid = jnp.zeros((TILE, RANK), f32)
    gm_in = jnp.zeros((TILE, RANK), f32)
    for c in range(0, HIDDEN, CHUNK):
        cs = slice(c, c + CHUNK)
        value, sl = gelu_parts(dot(nb, win[:, cs]))
        h = value.astype(bf16)
        gpre = (dot_t(go, wout[cs, :]) * sl).astype(bf16)
        out = out + dot(h, wout[cs, :])
        mid = mid + dot(h, aout[cs, :])
        gn = gn + dot_t(gpre, win[:, cs])
        gm_in = gm_in + dot_t(gpre, bin_[:, cs])
        grads[:, 512 + c : 512 + c + CHUNK] += t_dot(mid_in, gpre)
        grads[:, 2560 + c : 2560 + c + CHUNK] += t_dot(gm_out, h)
    gm_in = (adapter_scale * gm_in).astype(bf16)
    grads[:, 0:512] += t_dot(gm_in, nb)
    grads[:, 4608:5120] += t_dot(mid.astype(bf16), go)
    result = x[...].reshape(TILE, CHANS).astype(f32) + scale[...] * out
    out_ref[...] = result.reshape(TROWS, COLS, CHANS).astype(bf16)
    u = gn * gain[...]
    standard = xh[...]
    m1 = jnp.mean(u, -1, keepdims=True)
    m2 = jnp.mean(u * standard, -1, keepdims=True)
    inverse = jnp.concatenate([rs[...]] * GROUPS, axis=1)
    result = inverse * (u - m1 - standard * m2)
    gc[...] = result.reshape(TROWS, COLS, CHANS).astype(bf16)
    put_edges(edge, result, edges, step, inner)


def third_kernel(
    flags, cot, cv, w, e, taps, scale, wout, bin_, bout, nrm, hid, slope, mid_in, mid_out,
    grads, he, line, gos,
):
    step = pl.program_id(0)

    @pl.when(step == 0)
    def _():
        hold_strips(he, w, e, flags)
        grads[...] = jnp.zeros_like(grads)

    def rows(i, c):
        g = cot[i].astype(f32) + whole_row(cv, he, taps, True, line, step, i)
        gos[row_of(i), :] = (g * scale[...]).astype(bf16)
        return c

    lax.fori_loop(0, TROWS, rows, 0)
    nb = nrm[...]
    go = gos[...]
    mi = mid_in[...]
    gm_out = (adapter_scale * dot_t(go, bout[...])).astype(bf16)
    gm_in = jnp.zeros((TILE, RANK), f32)
    for c in range(0, HIDDEN, CHUNK):
        cs = slice(c, c + CHUNK)
        gpre = (dot_t(go, wout[cs, :]) * slope[:, cs].astype(f32)).astype(bf16)
        gm_in = gm_in + dot_t(gpre, bin_[:, cs])
        grads[:, 512 + c : 512 + c + CHUNK] += t_dot(mi, gpre)
        grads[:, 2560 + c : 2560 + c + CHUNK] += t_dot(gm_out, hid[:, cs])
    gm_in = (adapter_scale * gm_in).astype(bf16)
    grads[:, 0:512] += t_dot(gm_in, nb)
    grads[:, 4608:5120] += t_dot(mid_out[...], go)


PARAMS = dict(compiler_params=pltpu.CompilerParams(vmem_limit_bytes=60 * 2**20))
SMEM = pl.BlockSpec(memory_space=pltpu.SMEM)
ANY = pl.BlockSpec(memory_space=pl.ANY)
HE = pltpu.VMEM((40 * 48, 128), f32)
LINE = pltpu.VMEM((HALF * 8, 128), f32)
EDGE = pltpu.VMEM((TILE, 128), f32)


def fixed(*shape):
    return pl.BlockSpec(shape, lambda t: (0,) * len(shape))


def layer(l, *shape):
    return pl.BlockSpec((None,) + shape, lambda t: (l,) + (0,) * len(shape))


def tiled(place, *shape):
    return pl.BlockSpec(shape, lambda t: (place(t),) + (0,) * (len(shape) - 1))


def call(kernel, name, grid, ins, outs, scratch, aliases={}):
    return pl.pallas_call(
        kernel,
        grid=(grid,),
        out_shape=[jax.ShapeDtypeStruct(shape, dtype) for shape, dtype, _ in outs],
        in_specs=[spec for _, spec in ins],
        out_specs=[spec for _, _, spec in outs],
        scratch_shapes=scratch,
        input_output_aliases=aliases,
        name=name,
        **PARAMS,
    )(*[array for array, _ in ins])


def conv(arrays, sources, n, s, taps, bias, l, flip, flags):
    return call(
        functools.partial(conv_kernel, sources, flip),
        "conv",
        4,
        [(flags, SMEM)]
        + [(a, fixed(*a.shape)) for a in arrays]
        + [(n, fixed(3, COLS, CHANS)), (s, fixed(3, COLS, CHANS))]
        + [(taps, layer(l, 49, 8, 128)), (bias, layer(l, 8, 128))],
        [((PIXELS * 4, 128), f32, tiled(lambda t: t, TILE * 4, 128))],
        [pltpu.VMEM((40 * SPAN * 8, 128), f32)],
    )[0]


def swap(v, axis):
    n = lax.axis_size(axis)
    after = [(i, (i + 1) % n) for i in range(n)]
    before = [(j, i) for i, j in after]
    return lax.ppermute(v[1], axis, after), lax.ppermute(v[0], axis, before)


def strips(outer, inner, north, south):
    sent = []
    for side, cut in ((0, slice(0, 3)), (1, slice(COLS - 3, COLS))):
        corners = [
            jnp.pad(v[:, cut].transpose(1, 0, 2), ((0, 0), (0, 5), (0, 0))) for v in (north, south)
        ]
        sent.append(jnp.concatenate([outer[side], inner[side], *corners], axis=1))
    return swap(sent, "col")


def total(first, second):
    core = lax.axis_index("col") % 2
    mine = jnp.where(core == 0, first, second)
    other = jnp.where(core == 0, second, first).astype(bf16)
    pair = [(i, i ^ 1) for i in range(16)]
    part = (mine + lax.ppermute(other, "col", pair).astype(f32)).astype(bf16)
    for even, odd in ((32, 4), (64, 8), (4, 1), (8, 16), (1, 32), (16, 64)):
        pairs = [(i, i ^ (odd if i & 2 else even)) for i in range(128)]
        other = lax.ppermute(part, ("row", "col", "rep"), pairs)
        part = (part.astype(f32) + other.astype(f32)).astype(bf16)
    back = lax.ppermute(part, "col", pair)
    return jnp.stack([jnp.where(core == 0, part, back), jnp.where(core == 0, back, part)]).astype(f32)


def normalize(stacked):
    mean = jnp.mean(stacked * stacked, axis=(1, 2), keepdims=True)
    return stacked * lax.rsqrt(mean + step_eps)


def body(
    features,
    cotangent,
    depthwise_filters,
    depthwise_bias_vector,
    layernorm_gain,
    layernorm_shift,
    inner_frozen_weight,
    outer_frozen_weight,
    inner_down_factor,
    inner_up_factor,
    outer_down_factor,
    outer_up_factor,
    branch_channel_scale,
):
    x0 = features.reshape(ROWS, COLS, CHANS)
    cot = cotangent.reshape(ROWS, COLS, CHANS)
    ain, bin_, aout, bout = inner_down_factor, inner_up_factor, outer_down_factor, outer_up_factor
    taps = depthwise_filters.reshape(2, 49, GROUPS, 128)
    taps = jnp.concatenate([taps, taps], axis=2)
    bias = depthwise_bias_vector.reshape(2, GROUPS, 128)
    bias = jnp.concatenate([bias, bias], axis=1)
    gain, shift, scale = (
        v.reshape(2, 1, CHANS) for v in (layernorm_gain, layernorm_shift, branch_channel_scale)
    )
    row, col = lax.axis_index("row"), lax.axis_index("col")
    flags = jnp.stack(
        [row > 0, row < lax.axis_size("row") - 1, col > 0, col < lax.axis_size("col") - 1]
    ).astype(f32)

    def by_block(*shape):
        return pl.BlockSpec((None,) + shape, lambda t: (t, 0, 0))

    north, south = swap((x0[:3], x0[-3:]), "row")
    win, wout = call(
        fold_kernel,
        "fold",
        2,
        [
            (inner_frozen_weight, by_block(CHANS, HIDDEN)),
            (ain, by_block(CHANS, RANK)),
            (bin_, by_block(RANK, HIDDEN)),
            (outer_frozen_weight, by_block(HIDDEN, CHANS)),
            (aout, by_block(HIDDEN, RANK)),
            (bout, by_block(RANK, CHANS)),
        ],
        [
            ((2, CHANS, HIDDEN), bf16, by_block(CHANS, HIDDEN)),
            ((2, HIDDEN, CHANS), bf16, by_block(HIDDEN, CHANS)),
        ],
        [],
    )
    ends = [x0[:, :3].transpose(1, 0, 2), x0[:, -3:].transpose(1, 0, 2)]
    west, east = strips(
        [jnp.concatenate([v[:, :8], v[:, 24:]], axis=1) for v in ends],
        [v[:, 8:24] for v in ends],
        north,
        south,
    )
    cv = conv([x0], [[(0, 0, 32)]], north, south, taps, bias, 0, False, flags)

    pixels = tiled
    strip_spec = fixed(3, STRIP, CHANS)

    def common(l, place, x, x_place):
        return [
            (flags, SMEM),
            (x, tiled(x_place, TROWS, COLS, CHANS)),
            (cv, tiled(place, TILE * 4, 128)),
            (west, strip_spec),
            (east, strip_spec),
            (taps, layer(l, 49, 8, 128)),
            (gain, layer(l, 1, CHANS)),
            (shift, layer(l, 1, CHANS)),
            (win, layer(l, CHANS, HIDDEN)),
            (wout, layer(l, HIDDEN, CHANS)),
            (ain, layer(l, CHANS, RANK)),
        ]

    def outer_place(t):
        return 3 * t

    def inner_place(t):
        return t + 1

    def same(t):
        return t

    row_edges = [((3, COLS, CHANS), bf16, fixed(3, COLS, CHANS))] * 2
    col_edges = [((3, 16, CHANS), bf16, fixed(3, 16, CHANS))] * 2
    half = ((16, COLS, CHANS), bf16, tiled(same, TROWS, COLS, CHANS))

    def kept(place):
        return [
            ((PIXELS, width), bf16, tiled(place, TILE, width))
            for width in (CHANS, HIDDEN, HIDDEN, RANK, RANK)
        ]

    last = [(aout, layer(0, HIDDEN, RANK)), (scale, layer(0, 1, CHANS))]
    *saved, outer, top, bottom, west_a, east_a = call(
        functools.partial(first_kernel, False),
        "first_outer",
        2,
        common(0, outer_place, x0, outer_place) + last,
        kept(outer_place) + [half] + row_edges + col_edges,
        [HE, LINE, EDGE],
    )
    north, south = swap((top, bottom), "row")
    ins = common(0, inner_place, x0, inner_place) + last
    *saved, inner, west_b, east_b = call(
        functools.partial(first_kernel, True),
        "first_inner",
        2,
        ins + [(v, ANY) for v in saved],
        kept(inner_place) + [half] + col_edges,
        [HE, LINE, EDGE],
        {len(ins) + i: i for i in range(5)},
    )
    split = [[(0, 0, 8), (8, 24, 8)], [(0, 8, 16)]]
    west, east = strips([west_a, east_a], [west_b, east_b], north, south)
    cv = conv([outer, inner], split, north, south, taps, bias, 1, False, flags)

    def second(place):
        return [
            (bin_, layer(1, RANK, HIDDEN)),
            (aout, layer(1, HIDDEN, RANK)),
            (bout, layer(1, RANK, CHANS)),
            (scale, layer(1, 1, CHANS)),
            (cot, tiled(place, TROWS, COLS, CHANS)),
        ]

    def results(place):
        return [
            ((ROWS, COLS, CHANS), bf16, tiled(place, TROWS, COLS, CHANS)),
            ((RANK, GRADS), f32, fixed(RANK, GRADS)),
            half,
        ]

    work = [
        HE,
        LINE,
        EDGE,
        pltpu.VMEM((TILE, CHANS), bf16),
        pltpu.VMEM((TILE, CHANS), f32),
        pltpu.VMEM((TILE, 128), f32),
    ]
    out, grads1, outer_g, top, bottom, west_a, east_a = call(
        functools.partial(second_kernel, False),
        "second_outer",
        2,
        common(1, outer_place, outer, same) + second(outer_place),
        results(outer_place) + row_edges + col_edges,
        work,
    )
    north, south = swap((top, bottom), "row")
    ins = common(1, inner_place, inner, same) + second(inner_place)
    out, grads1, inner_g, west_b, east_b = call(
        functools.partial(second_kernel, True),
        "second_inner",
        2,
        ins + [(out, ANY), (grads1, fixed(RANK, GRADS))],
        results(inner_place) + col_edges,
        work,
        {len(ins): 0},
    )
    west, east = strips([west_a, east_a], [west_b, east_b], north, south)
    cv = conv([outer_g, inner_g], split, north, south, taps, bias, 1, True, flags)
    (grads0,) = call(
        third_kernel,
        "third",
        4,
        [
            (flags, SMEM),
            (cot, tiled(same, TROWS, COLS, CHANS)),
            (cv, tiled(same, TILE * 4, 128)),
            (west, strip_spec),
            (east, strip_spec),
            (taps, layer(1, 49, 8, 128)),
            (scale, layer(0, 1, CHANS)),
            (wout, layer(0, HIDDEN, CHANS)),
            (bin_, layer(0, RANK, HIDDEN)),
            (bout, layer(0, RANK, CHANS)),
        ]
        + [(v, tiled(same, TILE, v.shape[1])) for v in saved],
        [((RANK, GRADS), f32, fixed(RANK, GRADS))],
        [HE, LINE, pltpu.VMEM((TILE, CHANS), bf16)],
    )
    sums = total(grads0, grads1)
    return (
        out[None],
        normalize(sums[:, :, 0:512].transpose(0, 2, 1)),
        normalize(adapter_scale * sums[:, :, 512:2560]),
        normalize(sums[:, :, 2560:4608].transpose(0, 2, 1)),
        normalize(adapter_scale * sums[:, :, 4608:5120]),
    )


def solution(mesh):
    tile = P("rep", "row", "col", None)
    return jax.shard_map(
        body,
        mesh=mesh,
        in_specs=(tile, tile) + (P(),) * 11,
        out_specs=(tile, P(), P(), P(), P()),
        check_vma=False,
    )
```

time: 224 us -> 209 us (0.933)
  Pallas kernels: 91.4 us -> 111 us
  starting transfers between devices: 57.7 us -> 41.7 us
  waiting for transfers between devices: 41.7 us -> 28.5 us
  local copies, waits for them, and re-layouts: 25.8 us -> 18 us
  other arithmetic: 5.72 us -> 8.52 us
    pallas_call x4 -> x9, Pallas kernels: 91.4 us -> 111 us  [call(): pl.pallas_call(kernel, grid=(grid,), out_shape=[jax.ShapeDtypeStruct(shap...]
    ppermute x20, starting transfers between devices: 57.7 us -> 41.7 us  [the longest x12 21.6 us: swap(): return (lax.ppermute(v[1], axis, after), lax.ppermute(v[0], axis, before))]
    ppermute x20, waiting for transfers between devices: 41.7 us -> 28.5 us  [the longest x6 22.7 us: total(): other = lax.ppermute(part, ('row', 'col', 'rep'), pairs)]
    squeeze x7 -> x0, local copies, waits for them, and re-layouts: 10.9 us -> none  [the longest x1 4.61 us: body(): wout[1]]
    concatenate x0 -> x6, other arithmetic: none -> 3.95 us  [the longest x4 3.27 us: strips(): sent.append(jnp.concatenate([outer[side], inner[side], *corners], axis=1))]
    unnamed x39 -> x44, local copies, waits for them, and re-layouts: 5.4 us -> 6.19 us
  transfers between devices with their start and end apart: 20 -> 20, of which waited for: 15 -> 9; matrix products, arithmetic and copies ran while one was open for 9% -> 7% of each run, Pallas kernels for 3% -> 33%
where the time goes in v1:
time: 209 us; the launch traced here: 208 us
  Pallas kernels  111 us (53%)
  starting transfers between devices  41.7 us (20%)
  waiting for transfers between devices  28.5 us (14%)
  local copies, waits for them, and re-layouts  18 us (9%)
  other arithmetic  8.52 us (4%)
    pallas_call x9, Pallas kernels, call(): pl.pallas_call(kernel, grid=(grid,), out_shape=[jax.ShapeDtypeStruct(shap...  111 us
    ppermute x6, waiting for transfers between devices, total(): other = lax.ppermute(part, ('row', 'col', 'rep'), pairs)  22.7 us
    ppermute x12, starting transfers between devices, swap(): return (lax.ppermute(v[1], axis, after), lax.ppermute(v[0], axis, before))  21.6 us
    ppermute x1, starting transfers between devices, total(): back = lax.ppermute(part, 'col', pair)  8.02 us
    ppermute x6, starting transfers between devices, total(): other = lax.ppermute(part, ('row', 'col', 'rep'), pairs)  7.6 us
    unnamed x44, local copies, waits for them, and re-layouts  6.19 us
    ppermute x1, starting transfers between devices, total(): part = (mine + lax.ppermute(other, 'col', pair).astype(f32)).astype(bf16)  4.45 us
  transfers between devices with their start and end apart: 20, of which 9 were waited for; matrix products, arithmetic and copies ran while one was open for 7% of the time, Pallas kernels for 33%

profile of v1, /device:TPU:1, one launch (start us, length us, event | category | flops | bytes accessed | tf_op | source)
XLA Modules:
  0.0 208.5 jit_solution(6030749739642912436)
XLA Ops:
  0.7 1.9 copy.83
  2.7 3.6 %collective-permute-start.1 = (bf16[3,32,512]{2,0,1:T(4,128)(2,1)S(1)}, bf16[3,32,512]{2,0,1:T(4,128)(2,1)S(1)}, u32[]{:S(2)}, u32[]{:S(2)}) collective-permute-start(bf16[3,32,512]{2,0,1:T(4,128)(2,1)S(1)} %get-tuple-element.79), channel_id=1, source_target_pairs={{32,0},{64,32},{96,64},{0,96},{33,1},{65,33},{97,65},{1,97},{34,2}... | collective-permute-start | bytes 294920 | tf_op jit(solution)/shard_map/ppermute | solution.py:358
  6.3 1.1 reshape.66
  7.6 3.7 %collective-permute-done = bf16[3,32,512]{2,0,1:T(4,128)(2,1)S(1)} collective-permute-done((bf16[3,32,512]{2,0,1:T(4,128)(2,1)S(1)}, bf16[3,32,512]{2,0,1:T(4,128)(2,1)S(1)}, u32[]{:S(2)}, u32[]{:S(2)}) %collective-permute-start) | collective-permute-done | bytes 98336 | tf_op jit(solution)/shard_map/ppermute | solution.py:358
  11.4 3.7 %collective-permute-start.2 = (bf16[3,48,512]{2,1,0:T(8,128)(2,1)S(1)}, bf16[3,48,512]{2,1,0:T(8,128)(2,1)S(1)}, u32[]{:S(2)}, u32[]{:S(2)}) collective-permute-start(bf16[3,48,512]{2,1,0:T(8,128)(2,1)S(1)} %pad_dynamic-update-slice_fusion.2), channel_id=1, source_target_pairs={{0,2},{2,4},{4,6},{6,8},{8,10},{10,12},{12,14},{14,16},{16,18},{18... | collective-permute-start | bytes 442376 | tf_op jit(solution)/shard_map/ppermute | solution.py:358
  19.3 1.3 copy.60.aout
  20.6 6.6 %fold.1 = (bf16[2,512,2048]{2,1,0:T(8,128)(2,1)}, bf16[2,2048,512]{2,1,0:T(8,128)(2,1)}) custom-call(bf16[2,512,2048]{2,1,0:T(8,128)(2,1)} %win.1, bf16[2,512,16]{2,1,0:T(8,128)(2,1)} %copy.59.ain, bf16[2,16,2048]{2,1,0:T(8,128)(2,1)} %bin_.7, bf16[2,2048,512]{2,1,0:T(8,128)(2,1)} %wout.1, bf16[2,2048,16]{2,1,0:T(8,128)(2,1)} %copy.60.aout, ...), custom_call_target="tpu_custom_call" | custom-call | tf_op jit(solution)/shard_map/fold/pallas_call | solution.py:327
  29.1 11.2 %conv.3.cv = f32[4096,128]{1,0:T(8,128)} custom-call(f32[4]{0:T(128)} %add_convert_fusion.7.flags, bf16[32,32,512]{2,1,0:T(8,128)(2,1)} %bitcast.52, bf16[3,32,512]{2,1,0:T(8,128)(2,1)} %copy.57.refs_1_, bf16[3,32,512]{2,1,0:T(8,128)(2,1)} %copy.58.refs_2_, f32[2,49,8,128]{3,2,1,0:T(8,128)} %copy.80.refs_3_.taps.refs_4_, ...), custom_call_target="tpu_custom_call" | custom-call | tf_op jit(solution)/shard_map/conv/pallas_call | solution.py:327
  41.0 13.0 %first_outer.1 = (bf16[1024,512]{1,0:T(8,128)(2,1)}, bf16[1024,2048]{1,0:T(8,128)(2,1)}, bf16[1024,2048]{1,0:T(8,128)(2,1)}, bf16[1024,16]{1,0:T(8,128)(2,1)}, b...) custom-call(f32[4]{0:T(128)} %add_convert_fusion.7.flags, ...), custom_call_target="tpu_custom_call" | custom-call | tf_op jit(solution)/shard_map/first_outer/pallas_call | solution.py:327
  56.0 1.5 collective-permute-start.4
  57.5 12.5 %first_inner.1 = (bf16[1024,512]{1,0:T(8,128)(2,1)}, bf16[1024,2048]{1,0:T(8,128)(2,1)}, bf16[1024,2048]{1,0:T(8,128)(2,1)}, bf16[1024,16]{1,0:T(8,128)(2,1)}, b...) custom-call(f32[4]{0:T(128)} %add_convert_fusion.7.flags, ...), custom_call_target="tpu_custom_call", output_to_operand_aliasing={{0}: (13, {}), {1}: (14, {}), {2}: (15, {}), {3}: (16, {}),... | custom-call | tf_op jit(solution)/shard_map/first_inner/pallas_call | solution.py:327
  71.0 2.4 %collective-permute-start.6 = (bf16[3,48,512]{2,1,0:T(8,128)(2,1)S(1)}, bf16[3,48,512]{2,1,0:T(8,128)(2,1)S(1)}, u32[]{:S(2)}, u32[]{:S(2)}) collective-permute-start(bf16[3,48,512]{2,1,0:T(8,128)(2,1)S(1)} %fusion.5), channel_id=1, source_target_pairs={{0,2},{2,4},{4,6},{6,8},{8,10},{10,12},{12,14},{14,16},{16,18},{18... | collective-permute-start | bytes 442376 | tf_op jit(solution)/shard_map/ppermute | solution.py:358
  74.2 2.3 %collective-permute-start.7 = (bf16[3,48,512]{2,1,0:T(8,128)(2,1)S(1)}, bf16[3,48,512]{2,1,0:T(8,128)(2,1)S(1)}, u32[]{:S(2)}, u32[]{:S(2)}) collective-permute-start(bf16[3,48,512]{2,1,0:T(8,128)(2,1)S(1)} %fusion.6), channel_id=1, source_target_pairs={{2,0},{4,2},{6,4},{8,6},{10,8},{12,10},{14,12},{16,14},{18,16},{20... | collective-permute-start | bytes 442376 | tf_op jit(solution)/shard_map/ppermute | solution.py:358
  77.8 11.1 %conv.4.cv = f32[4096,128]{1,0:T(8,128)} custom-call(f32[4]{0:T(128)} %add_convert_fusion.7.flags, bf16[16,32,512]{2,1,0:T(8,128)(2,1)} %get-tuple-element.45.refs_0_.x, bf16[16,32,512]{2,1,0:T(8,128)(2,1)} %get-tuple-element.44.refs_1_.x, bf16[3,32,512]{2,1,0:T(8,128)(2,1)} %copy.69.refs_2_, bf16[3,32,512]{2,1,0:T(8,128)(2,1)} %copy.70.refs_3_, ...), custom_call_target="tpu_custom_call" | custom-call | tf_op jit(solution)/shard_map/conv/pallas_call | solution.py:327
  89.7 15.7 %second_outer.1 = (bf16[32,32,512]{2,1,0:T(8,128)(2,1)}, f32[16,5120]{1,0:T(8,128)}, bf16[16,32,512]{2,1,0:T(8,128)(2,1)}, bf16[3,32,512]{2,1,0:T(8,128)(2,1)}, ...) custom-call(f32[4]{0:T(128)} %add_convert_fusion.7.flags, ...), custom_call_target="tpu_custom_call" | custom-call | tf_op jit(solution)/shard_map/second_outer/pallas_call | solution.py:327
  106.4 1.2 collective-permute-start.9
  108.9 15.6 %second_inner.1 = (bf16[32,32,512]{2,1,0:T(8,128)(2,1)}, f32[16,5120]{1,0:T(8,128)}, bf16[16,32,512]{2,1,0:T(8,128)(2,1)}, bf16[3,16,512]{2,1,0:T(8,128)(2,1)}, bf16[3,16,512]{2,1,0:T(8,128)(2,1)}) custom-call(f32[4]{0:T(128)} %add_convert_fusion.7.flags, bf16[16,32,512]{2,1,0:T(8,128)(2,1)} %get-tuple-element.44.refs_1_.x, ...), custom_call_target="tpu_custom_call", output_to_operand_aliasing={{0}: (16, {})} | custom-call | tf_op jit(solution)/shard_map/second_inner/pallas_call | solution.py:327
  126.5 6.0 %collective-permute-start.11 = (bf16[3,48,512]{2,1,0:T(8,128)(2,1)S(1)}, bf16[3,48,512]{2,1,0:T(8,128)(2,1)S(1)}, u32[]{:S(2)}, u32[]{:S(2)}) collective-permute-start(bf16[3,48,512]{2,1,0:T(8,128)(2,1)S(1)} %fusion.8), channel_id=1, source_target_pairs={{2,0},{4,2},{6,4},{8,6},{10,8},{12,10},{14,12},{16,14},{18,16},{20... | collective-permute-start | bytes 442376 | tf_op jit(solution)/shard_map/ppermute | solution.py:358
  133.8 11.0 %conv.5.cv = f32[4096,128]{1,0:T(8,128)} custom-call(f32[4]{0:T(128)} %add_convert_fusion.7.flags, bf16[16,32,512]{2,1,0:T(8,128)(2,1)} %get-tuple-element.55.refs_0_, bf16[16,32,512]{2,1,0:T(8,128)(2,1)} %get-tuple-element.56.refs_1_, bf16[3,32,512]{2,1,0:T(8,128)(2,1)} %copy.77.refs_2_, bf16[3,32,512]{2,1,0:T(8,128)(2,1)} %copy.78.refs_3_, ...), custom_call_target="tpu_custom_call" | custom-call | tf_op jit(solution)/shard_map/conv/pallas_call | solution.py:327
  145.6 14.0 %third.1 = f32[16,5120]{1,0:T(8,128)} custom-call(f32[4]{0:T(128)} %add_convert_fusion.7.flags, bf16[32,32,512]{2,1,0:T(8,128)(2,1)} %bitcast.57, f32[4096,128]{1,0:T(8,128)} %conv.5.cv, bf16[3,48,512]{2,1,0:T(8,128)(2,1)} %copy-done.5, bf16[3,48,512]{2,1,0:T(8,128)(2,1)} %copy-done.6, f32[2,49,8,128]{3,2,1,0:T(8,128)} %copy.80.refs_3_.taps.refs_4_, ...), custom_call_target="tpu_custom_call" | custom-call | tf_op jit(solution)/shard_map/third/pallas_call | solution.py:327
  160.6 4.5 %collective-permute-start.12 = (bf16[16,5120]{1,0:T(8,128)(2,1)S(1)}, bf16[16,5120]{1,0:T(8,128)(2,1)S(1)}, u32[]{:S(2)}, u32[]{:S(2)}) collective-permute-start(bf16[16,5120]{1,0:T(8,128)(2,1)S(1)} %select_convert_fusion), channel_id=1, source_target_pairs={{0,2},{2,0},{4,6},{6,4},{8,10},{10,8},{12,14},{14,12},{16,18},{18,... | collective-permute-start | bytes 491528 | tf_op jit(solution)/shard_map/ppermute | solution.py:376
  166.2 4.2 %collective-permute-done.13 = bf16[16,5120]{1,0:T(8,128)(2,1)S(1)} collective-permute-done((bf16[16,5120]{1,0:T(8,128)(2,1)S(1)}, bf16[16,5120]{1,0:T(8,128)(2,1)S(1)}, u32[]{:S(2)}, u32[]{:S(2)}) %collective-permute-start.13) | collective-permute-done | bytes 163872 | tf_op jit(solution)/shard_map/ppermute | solution.py:379
  170.4 1.1 collective-permute-start.14
  171.6 4.6 %collective-permute-done.14 = bf16[16,5120]{1,0:T(8,128)(2,1)S(1)} collective-permute-done((bf16[16,5120]{1,0:T(8,128)(2,1)S(1)}, bf16[16,5120]{1,0:T(8,128)(2,1)S(1)}, u32[]{:S(2)}, u32[]{:S(2)}) %collective-permute-start.14) | collective-permute-done | bytes 163872 | tf_op jit(solution)/shard_map/ppermute | solution.py:379
  176.2 1.3 collective-permute-start.15
  177.5 3.0 %collective-permute-done.15 = bf16[16,5120]{1,0:T(8,128)(2,1)S(1)} collective-permute-done((bf16[16,5120]{1,0:T(8,128)(2,1)S(1)}, bf16[16,5120]{1,0:T(8,128)(2,1)S(1)}, u32[]{:S(2)}, u32[]{:S(2)}) %collective-permute-start.15) | collective-permute-done | bytes 163872 | tf_op jit(solution)/shard_map/ppermute | solution.py:379
  180.5 2.8 %collective-permute-start.16 = (bf16[16,5120]{1,0:T(8,128)(2,1)S(1)}, bf16[16,5120]{1,0:T(8,128)(2,1)S(1)}, u32[]{:S(2)}, u32[]{:S(2)}) collective-permute-start(bf16[16,5120]{1,0:T(8,128)(2,1)S(1)} %add_convert_fusion.3), channel_id=1, source_target_pairs={{0,8},{1,9},{2,18},{3,19},{4,12},{5,13},{6,22},{7,23},{8,0},{9,1},... | collective-permute-start | bytes 491528 | tf_op jit(solution)/shard_map/ppermute | solution.py:379
  183.4 2.9 %collective-permute-done.16 = bf16[16,5120]{1,0:T(8,128)(2,1)S(1)} collective-permute-done((bf16[16,5120]{1,0:T(8,128)(2,1)S(1)}, bf16[16,5120]{1,0:T(8,128)(2,1)S(1)}, u32[]{:S(2)}, u32[]{:S(2)}) %collective-permute-start.16) | collective-permute-done | bytes 163872 | tf_op jit(solution)/shard_map/ppermute | solution.py:379
  186.4 4.5 %collective-permute-done.17 = bf16[16,5120]{1,0:T(8,128)(2,1)S(1)} collective-permute-done((bf16[16,5120]{1,0:T(8,128)(2,1)S(1)}, bf16[16,5120]{1,0:T(8,128)(2,1)S(1)}, u32[]{:S(2)}, u32[]{:S(2)}) %collective-permute-start.17) | collective-permute-done | bytes 163872 | tf_op jit(solution)/shard_map/ppermute | solution.py:379
  190.9 2.2 %collective-permute-start.18 = (bf16[16,5120]{1,0:T(8,128)(2,1)S(1)}, bf16[16,5120]{1,0:T(8,128)(2,1)S(1)}, u32[]{:S(2)}, u32[]{:S(2)}) collective-permute-start(bf16[16,5120]{1,0:T(8,128)(2,1)S(1)} %add_convert_fusion.1), channel_id=1, source_target_pairs={{0,16},{1,17},{2,66},{3,67},{4,20},{5,21},{6,70},{7,71},{8,24},{9,... | collective-permute-start | bytes 491528 | tf_op jit(solution)/shard_map/ppermute | solution.py:379
  193.1 3.6 %collective-permute-done.18 = bf16[16,5120]{1,0:T(8,128)(2,1)S(1)} collective-permute-done((bf16[16,5120]{1,0:T(8,128)(2,1)S(1)}, bf16[16,5120]{1,0:T(8,128)(2,1)S(1)}, u32[]{:S(2)}, u32[]{:S(2)}) %collective-permute-start.18) | collective-permute-done | bytes 163872 | tf_op jit(solution)/shard_map/ppermute | solution.py:379
  196.7 8.0 %collective-permute-start.19 = (bf16[16,5120]{1,0:T(8,128)(2,1)S(1)}, bf16[16,5120]{1,0:T(8,128)(2,1)S(1)}, u32[]{:S(2)}, u32[]{:S(2)}) collective-permute-start(bf16[16,5120]{1,0:T(8,128)(2,1)S(1)} %add_convert_fusion), channel_id=1, source_target_pairs={{0,2},{2,0},{4,6},{6,4},{8,10},{10,8},{12,14},{14,12},{16,18},{18,... | collective-permute-start | bytes 491528 | tf_op jit(solution)/shard_map/ppermute | solution.py:381
  (113 shorter events, 25.2 us)
Async XLA Ops:
  0.6 15.2 %copy-start.13 = (f32[2,512]{1,0:T(2,128)S(1)}, f32[2,512]{1,0:T(2,128)}, u32[]{:S(2)}) copy-start(f32[2,512]{1,0:T(2,128)} %param.25) | copy-start | bytes 12292
  0.6 15.8 %copy-start.14 = (f32[2,512]{1,0:T(2,128)S(1)}, f32[2,512]{1,0:T(2,128)}, u32[]{:S(2)}) copy-start(f32[2,512]{1,0:T(2,128)} %param.17) | copy-start | bytes 12292
  0.7 16.4 %copy-start.15 = (f32[2,512]{1,0:T(2,128)S(1)}, f32[2,512]{1,0:T(2,128)}, u32[]{:S(2)}) copy-start(f32[2,512]{1,0:T(2,128)} %param.18) | copy-start | bytes 12292
  0.7 16.9 %copy-start.16 = (f32[2,512]{1,0:T(2,128)S(1)}, f32[2,512]{1,0:T(2,128)}, u32[]{:S(2)}) copy-start(f32[2,512]{1,0:T(2,128)} %param.16) | copy-start | bytes 12292
  0.7 17.7 %copy-start.12 = (bf16[2,512,16]{1,2,0:T(8,128)(2,1)S(1)}, bf16[2,512,16]{1,2,0:T(8,128)(2,1)}, u32[]{:S(2)}) copy-start(bf16[2,512,16]{1,2,0:T(8,128)(2,1)} %param.21) | copy-start | bytes 98308
  0.7 18.6 %copy-start.7 = (bf16[2,2048,16]{1,2,0:T(8,128)(2,1)S(1)}, bf16[2,2048,16]{1,2,0:T(8,128)(2,1)}, u32[]{:S(2)}) copy-start(bf16[2,2048,16]{1,2,0:T(8,128)(2,1)} %param.23) | copy-start | bytes 393220
  2.7 8.7 %collective-permute-start.1 = (bf16[3,32,512]{2,0,1:T(4,128)(2,1)S(1)}, bf16[3,32,512]{2,0,1:T(4,128)(2,1)S(1)}, u32[]{:S(2)}, u32[]{:S(2)}) collective-permute-start(bf16[3,32,512]{2,0,1:T(4,128)(2,1)S(1)} %get-tuple-element.79), channel_id=1, source_target_pairs={{32,0},{64,32},{96,64},{0,96},{33,1},{65,33},{97,65},{1,97},{34,2}... | collective-permute-start | bytes 294920 | tf_op jit(solution)/shard_map/ppermute | solution.py:358
  6.3 5.0 %collective-permute-start = (bf16[3,32,512]{2,0,1:T(4,128)(2,1)S(1)}, bf16[3,32,512]{2,0,1:T(4,128)(2,1)S(1)}, u32[]{:S(2)}, u32[]{:S(2)}) collective-permute-start(bf16[3,32,512]{2,0,1:T(4,128)(2,1)S(1)} %get-tuple-element.80), channel_id=1, source_target_pairs={{0,32},{32,64},{64,96},{96,0},{1,33},{33,65},{65,97},{97,1},{2,34}... | collective-permute-start | bytes 294920 | tf_op jit(solution)/shard_map/ppermute | solution.py:358
  11.4 28.8 %collective-permute-start.2 = (bf16[3,48,512]{2,1,0:T(8,128)(2,1)S(1)}, bf16[3,48,512]{2,1,0:T(8,128)(2,1)S(1)}, u32[]{:S(2)}, u32[]{:S(2)}) collective-permute-start(bf16[3,48,512]{2,1,0:T(8,128)(2,1)S(1)} %pad_dynamic-update-slice_fusion.2), channel_id=1, source_target_pairs={{0,2},{2,4},{4,6},{6,8},{8,10},{10,12},{12,14},{14,16},{16,18},{18... | collective-permute-start | bytes 442376 | tf_op jit(solution)/shard_map/ppermute | solution.py:358
  15.1 25.1 %collective-permute-start.3 = (bf16[3,48,512]{2,1,0:T(8,128)(2,1)S(1)}, bf16[3,48,512]{2,1,0:T(8,128)(2,1)S(1)}, u32[]{:S(2)}, u32[]{:S(2)}) collective-permute-start(bf16[3,48,512]{2,1,0:T(8,128)(2,1)S(1)} %pad_dynamic-update-slice_fusion), channel_id=1, source_target_pairs={{2,0},{4,2},{6,4},{8,6},{10,8},{12,10},{14,12},{16,14},{18,16},{20... | collective-permute-start | bytes 442376 | tf_op jit(solution)/shard_map/ppermute | solution.py:358
  55.0 15.1 %collective-permute-start.5 = (bf16[3,32,512]{2,0,1:T(4,128)(2,1)S(1)}, bf16[3,32,512]{2,0,1:T(4,128)(2,1)S(1)}, u32[]{:S(2)}, u32[]{:S(2)}) collective-permute-start(bf16[3,32,512]{2,0,1:T(4,128)(2,1)S(1)} %copy.68), channel_id=1, source_target_pairs={{32,0},{64,32},{96,64},{0,96},{33,1},{65,33},{97,65},{1,97},{34,2}... | collective-permute-start | bytes 294920 | tf_op jit(solution)/shard_map/ppermute | solution.py:358
  56.0 14.1 %collective-permute-start.4 = (bf16[3,32,512]{2,0,1:T(4,128)(2,1)S(1)}, bf16[3,32,512]{2,0,1:T(4,128)(2,1)S(1)}, u32[]{:S(2)}, u32[]{:S(2)}) collective-permute-start(bf16[3,32,512]{2,0,1:T(4,128)(2,1)S(1)} %copy.67), channel_id=1, source_target_pairs={{0,32},{32,64},{64,96},{96,0},{1,33},{33,65},{65,97},{97,1},{2,34}... | collective-permute-start | bytes 294920 | tf_op jit(solution)/shard_map/ppermute | solution.py:358
  57.5 12.6 %copy-start.11 = (bf16[3,16,512]{2,1,0:T(8,128)(2,1)S(1)}, bf16[3,16,512]{2,1,0:T(8,128)(2,1)}, u32[]{:S(2)}) copy-start(bf16[3,16,512]{2,1,0:T(8,128)(2,1)} %get-tuple-element.48) | copy-start | bytes 147460
  57.5 15.8 %copy-start.9 = (bf16[3,16,512]{2,1,0:T(8,128)(2,1)S(1)}, bf16[3,16,512]{2,1,0:T(8,128)(2,1)}, u32[]{:S(2)}) copy-start(bf16[3,16,512]{2,1,0:T(8,128)(2,1)} %get-tuple-element.50) | copy-start | bytes 147460
  71.0 18.0 %collective-permute-start.6 = (bf16[3,48,512]{2,1,0:T(8,128)(2,1)S(1)}, bf16[3,48,512]{2,1,0:T(8,128)(2,1)S(1)}, u32[]{:S(2)}, u32[]{:S(2)}) collective-permute-start(bf16[3,48,512]{2,1,0:T(8,128)(2,1)S(1)} %fusion.5), channel_id=1, source_target_pairs={{0,2},{2,4},{4,6},{6,8},{8,10},{10,12},{12,14},{14,16},{16,18},{18... | collective-permute-start | bytes 442376 | tf_op jit(solution)/shard_map/ppermute | solution.py:358
  74.2 14.8 %collective-permute-start.7 = (bf16[3,48,512]{2,1,0:T(8,128)(2,1)S(1)}, bf16[3,48,512]{2,1,0:T(8,128)(2,1)S(1)}, u32[]{:S(2)}, u32[]{:S(2)}) collective-permute-start(bf16[3,48,512]{2,1,0:T(8,128)(2,1)S(1)} %fusion.6), channel_id=1, source_target_pairs={{2,0},{4,2},{6,4},{8,6},{10,8},{12,10},{14,12},{16,14},{18,16},{20... | collective-permute-start | bytes 442376 | tf_op jit(solution)/shard_map/ppermute | solution.py:358
  89.0 0.7 copy-start.4
  106.4 18.2 %collective-permute-start.9 = (bf16[3,32,512]{2,0,1:T(4,128)(2,1)S(1)}, bf16[3,32,512]{2,0,1:T(4,128)(2,1)S(1)}, u32[]{:S(2)}, u32[]{:S(2)}) collective-permute-start(bf16[3,32,512]{2,0,1:T(4,128)(2,1)S(1)} %copy.76), channel_id=1, source_target_pairs={{32,0},{64,32},{96,64},{0,96},{33,1},{65,33},{97,65},{1,97},{34,2}... | collective-permute-start | bytes 294920 | tf_op jit(solution)/shard_map/ppermute | solution.py:358
  108.6 16.0 %collective-permute-start.8 = (bf16[3,32,512]{2,0,1:T(4,128)(2,1)S(1)}, bf16[3,32,512]{2,0,1:T(4,128)(2,1)S(1)}, u32[]{:S(2)}, u32[]{:S(2)}) collective-permute-start(bf16[3,32,512]{2,0,1:T(4,128)(2,1)S(1)} %copy.75), channel_id=1, source_target_pairs={{0,32},{32,64},{64,96},{96,0},{1,33},{33,65},{65,97},{97,1},{2,34}... | collective-permute-start | bytes 294920 | tf_op jit(solution)/shard_map/ppermute | solution.py:358
  108.9 15.7 %copy-start.10 = (bf16[3,16,512]{2,1,0:T(8,128)(2,1)S(1)}, bf16[3,16,512]{2,1,0:T(8,128)(2,1)}, u32[]{:S(2)}) copy-start(bf16[3,16,512]{2,1,0:T(8,128)(2,1)} %get-tuple-element.59) | copy-start | bytes 147460
  108.9 16.8 %copy-start.8 = (bf16[3,16,512]{2,1,0:T(8,128)(2,1)S(1)}, bf16[3,16,512]{2,1,0:T(8,128)(2,1)}, u32[]{:S(2)}) copy-start(bf16[3,16,512]{2,1,0:T(8,128)(2,1)} %get-tuple-element.61) | copy-start | bytes 147460
  125.4 19.4 %collective-permute-start.10 = (bf16[3,48,512]{2,1,0:T(8,128)(2,1)S(1)}, bf16[3,48,512]{2,1,0:T(8,128)(2,1)S(1)}, u32[]{:S(2)}, u32[]{:S(2)}) collective-permute-start(bf16[3,48,512]{2,1,0:T(8,128)(2,1)S(1)} %fusion.7), channel_id=1, source_target_pairs={{0,2},{2,4},{4,6},{6,8},{8,10},{10,12},{12,14},{14,16},{16,18},{18... | collective-permute-start | bytes 442376 | tf_op jit(solution)/shard_map/ppermute | solution.py:358
  126.5 18.3 %collective-permute-start.11 = (bf16[3,48,512]{2,1,0:T(8,128)(2,1)S(1)}, bf16[3,48,512]{2,1,0:T(8,128)(2,1)S(1)}, u32[]{:S(2)}, u32[]{:S(2)}) collective-permute-start(bf16[3,48,512]{2,1,0:T(8,128)(2,1)S(1)} %fusion.8), channel_id=1, source_target_pairs={{2,0},{4,2},{6,4},{8,6},{10,8},{12,10},{14,12},{16,14},{18,16},{20... | collective-permute-start | bytes 442376 | tf_op jit(solution)/shard_map/ppermute | solution.py:358
  145.6 14.0 %copy-start = (f32[16,5120]{1,0:T(8,128)S(1)}, f32[16,5120]{1,0:T(8,128)}, u32[]{:S(2)}) copy-start(f32[16,5120]{1,0:T(8,128)} %get-tuple-element.68) | copy-start | bytes 983044
  160.6 5.5 %collective-permute-start.12 = (bf16[16,5120]{1,0:T(8,128)(2,1)S(1)}, bf16[16,5120]{1,0:T(8,128)(2,1)S(1)}, u32[]{:S(2)}, u32[]{:S(2)}) collective-permute-start(bf16[16,5120]{1,0:T(8,128)(2,1)S(1)} %select_convert_fusion), channel_id=1, source_target_pairs={{0,2},{2,0},{4,6},{6,4},{8,10},{10,8},{12,14},{14,12},{16,18},{18,... | collective-permute-start | bytes 491528 | tf_op jit(solution)/shard_map/ppermute | solution.py:376
  166.1 4.2 %collective-permute-start.13 = (bf16[16,5120]{1,0:T(8,128)(2,1)S(1)}, bf16[16,5120]{1,0:T(8,128)(2,1)S(1)}, u32[]{:S(2)}, u32[]{:S(2)}) collective-permute-start(bf16[16,5120]{1,0:T(8,128)(2,1)S(1)} %add_convert_fusion.6), channel_id=1, source_target_pairs={{0,32},{1,33},{2,6},{3,7},{4,36},{5,37},{6,2},{7,3},{8,40},{9,41},... | collective-permute-start | bytes 491528 | tf_op jit(solution)/shard_map/ppermute | solution.py:379
  170.4 5.8 %collective-permute-start.14 = (bf16[16,5120]{1,0:T(8,128)(2,1)S(1)}, bf16[16,5120]{1,0:T(8,128)(2,1)S(1)}, u32[]{:S(2)}, u32[]{:S(2)}) collective-permute-start(bf16[16,5120]{1,0:T(8,128)(2,1)S(1)} %add_convert_fusion.5), channel_id=1, source_target_pairs={{0,64},{1,65},{2,10},{3,11},{4,68},{5,69},{6,14},{7,15},{8,72},{9,... | collective-permute-start | bytes 491528 | tf_op jit(solution)/shard_map/ppermute | solution.py:379
  176.2 4.2 %collective-permute-start.15 = (bf16[16,5120]{1,0:T(8,128)(2,1)S(1)}, bf16[16,5120]{1,0:T(8,128)(2,1)S(1)}, u32[]{:S(2)}, u32[]{:S(2)}) collective-permute-start(bf16[16,5120]{1,0:T(8,128)(2,1)S(1)} %add_convert_fusion.4), channel_id=1, source_target_pairs={{0,4},{1,5},{2,3},{3,2},{4,0},{5,1},{6,7},{7,6},{8,12},{9,13},{10,... | collective-permute-start | bytes 491528 | tf_op jit(solution)/shard_map/ppermute | solution.py:379
  180.5 5.8 %collective-permute-start.16 = (bf16[16,5120]{1,0:T(8,128)(2,1)S(1)}, bf16[16,5120]{1,0:T(8,128)(2,1)S(1)}, u32[]{:S(2)}, u32[]{:S(2)}) collective-permute-start(bf16[16,5120]{1,0:T(8,128)(2,1)S(1)} %add_convert_fusion.3), channel_id=1, source_target_pairs={{0,8},{1,9},{2,18},{3,19},{4,12},{5,13},{6,22},{7,23},{8,0},{9,1},... | collective-permute-start | bytes 491528 | tf_op jit(solution)/shard_map/ppermute | solution.py:379
  186.3 4.5 %collective-permute-start.17 = (bf16[16,5120]{1,0:T(8,128)(2,1)S(1)}, bf16[16,5120]{1,0:T(8,128)(2,1)S(1)}, u32[]{:S(2)}, u32[]{:S(2)}) collective-permute-start(bf16[16,5120]{1,0:T(8,128)(2,1)S(1)} %add_convert_fusion.2), channel_id=1, source_target_pairs={{0,1},{1,0},{2,34},{3,35},{4,5},{5,4},{6,38},{7,39},{8,9},{9,8},{1... | collective-permute-start | bytes 491528 | tf_op jit(solution)/shard_map/ppermute | solution.py:379
  190.9 5.8 %collective-permute-start.18 = (bf16[16,5120]{1,0:T(8,128)(2,1)S(1)}, bf16[16,5120]{1,0:T(8,128)(2,1)S(1)}, u32[]{:S(2)}, u32[]{:S(2)}) collective-permute-start(bf16[16,5120]{1,0:T(8,128)(2,1)S(1)} %add_convert_fusion.1), channel_id=1, source_target_pairs={{0,16},{1,17},{2,66},{3,67},{4,20},{5,21},{6,70},{7,71},{8,24},{9,... | collective-permute-start | bytes 491528 | tf_op jit(solution)/shard_map/ppermute | solution.py:379
  196.7 9.0 %collective-permute-start.19 = (bf16[16,5120]{1,0:T(8,128)(2,1)S(1)}, bf16[16,5120]{1,0:T(8,128)(2,1)S(1)}, u32[]{:S(2)}, u32[]{:S(2)}) collective-permute-start(bf16[16,5120]{1,0:T(8,128)(2,1)S(1)} %add_convert_fusion), channel_id=1, source_target_pairs={{0,2},{2,0},{4,6},{6,4},{8,10},{10,8},{12,14},{14,12},{16,18},{18,... | collective-permute-start | bytes 491528 | tf_op jit(solution)/shard_map/ppermute | solution.py:381
  (5 other events, 3.4 us)

commit v2 on v1

--- a/solution.py
+++ b/solution.py
@@ -16,7 +16,7 @@
 OFFSET = 5
 TROWS = 8
 TILE = TROWS * COLS
-CHUNK = 512
+CHUNK = 2048
 STRIP = 48
 GRADS = 2 * (CHANS + HIDDEN)
 
@@ -160,7 +160,7 @@
             rs[row_of(i), :] = jnp.broadcast_to(inverse, (COLS, 128))
         return c
 
-    lax.fori_loop(0, TROWS, body, 0)
+    lax.fori_loop(0, TROWS, body, 0, unroll=8)
 
 
 def put_edges(edge, value, refs, step, inner):
@@ -286,7 +286,7 @@
         gos[row_of(i), :] = (g * scale[...]).astype(bf16)
         return c
 
-    lax.fori_loop(0, TROWS, rows, 0)
+    lax.fori_loop(0, TROWS, rows, 0, unroll=8)
     nb = nrm[...]
     go = gos[...]
     mi = mid_in[...]
@@ -303,7 +303,7 @@
     grads[:, 4608:5120] += t_dot(mid_out[...], go)
 
 
-PARAMS = dict(compiler_params=pltpu.CompilerParams(vmem_limit_bytes=60 * 2**20))
+PARAMS = dict(compiler_params=pltpu.CompilerParams(vmem_limit_bytes=26 * 2**20))
 SMEM = pl.BlockSpec(memory_space=pltpu.SMEM)
 ANY = pl.BlockSpec(memory_space=pl.ANY)
 HE = pltpu.VMEM((40 * 48, 128), f32)
@@ -312,11 +312,11 @@
 
 
 def fixed(*shape):
-    return pl.BlockSpec(shape, lambda t: (0,) * len(shape))
+    return pl.BlockSpec(shape, lambda t: (0,) * len(shape), pipeline_mode=pl.Buffered(1))
 
 
 def layer(l, *shape):
-    return pl.BlockSpec((None,) + shape, lambda t: (l,) + (0,) * len(shape))
+    return pl.BlockSpec((None,) + shape, lambda t: (l,) + (0,) * len(shape), pipeline_mode=pl.Buffered(1))
 
 
 def tiled(place, *shape):

time: 209 us -> 172 us (0.82)
  Pallas kernels: 111 us -> 73 us
  local copies, waits for them, and re-layouts: 18 us -> 23.3 us
  other arithmetic: 8.52 us -> 4.57 us
    pallas_call x9, Pallas kernels: 111 us -> 73 us  [call(): pl.pallas_call(kernel, grid=(grid,), out_shape=[jax.ShapeDtypeStruct(shap...]
    unnamed x44 -> x66, local copies, waits for them, and re-layouts: 6.19 us -> 19.2 us
    pallas_call x4, local copies, waits for them, and re-layouts: 3.92 us -> 0.35 us  [call(): pl.pallas_call(kernel, grid=(grid,), out_shape=[jax.ShapeDtypeStruct(shap...]
  transfers between devices with their start and end apart: 20 -> 20, of which waited for: 9 -> 9; matrix products, arithmetic and copies ran while one was open for 7% -> 3% of each run, Pallas kernels for 33% -> 28%
where the time goes in v2:
time: 172 us
  Pallas kernels  73 us (42%)
  starting transfers between devices  39.9 us (23%)
  waiting for transfers between devices  29.8 us (17%)
  local copies, waits for them, and re-layouts  23.3 us (14%)
  other arithmetic  4.57 us (3%)
    pallas_call x9, Pallas kernels, call(): pl.pallas_call(kernel, grid=(grid,), out_shape=[jax.ShapeDtypeStruct(shap...  73 us
    ppermute x6, waiting for transfers between devices, total(): other = lax.ppermute(part, ('row', 'col', 'rep'), pairs)  24 us
    ppermute x12, starting transfers between devices, swap(): return (lax.ppermute(v[1], axis, after), lax.ppermute(v[0], axis, before))  21.2 us
    unnamed x66, local copies, waits for them, and re-layouts  19.2 us
    ppermute x1, starting transfers between devices, total(): back = lax.ppermute(part, 'col', pair)  6.75 us
    ppermute x6, starting transfers between devices, total(): other = lax.ppermute(part, ('row', 'col', 'rep'), pairs)  6.55 us
    ppermute x1, starting transfers between devices, total(): part = (mine + lax.ppermute(other, 'col', pair).astype(f32)).astype(bf16)  5.44 us
    ppermute x12, waiting for transfers between devices, swap(): return (lax.ppermute(v[1], axis, after), lax.ppermute(v[0], axis, before))  3.76 us
  transfers between devices with their start and end apart: 20, of which 9 were waited for; matrix products, arithmetic and copies ran while one was open for 3% of the time, Pallas kernels for 28%

profile of v2, /device:TPU:1, one launch (start us, length us, event | category | flops | bytes accessed | tf_op | source)
XLA Modules:
  0.0 172.0 jit_solution(11926689210989907)
XLA Ops:
  0.7 1.9 %copy.83 = bf16[1,32,32,512]{3,1,2,0:T(8,128)(2,1)S(1)} copy(bf16[1,32,32,512]{3,2,1,0:T(8,128)(2,1)} %param.13) | data formatting | bytes 2097152 | tf_op args[0]
  2.7 3.6 %collective-permute-start.1 = (bf16[3,32,512]{2,0,1:T(4,128)(2,1)S(1)}, bf16[3,32,512]{2,0,1:T(4,128)(2,1)S(1)}, u32[]{:S(2)}, u32[]{:S(2)}) collective-permute-start(bf16[3,32,512]{2,0,1:T(4,128)(2,1)S(1)} %get-tuple-element.79), channel_id=1, source_target_pairs={{32,0},{64,32},{96,64},{0,96},{33,1},{65,33},{97,65},{1,97},{34,2}... | collective-permute-start | bytes 294920 | tf_op jit(solution)/shard_map/ppermute | solution.py:358
  7.6 3.7 %collective-permute-done = bf16[3,32,512]{2,0,1:T(4,128)(2,1)S(1)} collective-permute-done((bf16[3,32,512]{2,0,1:T(4,128)(2,1)S(1)}, bf16[3,32,512]{2,0,1:T(4,128)(2,1)S(1)}, u32[]{:S(2)}, u32[]{:S(2)}) %collective-permute-start) | collective-permute-done | bytes 98336 | tf_op jit(solution)/shard_map/ppermute | solution.py:358
  11.5 3.7 %collective-permute-start.2 = (bf16[3,48,512]{2,1,0:T(8,128)(2,1)S(1)}, bf16[3,48,512]{2,1,0:T(8,128)(2,1)S(1)}, u32[]{:S(2)}, u32[]{:S(2)}) collective-permute-start(bf16[3,48,512]{2,1,0:T(8,128)(2,1)S(1)} %pad_dynamic-update-slice_fusion.2), channel_id=1, source_target_pairs={{0,2},{2,4},{4,6},{6,8},{8,10},{10,12},{12,14},{14,16},{16,18},{18... | collective-permute-start | bytes 442376 | tf_op jit(solution)/shard_map/ppermute | solution.py:358
  16.2 2.2 %copy-done.10 = bf16[2,512,2048]{2,1,0:T(8,128)(2,1)S(1)} copy-done((bf16[2,512,2048]{2,1,0:T(8,128)(2,1)S(1)}, bf16[2,512,2048]{2,1,0:T(8,128)(2,1)}, u32[]{:S(2)}) %copy-start.10) | copy-done | bytes 4194328
  18.3 2.2 %copy-done.11 = bf16[2,2048,512]{2,1,0:T(8,128)(2,1)S(1)} copy-done((bf16[2,2048,512]{2,1,0:T(8,128)(2,1)S(1)}, bf16[2,2048,512]{2,1,0:T(8,128)(2,1)}, u32[]{:S(2)}) %copy-start.11) | copy-done | bytes 4194328
  20.5 2.5 %fold.1 = (bf16[2,512,2048]{2,1,0:T(8,128)(2,1)S(1)}, bf16[2,2048,512]{2,1,0:T(8,128)(2,1)S(1)}) custom-call(bf16[2,512,2048]{2,1,0:T(8,128)(2,1)S(1)} %copy-done.10, bf16[2,512,16]{2,1,0:T(8,128)(2,1)S(1)} %copy.59.ain, bf16[2,16,2048]{2,1,0:T(8,128)(2,1)S(1)} %copy-done.12, bf16[2,2048,512]{2,1,0:T(8,128)(2,1)S(1)} %copy-done.11, ...), custom_call_target="tpu_custom_call" | custom-call | tf_op jit(solution)/shard_map/fold/pallas_call | solution.py:327
  23.1 10.5 %conv.3.cv = f32[4096,128]{1,0:T(8,128)S(1)} custom-call(f32[4]{0:T(128)S(1)} %add_convert_fusion.7.flags, bf16[32,32,512]{2,1,0:T(8,128)(2,1)S(1)} %bitcast.52, bf16[3,32,512]{2,1,0:T(8,128)(2,1)S(1)} %copy.57.refs_1_, bf16[3,32,512]{2,1,0:T(8,128)(2,1)S(1)} %copy.58.refs_2_, f32[2,49,8,128]{3,2,1,0:T(8,128)S(1)} %copy.80.refs_3_.taps.refs_4_, ...), custom_call_target="tpu_custom_call" | custom-call | tf_op jit(solution)/shard_map/conv/pallas_call | solution.py:327
  33.7 6.2 %first_outer.1 = (bf16[1024,512]{1,0:T(8,128)(2,1)S(1)}, bf16[1024,2048]{1,0:T(8,128)(2,1)S(1)}, bf16[1024,2048]{1,0:T(8,128)(2,1)S(1)}, bf16[1024,16]{1,0:T(8,1...) custom-call(f32[4]{0:T(128)S(1)} %add_convert_fusion.7.flags, ...), custom_call_target="tpu_custom_call" | custom-call | tf_op jit(solution)/shard_map/first_outer/pallas_call | solution.py:327
  40.2 1.5 collective-permute-start.4
  41.7 6.1 %first_inner.1 = (bf16[1024,512]{1,0:T(8,128)(2,1)S(1)}, bf16[1024,2048]{1,0:T(8,128)(2,1)S(1)}, bf16[1024,2048]{1,0:T(8,128)(2,1)S(1)}, bf16[1024,16]{1,0:T(8,1...) custom-call(f32[4]{0:T(128)S(1)} %add_convert_fusion.7.flags, ...), custom_call_target="tpu_custom_call", output_to_operand_aliasing={{0}: (13, {}), {1}: (14, {}), {2}: (15, {}), {3}: (16, {}),... | custom-call | tf_op jit(solution)/shard_map/first_inner/pallas_call | solution.py:327
  47.9 2.0 %copy-done.3 = bf16[1024,2048]{1,0:T(8,128)(2,1)} copy-done((bf16[1024,2048]{1,0:T(8,128)(2,1)}, bf16[1024,2048]{1,0:T(8,128)(2,1)S(1)}, u32[]{:S(2)}) %copy-start.3) | copy-done | bytes 4194328
  50.9 2.3 %collective-permute-start.6 = (bf16[3,48,512]{2,1,0:T(8,128)(2,1)S(1)}, bf16[3,48,512]{2,1,0:T(8,128)(2,1)S(1)}, u32[]{:S(2)}, u32[]{:S(2)}) collective-permute-start(bf16[3,48,512]{2,1,0:T(8,128)(2,1)S(1)} %fusion.5), channel_id=1, source_target_pairs={{0,2},{2,4},{4,6},{6,8},{8,10},{10,12},{12,14},{14,16},{16,18},{18... | collective-permute-start | bytes 442376 | tf_op jit(solution)/shard_map/ppermute | solution.py:358
  53.3 2.4 %collective-permute-start.7 = (bf16[3,48,512]{2,1,0:T(8,128)(2,1)S(1)}, bf16[3,48,512]{2,1,0:T(8,128)(2,1)S(1)}, u32[]{:S(2)}, u32[]{:S(2)}) collective-permute-start(bf16[3,48,512]{2,1,0:T(8,128)(2,1)S(1)} %fusion.6), channel_id=1, source_target_pairs={{2,0},{4,2},{6,4},{8,6},{10,8},{12,10},{14,12},{16,14},{18,16},{20... | collective-permute-start | bytes 442376 | tf_op jit(solution)/shard_map/ppermute | solution.py:358
  55.7 10.4 %conv.4.cv = f32[4096,128]{1,0:T(8,128)S(1)} custom-call(f32[4]{0:T(128)S(1)} %add_convert_fusion.7.flags, bf16[16,32,512]{2,1,0:T(8,128)(2,1)S(1)} %get-tuple-element.45.refs_0_.x, bf16[16,32,512]{2,1,0:T(8,128)(2,1)S(1)} %get-tuple-element.44.refs_1_.x, bf16[3,32,512]{2,1,0:T(8,128)(2,1)S(1)} %copy.69.refs_2_, bf16[3,32,512]{2,1,0:T(8,128)(2,1)S(1)} %copy.70.refs_3_, ...), custom_call_target="tpu_custom_call" | custom-call | tf_op jit(solution)/shard_map/conv/pallas_call | solution.py:327
  66.2 10.1 %second_outer.1 = (bf16[32,32,512]{2,1,0:T(8,128)(2,1)}, f32[16,5120]{1,0:T(8,128)S(1)}, bf16[16,32,512]{2,1,0:T(8,128)(2,1)S(1)}, bf16[3,32,512]{2,1,0:T(8,128)...) custom-call(f32[4]{0:T(128)S(1)} %add_convert_fusion.7.flags, ...), custom_call_target="tpu_custom_call" | custom-call | tf_op jit(solution)/shard_map/second_outer/pallas_call | solution.py:327
  78.8 9.4 %second_inner.1 = (bf16[32,32,512]{2,1,0:T(8,128)(2,1)}, f32[16,5120]{1,0:T(8,128)S(1)}, bf16[16,32,512]{2,1,0:T(8,128)(2,1)S(1)}, bf16[3,16,512]{2,1,0:T(8,128)(2,1)S(1)}, bf16[3,16,512]{2,1,0:T(8,128)(2,1)S(1)}) custom-call(f32[4]{0:T(128)S(1)} %add_convert_fusion.7.flags, ...), custom_call_target="tpu_custom_call", output_to_operand_aliasing={{0}: (16, {})} | custom-call | tf_op jit(solution)/shard_map/second_inner/pallas_call | solution.py:327
  90.6 5.7 %collective-permute-start.11 = (bf16[3,48,512]{2,1,0:T(8,128)(2,1)}, bf16[3,48,512]{2,1,0:T(8,128)(2,1)S(1)}, u32[]{:S(2)}, u32[]{:S(2)}) collective-permute-start(bf16[3,48,512]{2,1,0:T(8,128)(2,1)} %fusion.8), channel_id=1, source_target_pairs={{2,0},{4,2},{6,4},{8,6},{10,8},{12,10},{14,12},{16,14},{18,16},{20... | collective-permute-start | bytes 442376 | tf_op jit(solution)/shard_map/ppermute | solution.py:358
  100.7 10.0 %conv.5.cv = f32[4096,128]{1,0:T(8,128)S(1)} custom-call(f32[4]{0:T(128)S(1)} %add_convert_fusion.7.flags, bf16[16,32,512]{2,1,0:T(8,128)(2,1)S(1)} %copy-done.17, bf16[16,32,512]{2,1,0:T(8,128)(2,1)S(1)} %copy-done.19, bf16[3,32,512]{2,1,0:T(8,128)(2,1)S(1)} %copy.77.refs_2_, bf16[3,32,512]{2,1,0:T(8,128)(2,1)S(1)} %copy.78.refs_3_, ...), custom_call_target="tpu_custom_call" | custom-call | tf_op jit(solution)/shard_map/conv/pallas_call | solution.py:327
  110.8 2.2 %copy-done.4 = bf16[1024,2048]{1,0:T(8,128)(2,1)S(1)} copy-done((bf16[1024,2048]{1,0:T(8,128)(2,1)S(1)}, bf16[1024,2048]{1,0:T(8,128)(2,1)}, u32[]{:S(2)}) %copy-start.4) | copy-done | bytes 4194328
  113.0 2.2 %copy-done.6 = bf16[1024,2048]{1,0:T(8,128)(2,1)S(1)} copy-done((bf16[1024,2048]{1,0:T(8,128)(2,1)S(1)}, bf16[1024,2048]{1,0:T(8,128)(2,1)}, u32[]{:S(2)}) %copy-start.6) | copy-done | bytes 4194328
  116.4 7.7 %third.1 = f32[16,5120]{1,0:T(8,128)S(1)} custom-call(f32[4]{0:T(128)S(1)} %add_convert_fusion.7.flags, bf16[32,32,512]{2,1,0:T(8,128)(2,1)S(1)} %bitcast.57, f32[4096,128]{1,0:T(8,128)S(1)} %conv.5.cv, bf16[3,48,512]{2,1,0:T(8,128)(2,1)S(1)} %collective-permute-done.10.w, bf16[3,48,512]{2,1,0:T(8,128)(2,1)S(1)} %collective-permute-done.11.e, ...), custom_call_target="tpu_custom_call" | custom-call | tf_op jit(solution)/shard_map/third/pallas_call | solution.py:327
  124.1 5.4 %collective-permute-start.12 = (bf16[16,5120]{1,0:T(8,128)(2,1)S(1)}, bf16[16,5120]{1,0:T(8,128)(2,1)S(1)}, u32[]{:S(2)}, u32[]{:S(2)}) collective-permute-start(bf16[16,5120]{1,0:T(8,128)(2,1)S(1)} %select_convert_fusion), channel_id=1, source_target_pairs={{0,2},{2,0},{4,6},{6,4},{8,10},{10,8},{12,14},{14,12},{16,18},{18,... | collective-permute-start | bytes 491528 | tf_op jit(solution)/shard_map/ppermute | solution.py:376
  130.8 4.5 %collective-permute-done.13 = bf16[16,5120]{1,0:T(8,128)(2,1)S(1)} collective-permute-done((bf16[16,5120]{1,0:T(8,128)(2,1)S(1)}, bf16[16,5120]{1,0:T(8,128)(2,1)S(1)}, u32[]{:S(2)}, u32[]{:S(2)}) %collective-permute-start.13) | collective-permute-done | bytes 163872 | tf_op jit(solution)/shard_map/ppermute | solution.py:379
  135.3 6.0 %collective-permute-done.14 = bf16[16,5120]{1,0:T(8,128)(2,1)S(1)} collective-permute-done((bf16[16,5120]{1,0:T(8,128)(2,1)S(1)}, bf16[16,5120]{1,0:T(8,128)(2,1)S(1)}, u32[]{:S(2)}, u32[]{:S(2)}) %collective-permute-start.14) | collective-permute-done | bytes 163872 | tf_op jit(solution)/shard_map/ppermute | solution.py:379
  142.6 3.0 %collective-permute-done.15 = bf16[16,5120]{1,0:T(8,128)(2,1)S(1)} collective-permute-done((bf16[16,5120]{1,0:T(8,128)(2,1)S(1)}, bf16[16,5120]{1,0:T(8,128)(2,1)S(1)}, u32[]{:S(2)}, u32[]{:S(2)}) %collective-permute-start.15) | collective-permute-done | bytes 163872 | tf_op jit(solution)/shard_map/ppermute | solution.py:379
  145.6 2.8 %collective-permute-start.16 = (bf16[16,5120]{1,0:T(8,128)(2,1)S(1)}, bf16[16,5120]{1,0:T(8,128)(2,1)S(1)}, u32[]{:S(2)}, u32[]{:S(2)}) collective-permute-start(bf16[16,5120]{1,0:T(8,128)(2,1)S(1)} %add_convert_fusion.3), channel_id=1, source_target_pairs={{0,8},{1,9},{2,18},{3,19},{4,12},{5,13},{6,22},{7,23},{8,0},{9,1},... | collective-permute-start | bytes 491528 | tf_op jit(solution)/shard_map/ppermute | solution.py:379
  148.5 2.9 %collective-permute-done.16 = bf16[16,5120]{1,0:T(8,128)(2,1)S(1)} collective-permute-done((bf16[16,5120]{1,0:T(8,128)(2,1)S(1)}, bf16[16,5120]{1,0:T(8,128)(2,1)S(1)}, u32[]{:S(2)}, u32[]{:S(2)}) %collective-permute-start.16) | collective-permute-done | bytes 163872 | tf_op jit(solution)/shard_map/ppermute | solution.py:379
  151.5 4.2 %collective-permute-done.17 = bf16[16,5120]{1,0:T(8,128)(2,1)S(1)} collective-permute-done((bf16[16,5120]{1,0:T(8,128)(2,1)S(1)}, bf16[16,5120]{1,0:T(8,128)(2,1)S(1)}, u32[]{:S(2)}, u32[]{:S(2)}) %collective-permute-start.17) | collective-permute-done | bytes 163872 | tf_op jit(solution)/shard_map/ppermute | solution.py:379
  155.7 2.2 %collective-permute-start.18 = (bf16[16,5120]{1,0:T(8,128)(2,1)S(1)}, bf16[16,5120]{1,0:T(8,128)(2,1)S(1)}, u32[]{:S(2)}, u32[]{:S(2)}) collective-permute-start(bf16[16,5120]{1,0:T(8,128)(2,1)S(1)} %add_convert_fusion.1), channel_id=1, source_target_pairs={{0,16},{1,17},{2,66},{3,67},{4,20},{5,21},{6,70},{7,71},{8,24},{9,... | collective-permute-start | bytes 491528 | tf_op jit(solution)/shard_map/ppermute | solution.py:379
  157.9 3.6 %collective-permute-done.18 = bf16[16,5120]{1,0:T(8,128)(2,1)S(1)} collective-permute-done((bf16[16,5120]{1,0:T(8,128)(2,1)S(1)}, bf16[16,5120]{1,0:T(8,128)(2,1)S(1)}, u32[]{:S(2)}, u32[]{:S(2)}) %collective-permute-start.18) | collective-permute-done | bytes 163872 | tf_op jit(solution)/shard_map/ppermute | solution.py:379
  161.5 6.8 %collective-permute-start.19 = (bf16[16,5120]{1,0:T(8,128)(2,1)S(1)}, bf16[16,5120]{1,0:T(8,128)(2,1)S(1)}, u32[]{:S(2)}, u32[]{:S(2)}) collective-permute-start(bf16[16,5120]{1,0:T(8,128)(2,1)S(1)} %add_convert_fusion), channel_id=1, source_target_pairs={{0,2},{2,0},{4,6},{6,4},{8,10},{10,8},{12,14},{14,12},{16,18},{18,... | collective-permute-start | bytes 491528 | tf_op jit(solution)/shard_map/ppermute | solution.py:381
  (135 shorter events, 20.9 us)
Async XLA Ops:
  0.6 14.7 %copy-start.24 = (f32[2,512]{1,0:T(2,128)S(1)}, f32[2,512]{1,0:T(2,128)}, u32[]{:S(2)}) copy-start(f32[2,512]{1,0:T(2,128)} %param.25) | copy-start | bytes 12292
  0.7 14.7 %copy-start.26 = (f32[2,512]{1,0:T(2,128)S(1)}, f32[2,512]{1,0:T(2,128)}, u32[]{:S(2)}) copy-start(f32[2,512]{1,0:T(2,128)} %param.18) | copy-start | bytes 12292
  0.7 14.7 %copy-start.27 = (f32[2,512]{1,0:T(2,128)S(1)}, f32[2,512]{1,0:T(2,128)}, u32[]{:S(2)}) copy-start(f32[2,512]{1,0:T(2,128)} %param.16) | copy-start | bytes 12292
  0.7 14.8 %copy-start.23 = (bf16[2,512,16]{1,2,0:T(8,128)(2,1)S(1)}, bf16[2,512,16]{1,2,0:T(8,128)(2,1)}, u32[]{:S(2)}) copy-start(bf16[2,512,16]{1,2,0:T(8,128)(2,1)} %param.21) | copy-start | bytes 98308
  0.7 15.0 %copy-start.22 = (bf16[2,2048,16]{1,2,0:T(8,128)(2,1)S(1)}, bf16[2,2048,16]{1,2,0:T(8,128)(2,1)}, u32[]{:S(2)}) copy-start(bf16[2,2048,16]{1,2,0:T(8,128)(2,1)} %param.23) | copy-start | bytes 393220
  0.7 15.4 %copy-start.15 = (bf16[2,16,512]{2,1,0:T(8,128)(2,1)S(1)}, bf16[2,16,512]{2,1,0:T(8,128)(2,1)}, u32[]{:S(2)}) copy-start(bf16[2,16,512]{2,1,0:T(8,128)(2,1)} %bout.7) | copy-start | bytes 98308
  0.7 15.4 %copy-start.12 = (bf16[2,16,2048]{2,1,0:T(8,128)(2,1)S(1)}, bf16[2,16,2048]{2,1,0:T(8,128)(2,1)}, u32[]{:S(2)}) copy-start(bf16[2,16,2048]{2,1,0:T(8,128)(2,1)} %bin_.7) | copy-start | bytes 393220
  2.7 8.7 %collective-permute-start.1 = (bf16[3,32,512]{2,0,1:T(4,128)(2,1)S(1)}, bf16[3,32,512]{2,0,1:T(4,128)(2,1)S(1)}, u32[]{:S(2)}, u32[]{:S(2)}) collective-permute-start(bf16[3,32,512]{2,0,1:T(4,128)(2,1)S(1)} %get-tuple-element.79), channel_id=1, source_target_pairs={{32,0},{64,32},{96,64},{0,96},{33,1},{65,33},{97,65},{1,97},{34,2}... | collective-permute-start | bytes 294920 | tf_op jit(solution)/shard_map/ppermute | solution.py:358
  6.3 5.0 %collective-permute-start = (bf16[3,32,512]{2,0,1:T(4,128)(2,1)S(1)}, bf16[3,32,512]{2,0,1:T(4,128)(2,1)S(1)}, u32[]{:S(2)}, u32[]{:S(2)}) collective-permute-start(bf16[3,32,512]{2,0,1:T(4,128)(2,1)S(1)} %get-tuple-element.80), channel_id=1, source_target_pairs={{0,32},{32,64},{64,96},{96,0},{1,33},{33,65},{65,97},{97,1},{2,34}... | collective-permute-start | bytes 294920 | tf_op jit(solution)/shard_map/ppermute | solution.py:358
  11.5 22.2 %collective-permute-start.2 = (bf16[3,48,512]{2,1,0:T(8,128)(2,1)S(1)}, bf16[3,48,512]{2,1,0:T(8,128)(2,1)S(1)}, u32[]{:S(2)}, u32[]{:S(2)}) collective-permute-start(bf16[3,48,512]{2,1,0:T(8,128)(2,1)S(1)} %pad_dynamic-update-slice_fusion.2), channel_id=1, source_target_pairs={{0,2},{2,4},{4,6},{6,8},{8,10},{10,12},{12,14},{14,16},{16,18},{18... | collective-permute-start | bytes 442376 | tf_op jit(solution)/shard_map/ppermute | solution.py:358
  15.2 18.5 %collective-permute-start.3 = (bf16[3,48,512]{2,1,0:T(8,128)(2,1)S(1)}, bf16[3,48,512]{2,1,0:T(8,128)(2,1)S(1)}, u32[]{:S(2)}, u32[]{:S(2)}) collective-permute-start(bf16[3,48,512]{2,1,0:T(8,128)(2,1)S(1)} %pad_dynamic-update-slice_fusion), channel_id=1, source_target_pairs={{2,0},{4,2},{6,4},{8,6},{10,8},{12,10},{14,12},{16,14},{18,16},{20... | collective-permute-start | bytes 442376 | tf_op jit(solution)/shard_map/ppermute | solution.py:358
  23.0 55.8 %copy-start = (bf16[2,2048,512]{2,1,0:T(8,128)(2,1)}, bf16[2,2048,512]{2,1,0:T(8,128)(2,1)S(1)}, u32[]{:S(2)}) copy-start(bf16[2,2048,512]{2,1,0:T(8,128)(2,1)S(1)} %get-tuple-element.38.wout) | copy-start | bytes 12582916
  40.0 10.8 %collective-permute-start.5 = (bf16[3,32,512]{2,0,1:T(4,128)(2,1)S(1)}, bf16[3,32,512]{2,0,1:T(4,128)(2,1)S(1)}, u32[]{:S(2)}, u32[]{:S(2)}) collective-permute-start(bf16[3,32,512]{2,0,1:T(4,128)(2,1)S(1)} %copy.68), channel_id=1, source_target_pairs={{32,0},{64,32},{96,64},{0,96},{33,1},{65,33},{97,65},{1,97},{34,2}... | collective-permute-start | bytes 294920 | tf_op jit(solution)/shard_map/ppermute | solution.py:358
  40.2 10.7 %collective-permute-start.4 = (bf16[3,32,512]{2,0,1:T(4,128)(2,1)S(1)}, bf16[3,32,512]{2,0,1:T(4,128)(2,1)S(1)}, u32[]{:S(2)}, u32[]{:S(2)}) collective-permute-start(bf16[3,32,512]{2,0,1:T(4,128)(2,1)S(1)} %copy.67), channel_id=1, source_target_pairs={{0,32},{32,64},{64,96},{96,0},{1,33},{33,65},{65,97},{97,1},{2,34}... | collective-permute-start | bytes 294920 | tf_op jit(solution)/shard_map/ppermute | solution.py:358
  50.8 25.4 %copy-start.5 = (bf16[1024,2048]{1,0:T(8,128)(2,1)}, bf16[1024,2048]{1,0:T(8,128)(2,1)S(1)}, u32[]{:S(2)}) copy-start(bf16[1024,2048]{1,0:T(8,128)(2,1)S(1)} %get-tuple-element.65.slope) | copy-start | bytes 12582916
  50.8 25.4 %copy-start.13 = (bf16[1024,16]{1,0:T(8,128)(2,1)}, bf16[1024,16]{1,0:T(8,128)(2,1)S(1)}, u32[]{:S(2)}) copy-start(bf16[1024,16]{1,0:T(8,128)(2,1)S(1)} %get-tuple-element.67.mid_out) | copy-start | bytes 98308
  50.8 15.3 %copy-start.7 = (bf16[1,32,32,512]{3,2,1,0:T(8,128)(2,1)S(1)}, bf16[1,32,32,512]{3,2,1,0:T(8,128)(2,1)}, u32[]{:S(2)}) copy-start(bf16[1,32,32,512]{3,2,1,0:T(8,128)(2,1)} %param.14) | copy-start | bytes 3145732
  50.9 15.2 %collective-permute-start.6 = (bf16[3,48,512]{2,1,0:T(8,128)(2,1)S(1)}, bf16[3,48,512]{2,1,0:T(8,128)(2,1)S(1)}, u32[]{:S(2)}, u32[]{:S(2)}) collective-permute-start(bf16[3,48,512]{2,1,0:T(8,128)(2,1)S(1)} %fusion.5), channel_id=1, source_target_pairs={{0,2},{2,4},{4,6},{6,8},{8,10},{10,12},{12,14},{14,16},{16,18},{18... | collective-permute-start | bytes 442376 | tf_op jit(solution)/shard_map/ppermute | solution.py:358
  53.3 12.9 %collective-permute-start.7 = (bf16[3,48,512]{2,1,0:T(8,128)(2,1)S(1)}, bf16[3,48,512]{2,1,0:T(8,128)(2,1)S(1)}, u32[]{:S(2)}, u32[]{:S(2)}) collective-permute-start(bf16[3,48,512]{2,1,0:T(8,128)(2,1)S(1)} %fusion.6), channel_id=1, source_target_pairs={{2,0},{4,2},{6,4},{8,6},{10,8},{12,10},{14,12},{16,14},{18,16},{20... | collective-permute-start | bytes 442376 | tf_op jit(solution)/shard_map/ppermute | solution.py:358
  77.1 11.9 %collective-permute-start.9 = (bf16[3,32,512]{2,0,1:T(4,128)(2,1)S(1)}, bf16[3,32,512]{2,0,1:T(4,128)(2,1)S(1)}, u32[]{:S(2)}, u32[]{:S(2)}) collective-permute-start(bf16[3,32,512]{2,0,1:T(4,128)(2,1)S(1)} %copy.76), channel_id=1, source_target_pairs={{32,0},{64,32},{96,64},{0,96},{33,1},{65,33},{97,65},{1,97},{34,2}... | collective-permute-start | bytes 294920 | tf_op jit(solution)/shard_map/ppermute | solution.py:358
  78.5 10.6 %collective-permute-start.8 = (bf16[3,32,512]{2,0,1:T(4,128)(2,1)S(1)}, bf16[3,32,512]{2,0,1:T(4,128)(2,1)S(1)}, u32[]{:S(2)}, u32[]{:S(2)}) collective-permute-start(bf16[3,32,512]{2,0,1:T(4,128)(2,1)S(1)} %copy.75), channel_id=1, source_target_pairs={{0,32},{32,64},{64,96},{96,0},{1,33},{33,65},{65,97},{97,1},{2,34}... | collective-permute-start | bytes 294920 | tf_op jit(solution)/shard_map/ppermute | solution.py:358
  89.0 21.7 %copy-start.14 = (bf16[1024,16]{1,0:T(8,128)(2,1)S(1)}, bf16[1024,16]{1,0:T(8,128)(2,1)}, u32[]{:S(2)}) copy-start(bf16[1024,16]{1,0:T(8,128)(2,1)} %copy-done.13) | copy-start | bytes 98308
  89.8 21.0 %collective-permute-start.10 = (bf16[3,48,512]{2,1,0:T(8,128)(2,1)}, bf16[3,48,512]{2,1,0:T(8,128)(2,1)S(1)}, u32[]{:S(2)}, u32[]{:S(2)}) collective-permute-start(bf16[3,48,512]{2,1,0:T(8,128)(2,1)} %fusion.7), channel_id=1, source_target_pairs={{0,2},{2,4},{4,6},{6,8},{8,10},{10,12},{12,14},{14,16},{16,18},{18... | collective-permute-start | bytes 442376 | tf_op jit(solution)/shard_map/ppermute | solution.py:358
  90.6 20.1 %collective-permute-start.11 = (bf16[3,48,512]{2,1,0:T(8,128)(2,1)}, bf16[3,48,512]{2,1,0:T(8,128)(2,1)S(1)}, u32[]{:S(2)}, u32[]{:S(2)}) collective-permute-start(bf16[3,48,512]{2,1,0:T(8,128)(2,1)} %fusion.8), channel_id=1, source_target_pairs={{2,0},{4,2},{6,4},{8,6},{10,8},{12,10},{14,12},{16,14},{18,16},{20... | collective-permute-start | bytes 442376 | tf_op jit(solution)/shard_map/ppermute | solution.py:358
  124.1 6.5 %collective-permute-start.12 = (bf16[16,5120]{1,0:T(8,128)(2,1)S(1)}, bf16[16,5120]{1,0:T(8,128)(2,1)S(1)}, u32[]{:S(2)}, u32[]{:S(2)}) collective-permute-start(bf16[16,5120]{1,0:T(8,128)(2,1)S(1)} %select_convert_fusion), channel_id=1, source_target_pairs={{0,2},{2,0},{4,6},{6,4},{8,10},{10,8},{12,14},{14,12},{16,18},{18,... | collective-permute-start | bytes 491528 | tf_op jit(solution)/shard_map/ppermute | solution.py:376
  130.7 4.5 %collective-permute-start.13 = (bf16[16,5120]{1,0:T(8,128)(2,1)S(1)}, bf16[16,5120]{1,0:T(8,128)(2,1)S(1)}, u32[]{:S(2)}, u32[]{:S(2)}) collective-permute-start(bf16[16,5120]{1,0:T(8,128)(2,1)S(1)} %add_convert_fusion.6), channel_id=1, source_target_pairs={{0,32},{1,33},{2,6},{3,7},{4,36},{5,37},{6,2},{7,3},{8,40},{9,41},... | collective-permute-start | bytes 491528 | tf_op jit(solution)/shard_map/ppermute | solution.py:379
  135.3 6.0 %collective-permute-start.14 = (bf16[16,5120]{1,0:T(8,128)(2,1)S(1)}, bf16[16,5120]{1,0:T(8,128)(2,1)S(1)}, u32[]{:S(2)}, u32[]{:S(2)}) collective-permute-start(bf16[16,5120]{1,0:T(8,128)(2,1)S(1)} %add_convert_fusion.5), channel_id=1, source_target_pairs={{0,64},{1,65},{2,10},{3,11},{4,68},{5,69},{6,14},{7,15},{8,72},{9,... | collective-permute-start | bytes 491528 | tf_op jit(solution)/shard_map/ppermute | solution.py:379
  141.3 4.2 %collective-permute-start.15 = (bf16[16,5120]{1,0:T(8,128)(2,1)S(1)}, bf16[16,5120]{1,0:T(8,128)(2,1)S(1)}, u32[]{:S(2)}, u32[]{:S(2)}) collective-permute-start(bf16[16,5120]{1,0:T(8,128)(2,1)S(1)} %add_convert_fusion.4), channel_id=1, source_target_pairs={{0,4},{1,5},{2,3},{3,2},{4,0},{5,1},{6,7},{7,6},{8,12},{9,13},{10,... | collective-permute-start | bytes 491528 | tf_op jit(solution)/shard_map/ppermute | solution.py:379
  145.6 5.8 %collective-permute-start.16 = (bf16[16,5120]{1,0:T(8,128)(2,1)S(1)}, bf16[16,5120]{1,0:T(8,128)(2,1)S(1)}, u32[]{:S(2)}, u32[]{:S(2)}) collective-permute-start(bf16[16,5120]{1,0:T(8,128)(2,1)S(1)} %add_convert_fusion.3), channel_id=1, source_target_pairs={{0,8},{1,9},{2,18},{3,19},{4,12},{5,13},{6,22},{7,23},{8,0},{9,1},... | collective-permute-start | bytes 491528 | tf_op jit(solution)/shard_map/ppermute | solution.py:379
  151.4 4.2 %collective-permute-start.17 = (bf16[16,5120]{1,0:T(8,128)(2,1)S(1)}, bf16[16,5120]{1,0:T(8,128)(2,1)S(1)}, u32[]{:S(2)}, u32[]{:S(2)}) collective-permute-start(bf16[16,5120]{1,0:T(8,128)(2,1)S(1)} %add_convert_fusion.2), channel_id=1, source_target_pairs={{0,1},{1,0},{2,34},{3,35},{4,5},{5,4},{6,38},{7,39},{8,9},{9,8},{1... | collective-permute-start | bytes 491528 | tf_op jit(solution)/shard_map/ppermute | solution.py:379
  155.7 5.8 %collective-permute-start.18 = (bf16[16,5120]{1,0:T(8,128)(2,1)S(1)}, bf16[16,5120]{1,0:T(8,128)(2,1)S(1)}, u32[]{:S(2)}, u32[]{:S(2)}) collective-permute-start(bf16[16,5120]{1,0:T(8,128)(2,1)S(1)} %add_convert_fusion.1), channel_id=1, source_target_pairs={{0,16},{1,17},{2,66},{3,67},{4,20},{5,21},{6,70},{7,71},{8,24},{9,... | collective-permute-start | bytes 491528 | tf_op jit(solution)/shard_map/ppermute | solution.py:379
  161.5 7.8 %collective-permute-start.19 = (bf16[16,5120]{1,0:T(8,128)(2,1)S(1)}, bf16[16,5120]{1,0:T(8,128)(2,1)S(1)}, u32[]{:S(2)}, u32[]{:S(2)}) collective-permute-start(bf16[16,5120]{1,0:T(8,128)(2,1)S(1)} %add_convert_fusion), channel_id=1, source_target_pairs={{0,2},{2,0},{4,6},{6,4},{8,10},{10,8},{12,14},{14,12},{16,18},{18,... | collective-permute-start | bytes 491528 | tf_op jit(solution)/shard_map/ppermute | solution.py:381
  (16 other events, 51.5 us)

commit v3 on v2

--- a/solution.py
+++ b/solution.py
@@ -14,6 +14,7 @@
 HALF = COLS // 2
 SPAN = 32
 OFFSET = 5
+WIDE = HALF + 6
 TROWS = 8
 TILE = TROWS * COLS
 CHUNK = 2048
@@ -51,42 +52,38 @@
 
 
 def conv_kernel(sources, flip, flags, *refs):
-    xrefs, (n, s, taps, bias, cv, xs) = refs[: len(sources)], refs[len(sources) :]
+    xrefs, (n, s, taps, cv, held, spans, lines) = refs[: len(sources)], refs[len(sources) :]
     step = pl.program_id(0)
+    zero = jnp.zeros((8, 128), f32)
+    left = lax.broadcasted_iota(jnp.int32, (8, 128), 0) < GROUPS
+
+    def take(row):
+        spread(spans, 0, held[row].astype(f32))
+        base = pl.multiple_of(row * (WIDE * 8), WIDE * 8)
+        for k in range(WIDE):
+            reg = spans[(OFFSET + k) * 8 : (OFFSET + k) * 8 + 8, :]
+            if k < 3:
+                reg = jnp.where(left, zero, reg)
+            if k >= HALF + 3:
+                reg = jnp.where(left, reg, zero)
+            lines[pl.ds(base + k * 8, 8), :] = reg
 
     @pl.when(step == 0)
     def _():
-        zero = jnp.zeros((8, 128), f32)
         for ref, pieces in zip(xrefs, sources):
             for at, row, count in pieces:
-
-                def centre(i, c, ref=ref, at=at, row=row):
-                    spread(xs, row + 3 + i, ref[at + i].astype(f32))
-                    return c
-
-                lax.fori_loop(0, count, centre, 0)
-        for i in range(3):
-            spread(xs, i, n[i].astype(f32) * flags[0])
-            spread(xs, ROWS + 3 + i, s[i].astype(f32) * flags[1])
-        left = lax.broadcasted_iota(jnp.int32, (8, 128), 0) < GROUPS
-
-        def edge(r, c):
-            for k in (5, 6, 7):
-                at = pl.ds(pl.multiple_of((r * SPAN + k) * 8, 8), 8)
-                xs[at, :] = jnp.where(left, zero, xs[at, :])
-            for k in (24, 25, 26):
-                at = pl.ds(pl.multiple_of((r * SPAN + k) * 8, 8), 8)
-                xs[at, :] = jnp.where(left, xs[at, :], zero)
-            return c
-
-        lax.fori_loop(0, ROWS + 6, edge, 0)
+                held[row + 3 : row + 3 + count] = ref[at : at + count]
+        held[0:3] = (n[...].astype(f32) * flags[0]).astype(bf16)
+        held[ROWS + 3 : ROWS + 6] = (s[...].astype(f32) * flags[1]).astype(bf16)
+        held[ROWS + 6 :] = jnp.zeros((2, COLS, CHANS), bf16)
+        lax.fori_loop(0, 38, lambda r, c: (take(r), c)[1], 0)
 
     def row(i, c):
-        first = jnp.zeros((8, 128), f32) if flip else bias[...]
-        totals = [first] * HALF
+        at = step * TROWS + i
+        totals = [zero] * HALF
         for a in range(7):
-            base = pl.multiple_of((step * TROWS + i + a) * (SPAN * 8), SPAN * 8)
-            line = [xs[pl.ds(base + (OFFSET + k) * 8, 8), :] for k in range(HALF + 6)]
+            base = pl.multiple_of((at + a) * (WIDE * 8), WIDE * 8)
+            line = [lines[pl.ds(base + k * 8, 8), :] for k in range(WIDE)]
             for b in range(7):
                 tap = taps[48 - (a * 7 + b) if flip else a * 7 + b]
                 for k in range(HALF):
@@ -148,13 +145,13 @@
     return pl.ds(pl.multiple_of(i * COLS, COLS), COLS)
 
 
-def norm_rows(cv, he, taps, line, tile, gain, shift, nrm, xh=None, rs=None):
+def norm_rows(cv, he, taps, line, tile, bias, gain, shift, nrm, xh=None, rs=None):
     def body(i, c):
-        conv = whole_row(cv, he, taps, False, line, tile, i)
+        conv = whole_row(cv, he, taps, False, line, tile, i) + bias
         centred = conv - jnp.mean(conv, -1, keepdims=True)
         inverse = lax.rsqrt(jnp.mean(centred * centred, -1, keepdims=True) + norm_eps)
         standard = centred * inverse
-        nrm[row_of(i), :] = (standard * gain[...] + shift[...]).astype(bf16)
+        nrm[row_of(i), :] = (standard * gain + shift).astype(bf16)
         if xh is not None:
             xh[row_of(i), :] = standard
             rs[row_of(i), :] = jnp.broadcast_to(inverse, (COLS, 128))
@@ -185,13 +182,51 @@
             east[c, at, cs] = edge[pl.ds(COLS - 3 + c, 8, stride=COLS), :].astype(bf16)
 
 
-def fold_kernel(win, ain, bin_, wout, aout, bout, win_out, wout_out):
-    win_out[...] = (win[...].astype(f32) + adapter_scale * dot(ain[...], bin_[...])).astype(bf16)
-    wout_out[...] = (wout[...].astype(f32) + adapter_scale * dot(aout[...], bout[...])).astype(bf16)
-
-
-def first_kernel(inner, flags, x, cv, w, e, taps, gain, shift, win, wout, ain, aout, scale, *refs):
+def edge_kernel(first, last, west, east, edge):
+    for ref, out, at in ((first, west, 0), (last, east, 5)):
+        for g in range(GROUPS):
+            cs = slice(128 * g, 128 * g + 128)
+            edge[...] = ref[:, :, cs].reshape(ROWS * 8, 128).astype(f32)
+            for c in range(3):
+                out[c, :, cs] = edge[pl.ds(at + c, ROWS, stride=8), :].astype(bf16)
+
+
+def pack_kernel(split, *refs):
+    pieces, (n, s, west, east) = refs[:-4], refs[-4:]
+    for side, out in ((0, west), (1, east)):
+        if split:
+            out[:, 0:16] = pieces[2 * side][...]
+            out[:, 16:32] = pieces[2 * side + 1][...]
+        else:
+            v = pieces[side]
+            for block, row in enumerate((0, 24, 8, 16)):
+                out[:, 8 * block : 8 * block + 8] = v[:, row : row + 8]
+        for at, ref in ((32, n), (40, s)):
+            cut = slice(COLS - 8, COLS) if side else slice(0, 8)
+            v = [ref[r, cut, :].astype(f32) for r in range(3)]
+            for c in range(3):
+                k = c + 5 if side else c
+                rows = [v[r][k : k + 1] for r in range(3)] + [jnp.zeros((5, CHANS), f32)]
+                out[c, at : at + 8] = jnp.concatenate(rows, axis=0).astype(bf16)
+
+
+def fold_kernel(win, ain, bin_, wout, aout, bout, filters, win_out, wout_out, taps):
+    @pl.when((pl.program_id(0) == 0) & (pl.program_id(1) == 0))
+    def _():
+        for t in range(49):
+            v = filters[t]
+            for l in range(2):
+                for g in range(8):
+                    at = 128 * (g % GROUPS)
+                    taps[l, t, g : g + 1, :] = v[l : l + 1, at : at + 128]
+
+    win_out[...] = (win[...].astype(f32) + adapter_scale * t_dot(ain[...], bin_[...])).astype(bf16)
+    wout_out[...] = (wout[...].astype(f32) + adapter_scale * t_dot(aout[...], bout[...])).astype(bf16)
+
+
+def first_kernel(inner, flags, x, cv, w, e, taps, bias, gain, shift, scale, win, wout, ain, aout, *refs):
     refs = refs[5 if inner else 0 :]
+    bias, gain, shift, scale = (v[0:1, :] for v in (bias, gain, shift, scale))
     nrm, hid, slope, mid_in, mid_out, y = refs[:6]
     edges, (he, line, edge) = refs[6:-3], refs[-3:]
     step = pl.program_id(0)
@@ -201,9 +236,9 @@
     def _():
         hold_strips(he, w, e, flags)
 
-    norm_rows(cv, he, taps, line, tile, gain, shift, nrm)
+    norm_rows(cv, he, taps, line, tile, bias, gain, shift, nrm)
     nb = nrm[...]
-    mid_in[...] = dot(nb, ain[...]).astype(bf16)
+    mid_in[...] = dot_t(nb, ain[...]).astype(bf16)
     out = jnp.zeros((TILE, CHANS), f32)
     mid = jnp.zeros((TILE, RANK), f32)
     for c in range(0, HIDDEN, CHUNK):
@@ -213,16 +248,17 @@
         hid[:, cs] = h
         slope[:, cs] = sl.astype(bf16)
         out = out + dot(h, wout[cs, :])
-        mid = mid + dot(h, aout[cs, :])
+        mid = mid + dot_t(h, aout[:, cs])
     mid_out[...] = mid.astype(bf16)
-    result = x[...].reshape(TILE, CHANS).astype(f32) + scale[...] * out
+    result = x[...].reshape(TILE, CHANS).astype(f32) + scale * out
     y[...] = result.reshape(TROWS, COLS, CHANS).astype(bf16)
     put_edges(edge, result, edges, step, inner)
 
 
 def second_kernel(
-    inner, flags, x, cv, w, e, taps, gain, shift, win, wout, ain, bin_, aout, bout, scale, cot, *refs
+    inner, flags, x, cv, w, e, taps, bias, gain, shift, scale, win, wout, ain, aout, bin_, bout, cot, *refs
 ):
+    bias, gain, shift, scale = (v[1:2, :] for v in (bias, gain, shift, scale))
     if inner:
         before, refs = refs[1], refs[2:]
     out_ref, grads, gc = refs[:3]
@@ -235,10 +271,10 @@
         hold_strips(he, w, e, flags)
         grads[...] = before[...] if inner else jnp.zeros_like(grads)
 
-    norm_rows(cv, he, taps, line, tile, gain, shift, nrm, xh, rs)
+    norm_rows(cv, he, taps, line, tile, bias, gain, shift, nrm, xh, rs)
     nb = nrm[...]
-    go = (cot[...].reshape(TILE, CHANS).astype(f32) * scale[...]).astype(bf16)
-    mid_in = dot(nb, ain[...]).astype(bf16)
+    go = (cot[...].reshape(TILE, CHANS).astype(f32) * scale).astype(bf16)
+    mid_in = dot_t(nb, ain[...]).astype(bf16)
     gm_out = (adapter_scale * dot_t(go, bout[...])).astype(bf16)
     out = jnp.zeros((TILE, CHANS), f32)
     gn = jnp.zeros((TILE, CHANS), f32)
@@ -250,7 +286,7 @@
         h = value.astype(bf16)
         gpre = (dot_t(go, wout[cs, :]) * sl).astype(bf16)
         out = out + dot(h, wout[cs, :])
-        mid = mid + dot(h, aout[cs, :])
+        mid = mid + dot_t(h, aout[:, cs])
         gn = gn + dot_t(gpre, win[:, cs])
         gm_in = gm_in + dot_t(gpre, bin_[:, cs])
         grads[:, 512 + c : 512 + c + CHUNK] += t_dot(mid_in, gpre)
@@ -258,9 +294,9 @@
     gm_in = (adapter_scale * gm_in).astype(bf16)
     grads[:, 0:512] += t_dot(gm_in, nb)
     grads[:, 4608:5120] += t_dot(mid.astype(bf16), go)
-    result = x[...].reshape(TILE, CHANS).astype(f32) + scale[...] * out
+    result = x[...].reshape(TILE, CHANS).astype(f32) + scale * out
     out_ref[...] = result.reshape(TROWS, COLS, CHANS).astype(bf16)
-    u = gn * gain[...]
+    u = gn * gain
     standard = xh[...]
     m1 = jnp.mean(u, -1, keepdims=True)
     m2 = jnp.mean(u * standard, -1, keepdims=True)
@@ -271,39 +307,51 @@
 
 
 def third_kernel(
-    flags, cot, cv, w, e, taps, scale, wout, bin_, bout, nrm, hid, slope, mid_in, mid_out,
-    grads, he, line, gos,
+    flags, cot, cv, w, e, taps, scale, wout, bin_, bout, mid_in, mid_out, nrm_far, hid_far, slope_far,
+    grads, he, line, gos, nrm, hid, slope, sems,
 ):
     step = pl.program_id(0)
+    scale = scale[0:1, :]
+
+    def copies(t):
+        at = pl.ds(pl.multiple_of(t * TILE, TILE), TILE)
+        return [
+            pltpu.make_async_copy(far.at[at, :], near.at[t], sems.at[k, t])
+            for k, (far, near) in enumerate(((nrm_far, nrm), (hid_far, hid), (slope_far, slope)))
+        ]
 
     @pl.when(step == 0)
     def _():
+        for t in range(PIXELS // TILE):
+            for copy in copies(t):
+                copy.start()
         hold_strips(he, w, e, flags)
         grads[...] = jnp.zeros_like(grads)
 
     def rows(i, c):
         g = cot[i].astype(f32) + whole_row(cv, he, taps, True, line, step, i)
-        gos[row_of(i), :] = (g * scale[...]).astype(bf16)
+        gos[row_of(i), :] = (g * scale).astype(bf16)
         return c
 
     lax.fori_loop(0, TROWS, rows, 0, unroll=8)
-    nb = nrm[...]
+    for copy in copies(step):
+        copy.wait()
+    nb = nrm[step]
     go = gos[...]
     mi = mid_in[...]
     gm_out = (adapter_scale * dot_t(go, bout[...])).astype(bf16)
     gm_in = jnp.zeros((TILE, RANK), f32)
     for c in range(0, HIDDEN, CHUNK):
         cs = slice(c, c + CHUNK)
-        gpre = (dot_t(go, wout[cs, :]) * slope[:, cs].astype(f32)).astype(bf16)
+        gpre = (dot_t(go, wout[cs, :]) * slope[step, :, cs].astype(f32)).astype(bf16)
         gm_in = gm_in + dot_t(gpre, bin_[:, cs])
         grads[:, 512 + c : 512 + c + CHUNK] += t_dot(mi, gpre)
-        grads[:, 2560 + c : 2560 + c + CHUNK] += t_dot(gm_out, hid[:, cs])
+        grads[:, 2560 + c : 2560 + c + CHUNK] += t_dot(gm_out, hid[step, :, cs])
     gm_in = (adapter_scale * gm_in).astype(bf16)
     grads[:, 0:512] += t_dot(gm_in, nb)
     grads[:, 4608:5120] += t_dot(mid_out[...], go)
 
 
-PARAMS = dict(compiler_params=pltpu.CompilerParams(vmem_limit_bytes=26 * 2**20))
 SMEM = pl.BlockSpec(memory_space=pltpu.SMEM)
 ANY = pl.BlockSpec(memory_space=pl.ANY)
 HE = pltpu.VMEM((40 * 48, 128), f32)
@@ -312,7 +360,7 @@
 
 
 def fixed(*shape):
-    return pl.BlockSpec(shape, lambda t: (0,) * len(shape), pipeline_mode=pl.Buffered(1))
+    return pl.BlockSpec(shape, lambda *t: (0,) * len(shape), pipeline_mode=pl.Buffered(1))
 
 
 def layer(l, *shape):
@@ -323,21 +371,21 @@
     return pl.BlockSpec(shape, lambda t: (place(t),) + (0,) * (len(shape) - 1))
 
 
-def call(kernel, name, grid, ins, outs, scratch, aliases={}):
+def call(kernel, name, grid, ins, outs, scratch, aliases={}, limit=26):
     return pl.pallas_call(
         kernel,
-        grid=(grid,),
+        grid=grid if isinstance(grid, tuple) else (grid,),
         out_shape=[jax.ShapeDtypeStruct(shape, dtype) for shape, dtype, _ in outs],
         in_specs=[spec for _, spec in ins],
         out_specs=[spec for _, _, spec in outs],
         scratch_shapes=scratch,
         input_output_aliases=aliases,
         name=name,
-        **PARAMS,
+        compiler_params=pltpu.CompilerParams(vmem_limit_bytes=limit * 2**20),
     )(*[array for array, _ in ins])
 
 
-def conv(arrays, sources, n, s, taps, bias, l, flip, flags):
+def conv(arrays, sources, n, s, taps, l, flip, flags):
     return call(
         functools.partial(conv_kernel, sources, flip),
         "conv",
@@ -345,9 +393,14 @@
         [(flags, SMEM)]
         + [(a, fixed(*a.shape)) for a in arrays]
         + [(n, fixed(3, COLS, CHANS)), (s, fixed(3, COLS, CHANS))]
-        + [(taps, layer(l, 49, 8, 128)), (bias, layer(l, 8, 128))],
+        + [(taps, layer(l, 49, 8, 128))],
         [((PIXELS * 4, 128), f32, tiled(lambda t: t, TILE * 4, 128))],
-        [pltpu.VMEM((40 * SPAN * 8, 128), f32)],
+        [
+            pltpu.VMEM((40, COLS, CHANS), bf16),
+            pltpu.VMEM((SPAN * 8, 128), f32),
+            pltpu.VMEM((40 * WIDE * 8, 128), f32),
+        ],
+        limit=12,
     )[0]
 
 
@@ -358,13 +411,16 @@
     return lax.ppermute(v[1], axis, after), lax.ppermute(v[0], axis, before)
 
 
-def strips(outer, inner, north, south):
-    sent = []
-    for side, cut in ((0, slice(0, 3)), (1, slice(COLS - 3, COLS))):
-        corners = [
-            jnp.pad(v[:, cut].transpose(1, 0, 2), ((0, 0), (0, 5), (0, 0))) for v in (north, south)
-        ]
-        sent.append(jnp.concatenate([outer[side], inner[side], *corners], axis=1))
+def strips(columns, north, south):
+    sent = call(
+        functools.partial(pack_kernel, len(columns) == 4),
+        "pack",
+        1,
+        [(v, fixed(*v.shape)) for v in (*columns, north, south)],
+        [((3, STRIP, CHANS), bf16, fixed(3, STRIP, CHANS))] * 2,
+        [],
+        limit=6,
+    )
     return swap(sent, "col")
 
 
@@ -404,51 +460,57 @@
 ):
     x0 = features.reshape(ROWS, COLS, CHANS)
     cot = cotangent.reshape(ROWS, COLS, CHANS)
-    ain, bin_, aout, bout = inner_down_factor, inner_up_factor, outer_down_factor, outer_up_factor
-    taps = depthwise_filters.reshape(2, 49, GROUPS, 128)
-    taps = jnp.concatenate([taps, taps], axis=2)
-    bias = depthwise_bias_vector.reshape(2, GROUPS, 128)
-    bias = jnp.concatenate([bias, bias], axis=1)
-    gain, shift, scale = (
-        v.reshape(2, 1, CHANS) for v in (layernorm_gain, layernorm_shift, branch_channel_scale)
+    ain, bin_ = inner_down_factor.transpose(0, 2, 1), inner_up_factor
+    aout, bout = outer_down_factor.transpose(0, 2, 1), outer_up_factor
+    filters = depthwise_filters.transpose(1, 2, 0, 3).reshape(49, 2, CHANS)
+    bias, gain, shift, scale = (
+        depthwise_bias_vector, layernorm_gain, layernorm_shift, branch_channel_scale
     )
     row, col = lax.axis_index("row"), lax.axis_index("col")
     flags = jnp.stack(
         [row > 0, row < lax.axis_size("row") - 1, col > 0, col < lax.axis_size("col") - 1]
     ).astype(f32)
 
-    def by_block(*shape):
-        return pl.BlockSpec((None,) + shape, lambda t: (t, 0, 0))
-
+    west, east = call(
+        edge_kernel,
+        "edges",
+        1,
+        [(x0, pl.BlockSpec((ROWS, 8, CHANS), lambda t, k=k: (0, k, 0))) for k in (0, 3)],
+        [((3, ROWS, CHANS), bf16, fixed(3, ROWS, CHANS))] * 2,
+        [pltpu.VMEM((ROWS * 8, 128), f32)],
+        limit=6,
+    )
     north, south = swap((x0[:3], x0[-3:]), "row")
-    win, wout = call(
+    part = HIDDEN // 4
+    wide = (None, CHANS, part), lambda l, c: (l, 0, c)
+    tall = (None, part, CHANS), lambda l, c: (l, c, 0)
+    flat = (None, RANK, part), lambda l, c: (l, 0, c)
+    full = (None, RANK, CHANS), lambda l, c: (l, 0, 0)
+    win, wout, taps = call(
         fold_kernel,
         "fold",
-        2,
+        (2, 4),
         [
-            (inner_frozen_weight, by_block(CHANS, HIDDEN)),
-            (ain, by_block(CHANS, RANK)),
-            (bin_, by_block(RANK, HIDDEN)),
-            (outer_frozen_weight, by_block(HIDDEN, CHANS)),
-            (aout, by_block(HIDDEN, RANK)),
-            (bout, by_block(RANK, CHANS)),
+            (inner_frozen_weight, pl.BlockSpec(*wide)),
+            (ain, pl.BlockSpec(*full)),
+            (bin_, pl.BlockSpec(*flat)),
+            (outer_frozen_weight, pl.BlockSpec(*tall)),
+            (aout, pl.BlockSpec(*flat)),
+            (bout, pl.BlockSpec(*full)),
+            (filters, fixed(49, 2, CHANS)),
         ],
         [
-            ((2, CHANS, HIDDEN), bf16, by_block(CHANS, HIDDEN)),
-            ((2, HIDDEN, CHANS), bf16, by_block(HIDDEN, CHANS)),
+            ((2, CHANS, HIDDEN), bf16, pl.BlockSpec(*wide)),
+            ((2, HIDDEN, CHANS), bf16, pl.BlockSpec(*tall)),
+            ((2, 49, 8, 128), f32, fixed(2, 49, 8, 128)),
         ],
         [],
-    )
-    ends = [x0[:, :3].transpose(1, 0, 2), x0[:, -3:].transpose(1, 0, 2)]
-    west, east = strips(
-        [jnp.concatenate([v[:, :8], v[:, 24:]], axis=1) for v in ends],
-        [v[:, 8:24] for v in ends],
-        north,
-        south,
-    )
-    cv = conv([x0], [[(0, 0, 32)]], north, south, taps, bias, 0, False, flags)
-
-    pixels = tiled
+        limit=12,
+    )
+    west, east, win, wout = lax.optimization_barrier((west, east, win, wout))
+    west, east = strips([west, east], north, south)
+    cv = conv([x0], [[(0, 0, 32)]], north, south, taps, 0, False, flags)
+
     strip_spec = fixed(3, STRIP, CHANS)
 
     def common(l, place, x, x_place):
@@ -459,11 +521,14 @@
             (west, strip_spec),
             (east, strip_spec),
             (taps, layer(l, 49, 8, 128)),
-            (gain, layer(l, 1, CHANS)),
-            (shift, layer(l, 1, CHANS)),
+            (bias, fixed(2, CHANS)),
+            (gain, fixed(2, CHANS)),
+            (shift, fixed(2, CHANS)),
+            (scale, fixed(2, CHANS)),
             (win, layer(l, CHANS, HIDDEN)),
             (wout, layer(l, HIDDEN, CHANS)),
-            (ain, layer(l, CHANS, RANK)),
+            (ain, layer(l, RANK, CHANS)),
+            (aout, layer(l, RANK, HIDDEN)),
         ]
 
     def outer_place(t):
@@ -485,17 +550,16 @@
             for width in (CHANS, HIDDEN, HIDDEN, RANK, RANK)
         ]
 
-    last = [(aout, layer(0, HIDDEN, RANK)), (scale, layer(0, 1, CHANS))]
     *saved, outer, top, bottom, west_a, east_a = call(
         functools.partial(first_kernel, False),
         "first_outer",
         2,
-        common(0, outer_place, x0, outer_place) + last,
+        common(0, outer_place, x0, outer_place),
         kept(outer_place) + [half] + row_edges + col_edges,
         [HE, LINE, EDGE],
     )
     north, south = swap((top, bottom), "row")
-    ins = common(0, inner_place, x0, inner_place) + last
+    ins = common(0, inner_place, x0, inner_place)
     *saved, inner, west_b, east_b = call(
         functools.partial(first_kernel, True),
         "first_inner",
@@ -506,15 +570,13 @@
         {len(ins) + i: i for i in range(5)},
     )
     split = [[(0, 0, 8), (8, 24, 8)], [(0, 8, 16)]]
-    west, east = strips([west_a, east_a], [west_b, east_b], north, south)
-    cv = conv([outer, inner], split, north, south, taps, bias, 1, False, flags)
+    west, east = strips([west_a, west_b, east_a, east_b], north, south)
+    cv = conv([outer, inner], split, north, south, taps, 1, False, flags)
 
     def second(place):
         return [
             (bin_, layer(1, RANK, HIDDEN)),
-            (aout, layer(1, HIDDEN, RANK)),
             (bout, layer(1, RANK, CHANS)),
-            (scale, layer(1, 1, CHANS)),
             (cot, tiled(place, TROWS, COLS, CHANS)),
         ]
 
@@ -552,8 +614,8 @@
         work,
         {len(ins): 0},
     )
-    west, east = strips([west_a, east_a], [west_b, east_b], north, south)
-    cv = conv([outer_g, inner_g], split, north, south, taps, bias, 1, True, flags)
+    west, east = strips([west_a, west_b, east_a, east_b], north, south)
+    cv = conv([outer_g, inner_g], split, north, south, taps, 1, True, flags)
     (grads0,) = call(
         third_kernel,
         "third",
@@ -565,14 +627,17 @@
             (west, strip_spec),
             (east, strip_spec),
             (taps, layer(1, 49, 8, 128)),
-            (scale, layer(0, 1, CHANS)),
+            (scale, fixed(2, CHANS)),
             (wout, layer(0, HIDDEN, CHANS)),
             (bin_, layer(0, RANK, HIDDEN)),
             (bout, layer(0, RANK, CHANS)),
         ]
-        + [(v, tiled(same, TILE, v.shape[1])) for v in saved],
+        + [(v, tiled(same, TILE, RANK)) for v in saved[3:]]
+        + [(v, pl.BlockSpec(memory_space=pltpu.HBM)) for v in saved[:3]],
         [((RANK, GRADS), f32, fixed(RANK, GRADS))],
-        [HE, LINE, pltpu.VMEM((TILE, CHANS), bf16)],
+        [HE, LINE, pltpu.VMEM((TILE, CHANS), bf16)]
+        + [pltpu.VMEM((4, TILE, width), bf16) for width in (CHANS, HIDDEN, HIDDEN)]
+        + [pltpu.SemaphoreType.DMA((3, 4))],
     )
     sums = total(grads0, grads1)
     return (

time: 172 us -> 183 us (1.064)
  local copies, waits for them, and re-layouts: 23.3 us -> 33.8 us
  Pallas kernels: 73 us -> 77.5 us
  other arithmetic: 4.57 us -> 2.41 us
    unnamed x66 -> x74, local copies, waits for them, and re-layouts: 19.2 us -> 32.9 us
    pallas_call x9 -> x13, Pallas kernels: 73 us -> 77.5 us  [call(): pl.pallas_call(kernel, grid=grid if isinstance(grid, tuple) else (grid,),...]
    ppermute x12, waiting for transfers between devices: 3.76 us -> 0.03 us  [swap(): return (lax.ppermute(v[1], axis, after), lax.ppermute(v[0], axis, before))]
    ppermute x6, starting transfers between devices: 6.55 us -> 3.84 us  [total(): other = lax.ppermute(part, ('row', 'col', 'rep'), pairs)]
    ppermute x6, waiting for transfers between devices: 24 us -> 26.7 us  [total(): other = lax.ppermute(part, ('row', 'col', 'rep'), pairs)]
    ppermute x6 -> x0, local copies, waits for them, and re-layouts: 2.34 us -> none  [swap(): return (lax.ppermute(v[1], axis, after), lax.ppermute(v[0], axis, before))]
  transfers between devices with their start and end apart: 20 -> 20, of which waited for: 9 -> 8; matrix products, arithmetic and copies ran while one was open for 3% -> 0% of each run, Pallas kernels for 28% -> 28%
where the time goes in v3:
time: 183 us; the launch traced here: 182 us
  Pallas kernels  77.5 us (42%)
  starting transfers between devices  38.4 us (21%)
  local copies, waits for them, and re-layouts  33.8 us (18%)
  waiting for transfers between devices  28.8 us (16%)
  other arithmetic  2.41 us (1%)
    pallas_call x13, Pallas kernels, call(): pl.pallas_call(kernel, grid=grid if isinstance(grid, tuple) else (grid,),...  77.5 us
    unnamed x74, local copies, waits for them, and re-layouts  32.9 us
    ppermute x6, waiting for transfers between devices, total(): other = lax.ppermute(part, ('row', 'col', 'rep'), pairs)  26.7 us
    ppermute x12, starting transfers between devices, swap(): return (lax.ppermute(v[1], axis, after), lax.ppermute(v[0], axis, before))  22.4 us
    ppermute x1, starting transfers between devices, total(): back = lax.ppermute(part, 'col', pair)  6.75 us
    ppermute x1, starting transfers between devices, total(): part = (mine + lax.ppermute(other, 'col', pair).astype(f32)).astype(bf16)  5.43 us
    ppermute x6, starting transfers between devices, total(): other = lax.ppermute(part, ('row', 'col', 'rep'), pairs)  3.84 us
  transfers between devices with their start and end apart: 20, of which 8 were waited for; matrix products, arithmetic and copies ran while one was open for 0% of the time, Pallas kernels for 28%

profile of v3, /device:TPU:1, one launch (start us, length us, event | category | flops | bytes accessed | tf_op | source)
XLA Modules:
  0.0 182.0 jit_solution(9563947919617376561)
XLA Ops:
  1.6 3.6 %collective-permute-start.1 = (bf16[3,32,512]{2,1,0:T(8,128)(2,1)S(1)}, bf16[3,32,512]{2,1,0:T(8,128)(2,1)S(1)}, u32[]{:S(2)}, u32[]{:S(2)}) collective-permute-start(bf16[3,32,512]{2,1,0:T(8,128)(2,1)S(1)} %get-tuple-element.101), channel_id=1, source_target_pairs={{32,0},{64,32},{96,64},{0,96},{33,1},{65,33},{97,65},{1,97},{34,2}... | collective-permute-start | bytes 294920 | tf_op jit(solution)/shard_map/ppermute | solution.py:411
  6.6 2.2 %copy-done.14 = bf16[2,512,2048]{2,1,0:T(8,128)(2,1)S(1)} copy-done((bf16[2,512,2048]{2,1,0:T(8,128)(2,1)S(1)}, bf16[2,512,2048]{2,1,0:T(8,128)(2,1)}, u32[]{:S(2)}) %copy-start.14) | copy-done | bytes 4194328
  8.8 2.2 %copy-done.15 = bf16[2,2048,512]{2,1,0:T(8,128)(2,1)S(1)} copy-done((bf16[2,2048,512]{2,1,0:T(8,128)(2,1)S(1)}, bf16[2,2048,512]{2,1,0:T(8,128)(2,1)}, u32[]{:S(2)}) %copy-start.15) | copy-done | bytes 4194328
  15.3 4.7 %fold.1 = (bf16[2,512,2048]{2,1,0:T(8,128)(2,1)S(1)}, bf16[2,2048,512]{2,1,0:T(8,128)(2,1)S(1)}, f32[2,49,8,128]{3,2,1,0:T(8,128)S(1)}) custom-call(bf16[2,512,2048]{2,1,0:T(8,128)(2,1)S(1)} %copy-done.14, bf16[2,16,512]{2,1,0:T(8,128)(2,1)S(1)} %bitcast.37, bf16[2,16,2048]{2,1,0:T(8,128)(2,1)S(1)} %copy-done.18, bf16[2,2048,512]{2,1,0:T(8,128)(2,1)S(1)} %copy-done.15, ...), custom_call_target="tpu_custom_call" | custom-call | tf_op jit(solution)/shard_map/fold/pallas_call | solution.py:375
  24.0 2.6 %collective-permute-start.2 = (bf16[3,48,512]{2,1,0:T(8,128)(2,1)S(1)}, bf16[3,48,512]{2,1,0:T(8,128)(2,1)S(1)}, u32[]{:S(2)}, u32[]{:S(2)}) collective-permute-start(bf16[3,48,512]{2,1,0:T(8,128)(2,1)S(1)} %get-tuple-element.57), channel_id=1, source_target_pairs={{0,2},{2,4},{4,6},{6,8},{8,10},{10,12},{12,14},{14,16},{16,18},{18... | collective-permute-start | bytes 442376 | tf_op jit(solution)/shard_map/ppermute | solution.py:411
  26.6 10.1 %conv.3.cv = f32[4096,128]{1,0:T(8,128)S(1)} custom-call(f32[4]{0:T(128)S(1)} %add_convert_fusion.7.flags, bf16[32,32,512]{2,1,0:T(8,128)(2,1)S(1)} %bitcast.26, bf16[3,32,512]{2,1,0:T(8,128)(2,1)S(1)} %collective-permute-done.refs_1_.refs_2_, bf16[3,32,512]{2,1,0:T(8,128)(2,1)S(1)} %collective-permute-done.1.refs_2_.refs_3_, ...), custom_call_target="tpu_custom_call" | custom-call | tf_op jit(solution)/shard_map/conv/pallas_call | solution.py:375
  36.8 2.2 %copy-done.1 = bf16[2,2048,512]{2,1,0:T(8,128)(2,1)S(1)} copy-done((bf16[2,2048,512]{2,1,0:T(8,128)(2,1)S(1)}, bf16[2,2048,512]{2,1,0:T(8,128)(2,1)}, u32[]{:S(2)}) %copy-start.1) | copy-done | bytes 4194328
  39.0 2.2 %copy-done.5 = bf16[2,512,2048]{2,1,0:T(8,128)(2,1)S(1)} copy-done((bf16[2,512,2048]{2,1,0:T(8,128)(2,1)S(1)}, bf16[2,512,2048]{2,1,0:T(8,128)(2,1)}, u32[]{:S(2)}) %copy-start.5) | copy-done | bytes 4194328
  41.2 6.1 %first_outer.1 = (bf16[1024,512]{1,0:T(8,128)(2,1)S(1)}, bf16[1024,2048]{1,0:T(8,128)(2,1)S(1)}, bf16[1024,2048]{1,0:T(8,128)(2,1)S(1)}, bf16[1024,16]{1,0:T(8,1...) custom-call(f32[4]{0:T(128)S(1)} %add_convert_fusion.7.flags, ...), custom_call_target="tpu_custom_call" | custom-call | tf_op jit(solution)/shard_map/first_outer/pallas_call | solution.py:375
  47.6 2.7 %collective-permute-start.5 = (bf16[3,32,512]{2,1,0:T(8,128)(2,1)S(1)}, bf16[3,32,512]{2,1,0:T(8,128)(2,1)S(1)}, u32[]{:S(2)}, u32[]{:S(2)}) collective-permute-start(bf16[3,32,512]{2,1,0:T(8,128)(2,1)S(1)} %get-tuple-element.69), channel_id=1, source_target_pairs={{32,0},{64,32},{96,64},{0,96},{33,1},{65,33},{97,65},{1,97},{34,2}... | collective-permute-start | bytes 294920 | tf_op jit(solution)/shard_map/ppermute | solution.py:411
  50.4 6.0 %first_inner.1 = (bf16[1024,512]{1,0:T(8,128)(2,1)S(1)}, bf16[1024,2048]{1,0:T(8,128)(2,1)S(1)}, bf16[1024,2048]{1,0:T(8,128)(2,1)S(1)}, bf16[1024,16]{1,0:T(8,1...) custom-call(f32[4]{0:T(128)S(1)} %add_convert_fusion.7.flags, ...), custom_call_target="tpu_custom_call", output_to_operand_aliasing={{0}: (14, {}), {1}: (15, {}), {2}: (16, {}), {3}: (17, {}),... | custom-call | tf_op jit(solution)/shard_map/first_inner/pallas_call | solution.py:375
  58.5 2.1 %collective-permute-start.6 = (bf16[3,48,512]{2,1,0:T(8,128)(2,1)S(1)}, bf16[3,48,512]{2,1,0:T(8,128)(2,1)S(1)}, u32[]{:S(2)}, u32[]{:S(2)}) collective-permute-start(bf16[3,48,512]{2,1,0:T(8,128)(2,1)S(1)} %get-tuple-element.74), channel_id=1, source_target_pairs={{0,2},{2,4},{4,6},{6,8},{8,10},{10,12},{12,14},{14,16},{16,18},{18... | collective-permute-start | bytes 442376 | tf_op jit(solution)/shard_map/ppermute | solution.py:411
  60.5 2.7 %collective-permute-start.7 = (bf16[3,48,512]{2,1,0:T(8,128)(2,1)S(1)}, bf16[3,48,512]{2,1,0:T(8,128)(2,1)S(1)}, u32[]{:S(2)}, u32[]{:S(2)}) collective-permute-start(bf16[3,48,512]{2,1,0:T(8,128)(2,1)S(1)} %get-tuple-element.75), channel_id=1, source_target_pairs={{2,0},{4,2},{6,4},{8,6},{10,8},{12,10},{14,12},{16,14},{18,16},{20... | collective-permute-start | bytes 442376 | tf_op jit(solution)/shard_map/ppermute | solution.py:411
  63.2 9.9 %conv.4.cv = f32[4096,128]{1,0:T(8,128)S(1)} custom-call(f32[4]{0:T(128)S(1)} %add_convert_fusion.7.flags, bf16[16,32,512]{2,1,0:T(8,128)(2,1)S(1)} %get-tuple-element.67.refs_0_.x, bf16[16,32,512]{2,1,0:T(8,128)(2,1)S(1)} %get-tuple-element.66.refs_1_.x, bf16[3,32,512]{2,1,0:T(8,128)(2,1)S(1)} %collective-permute-done.4.refs_2_.refs_4_, ...), custom_call_target="tpu_custom_call" | custom-call | tf_op jit(solution)/shard_map/conv/pallas_call | solution.py:375
  73.1 10.4 %second_outer.1 = (bf16[32,32,512]{2,1,0:T(8,128)(2,1)}, f32[16,5120]{1,0:T(8,128)S(1)}, bf16[16,32,512]{2,1,0:T(8,128)(2,1)S(1)}, bf16[3,32,512]{2,1,0:T(8,128)...) custom-call(f32[4]{0:T(128)S(1)} %add_convert_fusion.7.flags, ...), custom_call_target="tpu_custom_call" | custom-call | tf_op jit(solution)/shard_map/second_outer/pallas_call | solution.py:375
  84.4 2.7 %collective-permute-start.9 = (bf16[3,32,512]{2,1,0:T(8,128)(2,1)S(1)}, bf16[3,32,512]{2,1,0:T(8,128)(2,1)S(1)}, u32[]{:S(2)}, u32[]{:S(2)}) collective-permute-start(bf16[3,32,512]{2,1,0:T(8,128)(2,1)S(1)} %get-tuple-element.82), channel_id=1, source_target_pairs={{32,0},{64,32},{96,64},{0,96},{33,1},{65,33},{97,65},{1,97},{34,2}... | collective-permute-start | bytes 294920 | tf_op jit(solution)/shard_map/ppermute | solution.py:411
  87.0 10.2 %second_inner.1 = (bf16[32,32,512]{2,1,0:T(8,128)(2,1)}, f32[16,5120]{1,0:T(8,128)S(1)}, bf16[16,32,512]{2,1,0:T(8,128)(2,1)S(1)}, bf16[3,16,512]{2,1,0:T(8,128)(2,1)S(1)}, bf16[3,16,512]{2,1,0:T(8,128)(2,1)S(1)}) custom-call(f32[4]{0:T(128)S(1)} %add_convert_fusion.7.flags, ...), custom_call_target="tpu_custom_call", output_to_operand_aliasing={{0}: (17, {})} | custom-call | tf_op jit(solution)/shard_map/second_inner/pallas_call | solution.py:375
  99.4 5.7 %collective-permute-start.11 = (bf16[3,48,512]{2,1,0:T(8,128)(2,1)}, bf16[3,48,512]{2,1,0:T(8,128)(2,1)}, u32[]{:S(2)}, u32[]{:S(2)}) collective-permute-start(bf16[3,48,512]{2,1,0:T(8,128)(2,1)} %get-tuple-element.88), channel_id=1, source_target_pairs={{2,0},{4,2},{6,4},{8,6},{10,8},{12,10},{14,12},{16,14},{18,16},{20... | collective-permute-start | bytes 442376 | tf_op jit(solution)/shard_map/ppermute | solution.py:411
  108.1 9.9 %conv.5.cv = f32[4096,128]{1,0:T(8,128)S(1)} custom-call(f32[4]{0:T(128)S(1)} %add_convert_fusion.7.flags, bf16[16,32,512]{2,1,0:T(8,128)(2,1)S(1)} %copy-done.27, bf16[16,32,512]{2,1,0:T(8,128)(2,1)S(1)} %copy-done.29, bf16[3,32,512]{2,1,0:T(8,128)(2,1)S(1)} %collective-permute-done.8.refs_2_.refs_4_, bf16[3,32,512]{2,1,0:T(8,128)(2,1)S(1)} %copy-done.31, ...), custom_call_target="tpu_custom_call" | custom-call | tf_op jit(solution)/shard_map/conv/pallas_call | solution.py:375
  118.1 2.2 %copy-done.3 = bf16[2,2048,512]{2,1,0:T(8,128)(2,1)S(1)} copy-done((bf16[2,2048,512]{2,1,0:T(8,128)(2,1)S(1)}, bf16[2,2048,512]{2,1,0:T(8,128)(2,1)}, u32[]{:S(2)}) %copy-start.3) | copy-done | bytes 4194328
  120.3 2.2 %copy-done.10 = bf16[1024,2048]{1,0:T(8,128)(2,1)S(1)} copy-done((bf16[1024,2048]{1,0:T(8,128)(2,1)S(1)}, bf16[1024,2048]{1,0:T(8,128)(2,1)}, u32[]{:S(2)}) %copy-start.10) | copy-done | bytes 4194328
  122.4 2.2 %copy-done.12 = bf16[1024,2048]{1,0:T(8,128)(2,1)S(1)} copy-done((bf16[1024,2048]{1,0:T(8,128)(2,1)S(1)}, bf16[1024,2048]{1,0:T(8,128)(2,1)}, u32[]{:S(2)}) %copy-start.12) | copy-done | bytes 4194328
  125.6 9.2 %third.1 = f32[16,5120]{1,0:T(8,128)S(1)} custom-call(f32[4]{0:T(128)S(1)} %add_convert_fusion.7.flags, bf16[32,32,512]{2,1,0:T(8,128)(2,1)S(1)} %bitcast.31, f32[4096,128]{1,0:T(8,128)S(1)} %conv.5.cv, bf16[3,48,512]{2,1,0:T(8,128)(2,1)} %collective-permute-done.10.w, bf16[3,48,512]{2,1,0:T(8,128)(2,1)} %collective-permute-done.11.e, ...), custom_call_target="tpu_custom_call" | custom-call | tf_op jit(solution)/shard_map/third/pallas_call | solution.py:375
  134.8 5.4 %collective-permute-start.12 = (bf16[16,5120]{1,0:T(8,128)(2,1)S(1)}, bf16[16,5120]{1,0:T(8,128)(2,1)S(1)}, u32[]{:S(2)}, u32[]{:S(2)}) collective-permute-start(bf16[16,5120]{1,0:T(8,128)(2,1)S(1)} %select_convert_fusion), channel_id=1, source_target_pairs={{0,2},{2,0},{4,6},{6,4},{8,10},{10,8},{12,14},{14,12},{16,18},{18,... | collective-permute-start | bytes 491528 | tf_op jit(solution)/shard_map/ppermute | solution.py:432
  141.4 4.5 %collective-permute-done.13 = bf16[16,5120]{1,0:T(8,128)(2,1)S(1)} collective-permute-done((bf16[16,5120]{1,0:T(8,128)(2,1)S(1)}, bf16[16,5120]{1,0:T(8,128)(2,1)S(1)}, u32[]{:S(2)}, u32[]{:S(2)}) %collective-permute-start.13) | collective-permute-done | bytes 163872 | tf_op jit(solution)/shard_map/ppermute | solution.py:435
  146.0 6.0 %collective-permute-done.14 = bf16[16,5120]{1,0:T(8,128)(2,1)S(1)} collective-permute-done((bf16[16,5120]{1,0:T(8,128)(2,1)S(1)}, bf16[16,5120]{1,0:T(8,128)(2,1)S(1)}, u32[]{:S(2)}, u32[]{:S(2)}) %collective-permute-start.14) | collective-permute-done | bytes 163872 | tf_op jit(solution)/shard_map/ppermute | solution.py:435
  153.0 3.3 %collective-permute-done.15 = bf16[16,5120]{1,0:T(8,128)(2,1)S(1)} collective-permute-done((bf16[16,5120]{1,0:T(8,128)(2,1)S(1)}, bf16[16,5120]{1,0:T(8,128)(2,1)S(1)}, u32[]{:S(2)}, u32[]{:S(2)}) %collective-permute-start.15) | collective-permute-done | bytes 163872 | tf_op jit(solution)/shard_map/ppermute | solution.py:435
  156.3 2.5 %collective-permute-start.16 = (bf16[16,5120]{1,0:T(8,128)(2,1)S(1)}, bf16[16,5120]{1,0:T(8,128)(2,1)S(1)}, u32[]{:S(2)}, u32[]{:S(2)}) collective-permute-start(bf16[16,5120]{1,0:T(8,128)(2,1)S(1)} %add_convert_fusion.3), channel_id=1, source_target_pairs={{0,8},{1,9},{2,18},{3,19},{4,12},{5,13},{6,22},{7,23},{8,0},{9,1},... | collective-permute-start | bytes 491528 | tf_op jit(solution)/shard_map/ppermute | solution.py:435
  158.8 3.2 %collective-permute-done.16 = bf16[16,5120]{1,0:T(8,128)(2,1)S(1)} collective-permute-done((bf16[16,5120]{1,0:T(8,128)(2,1)S(1)}, bf16[16,5120]{1,0:T(8,128)(2,1)S(1)}, u32[]{:S(2)}, u32[]{:S(2)}) %collective-permute-start.16) | collective-permute-done | bytes 163872 | tf_op jit(solution)/shard_map/ppermute | solution.py:435
  162.2 4.2 %collective-permute-done.17 = bf16[16,5120]{1,0:T(8,128)(2,1)S(1)} collective-permute-done((bf16[16,5120]{1,0:T(8,128)(2,1)S(1)}, bf16[16,5120]{1,0:T(8,128)(2,1)S(1)}, u32[]{:S(2)}, u32[]{:S(2)}) %collective-permute-start.17) | collective-permute-done | bytes 163872 | tf_op jit(solution)/shard_map/ppermute | solution.py:435
  166.5 5.7 %collective-permute-done.18 = bf16[16,5120]{1,0:T(8,128)(2,1)S(1)} collective-permute-done((bf16[16,5120]{1,0:T(8,128)(2,1)S(1)}, bf16[16,5120]{1,0:T(8,128)(2,1)S(1)}, u32[]{:S(2)}, u32[]{:S(2)}) %collective-permute-start.18) | collective-permute-done | bytes 163872 | tf_op jit(solution)/shard_map/ppermute | solution.py:435
  172.2 6.8 %collective-permute-start.19 = (bf16[16,5120]{1,0:T(8,128)(2,1)S(1)}, bf16[16,5120]{1,0:T(8,128)(2,1)S(1)}, u32[]{:S(2)}, u32[]{:S(2)}) collective-permute-start(bf16[16,5120]{1,0:T(8,128)(2,1)S(1)} %add_convert_fusion), channel_id=1, source_target_pairs={{0,2},{2,0},{4,6},{6,4},{8,10},{10,8},{12,14},{14,12},{16,18},{18,... | collective-permute-start | bytes 491528 | tf_op jit(solution)/shard_map/ppermute | solution.py:437
  (114 shorter events, 25.8 us)
Async XLA Ops:
  1.6 22.3 %collective-permute-start.1 = (bf16[3,32,512]{2,1,0:T(8,128)(2,1)S(1)}, bf16[3,32,512]{2,1,0:T(8,128)(2,1)S(1)}, u32[]{:S(2)}, u32[]{:S(2)}) collective-permute-start(bf16[3,32,512]{2,1,0:T(8,128)(2,1)S(1)} %get-tuple-element.101), channel_id=1, source_target_pairs={{32,0},{64,32},{96,64},{0,96},{33,1},{65,33},{97,65},{1,97},{34,2}... | collective-permute-start | bytes 294920 | tf_op jit(solution)/shard_map/ppermute | solution.py:411
  5.2 18.7 %collective-permute-start = (bf16[3,32,512]{2,1,0:T(8,128)(2,1)S(1)}, bf16[3,32,512]{2,1,0:T(8,128)(2,1)S(1)}, u32[]{:S(2)}, u32[]{:S(2)}) collective-permute-start(bf16[3,32,512]{2,1,0:T(8,128)(2,1)S(1)} %get-tuple-element.102), channel_id=1, source_target_pairs={{0,32},{32,64},{64,96},{96,0},{1,33},{33,65},{65,97},{97,1},{2,34}... | collective-permute-start | bytes 294920 | tf_op jit(solution)/shard_map/ppermute | solution.py:411
  15.3 21.5 %copy-start.33 = (f32[2,512]{1,0:T(2,128)S(1)}, f32[2,512]{1,0:T(2,128)}, u32[]{:S(2)}) copy-start(f32[2,512]{1,0:T(2,128)} %scale.9) | copy-start | bytes 12292
  15.3 21.5 %copy-start.34 = (f32[2,512]{1,0:T(2,128)S(1)}, f32[2,512]{1,0:T(2,128)}, u32[]{:S(2)}) copy-start(f32[2,512]{1,0:T(2,128)} %bias.7) | copy-start | bytes 12292
  15.3 21.5 %copy-start.35 = (f32[2,512]{1,0:T(2,128)S(1)}, f32[2,512]{1,0:T(2,128)}, u32[]{:S(2)}) copy-start(f32[2,512]{1,0:T(2,128)} %gain.7) | copy-start | bytes 12292
  15.3 21.5 %copy-start.36 = (f32[2,512]{1,0:T(2,128)S(1)}, f32[2,512]{1,0:T(2,128)}, u32[]{:S(2)}) copy-start(f32[2,512]{1,0:T(2,128)} %shift.7) | copy-start | bytes 12292
  23.9 12.9 %copy-start.23 = (bf16[2,512,16]{1,2,0:T(8,128)(2,1)S(1)}, bf16[2,512,16]{1,2,0:T(8,128)(2,1)}, u32[]{:S(2)}) copy-start(bf16[2,512,16]{1,2,0:T(8,128)(2,1)} %param.21) | copy-start | bytes 98308
  24.0 12.7 %collective-permute-start.2 = (bf16[3,48,512]{2,1,0:T(8,128)(2,1)S(1)}, bf16[3,48,512]{2,1,0:T(8,128)(2,1)S(1)}, u32[]{:S(2)}, u32[]{:S(2)}) collective-permute-start(bf16[3,48,512]{2,1,0:T(8,128)(2,1)S(1)} %get-tuple-element.57), channel_id=1, source_target_pairs={{0,2},{2,4},{4,6},{6,8},{8,10},{10,12},{12,14},{14,16},{16,18},{18... | collective-permute-start | bytes 442376 | tf_op jit(solution)/shard_map/ppermute | solution.py:411
  26.5 10.2 %collective-permute-start.3 = (bf16[3,48,512]{2,1,0:T(8,128)(2,1)S(1)}, bf16[3,48,512]{2,1,0:T(8,128)(2,1)S(1)}, u32[]{:S(2)}, u32[]{:S(2)}) collective-permute-start(bf16[3,48,512]{2,1,0:T(8,128)(2,1)S(1)} %get-tuple-element.58), channel_id=1, source_target_pairs={{2,0},{4,2},{6,4},{8,6},{10,8},{12,10},{14,12},{16,14},{18,16},{20... | collective-permute-start | bytes 442376 | tf_op jit(solution)/shard_map/ppermute | solution.py:411
  47.3 11.1 %collective-permute-start.4 = (bf16[3,32,512]{2,1,0:T(8,128)(2,1)S(1)}, bf16[3,32,512]{2,1,0:T(8,128)(2,1)S(1)}, u32[]{:S(2)}, u32[]{:S(2)}) collective-permute-start(bf16[3,32,512]{2,1,0:T(8,128)(2,1)S(1)} %get-tuple-element.68), channel_id=1, source_target_pairs={{0,32},{32,64},{64,96},{96,0},{1,33},{33,65},{65,97},{97,1},{2,34}... | collective-permute-start | bytes 294920 | tf_op jit(solution)/shard_map/ppermute | solution.py:411
  47.6 10.8 %collective-permute-start.5 = (bf16[3,32,512]{2,1,0:T(8,128)(2,1)S(1)}, bf16[3,32,512]{2,1,0:T(8,128)(2,1)S(1)}, u32[]{:S(2)}, u32[]{:S(2)}) collective-permute-start(bf16[3,32,512]{2,1,0:T(8,128)(2,1)S(1)} %get-tuple-element.69), channel_id=1, source_target_pairs={{32,0},{64,32},{96,64},{0,96},{33,1},{65,33},{97,65},{1,97},{34,2}... | collective-permute-start | bytes 294920 | tf_op jit(solution)/shard_map/ppermute | solution.py:411
  50.4 22.7 %copy-start.2 = (bf16[2,2048,512]{2,1,0:T(8,128)(2,1)S(1)}, bf16[2,2048,512]{2,1,0:T(8,128)(2,1)}, u32[]{:S(2)}) copy-start(bf16[2,2048,512]{2,1,0:T(8,128)(2,1)} %copy-done) | copy-start | bytes 12582916
  50.4 22.7 %copy-start.6 = (bf16[2,512,2048]{2,1,0:T(8,128)(2,1)S(1)}, bf16[2,512,2048]{2,1,0:T(8,128)(2,1)}, u32[]{:S(2)}) copy-start(bf16[2,512,2048]{2,1,0:T(8,128)(2,1)} %copy-done.4) | copy-start | bytes 12582916
  50.4 22.7 %copy-start.25 = (bf16[2,16,512]{2,1,0:T(8,128)(2,1)S(1)}, bf16[2,16,512]{2,1,0:T(8,128)(2,1)}, u32[]{:S(2)}) copy-start(bf16[2,16,512]{2,1,0:T(8,128)(2,1)} %bout.7) | copy-start | bytes 98308
  58.4 25.2 %copy-start.11 = (bf16[1024,2048]{1,0:T(8,128)(2,1)}, bf16[1024,2048]{1,0:T(8,128)(2,1)S(1)}, u32[]{:S(2)}) copy-start(bf16[1024,2048]{1,0:T(8,128)(2,1)S(1)} %get-tuple-element.93.slope_far) | copy-start | bytes 12582916
  58.4 25.2 %copy-start.20 = (bf16[1024,16]{1,0:T(8,128)(2,1)}, bf16[1024,16]{1,0:T(8,128)(2,1)S(1)}, u32[]{:S(2)}) copy-start(bf16[1024,16]{1,0:T(8,128)(2,1)S(1)} %get-tuple-element.90.mid_out) | copy-start | bytes 98308
  58.4 14.8 %copy-start.13 = (bf16[1,32,32,512]{3,2,1,0:T(8,128)(2,1)S(1)}, bf16[1,32,32,512]{3,2,1,0:T(8,128)(2,1)}, u32[]{:S(2)}) copy-start(bf16[1,32,32,512]{3,2,1,0:T(8,128)(2,1)} %param.14) | copy-start | bytes 3145732
  58.4 14.8 %copy-start.19 = (bf16[2,16,2048]{2,1,0:T(8,128)(2,1)S(1)}, bf16[2,16,2048]{2,1,0:T(8,128)(2,1)}, u32[]{:S(2)}) copy-start(bf16[2,16,2048]{2,1,0:T(8,128)(2,1)} %bin_.7) | copy-start | bytes 393220
  58.5 14.6 %collective-permute-start.6 = (bf16[3,48,512]{2,1,0:T(8,128)(2,1)S(1)}, bf16[3,48,512]{2,1,0:T(8,128)(2,1)S(1)}, u32[]{:S(2)}, u32[]{:S(2)}) collective-permute-start(bf16[3,48,512]{2,1,0:T(8,128)(2,1)S(1)} %get-tuple-element.74), channel_id=1, source_target_pairs={{0,2},{2,4},{4,6},{6,8},{8,10},{10,12},{12,14},{14,16},{16,18},{18... | collective-permute-start | bytes 442376 | tf_op jit(solution)/shard_map/ppermute | solution.py:411
  60.5 12.5 %collective-permute-start.7 = (bf16[3,48,512]{2,1,0:T(8,128)(2,1)S(1)}, bf16[3,48,512]{2,1,0:T(8,128)(2,1)S(1)}, u32[]{:S(2)}, u32[]{:S(2)}) collective-permute-start(bf16[3,48,512]{2,1,0:T(8,128)(2,1)S(1)} %get-tuple-element.75), channel_id=1, source_target_pairs={{2,0},{4,2},{6,4},{8,6},{10,8},{12,10},{14,12},{16,14},{18,16},{20... | collective-permute-start | bytes 442376 | tf_op jit(solution)/shard_map/ppermute | solution.py:411
  84.4 13.7 %collective-permute-start.8 = (bf16[3,32,512]{2,1,0:T(8,128)(2,1)S(1)}, bf16[3,32,512]{2,1,0:T(8,128)(2,1)S(1)}, u32[]{:S(2)}, u32[]{:S(2)}) collective-permute-start(bf16[3,32,512]{2,1,0:T(8,128)(2,1)S(1)} %get-tuple-element.81), channel_id=1, source_target_pairs={{0,32},{32,64},{64,96},{96,0},{1,33},{33,65},{65,97},{97,1},{2,34}... | collective-permute-start | bytes 294920 | tf_op jit(solution)/shard_map/ppermute | solution.py:411
  84.4 13.7 %collective-permute-start.9 = (bf16[3,32,512]{2,1,0:T(8,128)(2,1)S(1)}, bf16[3,32,512]{2,1,0:T(8,128)(2,1)S(1)}, u32[]{:S(2)}, u32[]{:S(2)}) collective-permute-start(bf16[3,32,512]{2,1,0:T(8,128)(2,1)S(1)} %get-tuple-element.82), channel_id=1, source_target_pairs={{32,0},{64,32},{96,64},{0,96},{33,1},{65,33},{97,65},{1,97},{34,2}... | collective-permute-start | bytes 294920 | tf_op jit(solution)/shard_map/ppermute | solution.py:411
  99.4 18.6 %collective-permute-start.10 = (bf16[3,48,512]{2,1,0:T(8,128)(2,1)}, bf16[3,48,512]{2,1,0:T(8,128)(2,1)}, u32[]{:S(2)}, u32[]{:S(2)}) collective-permute-start(bf16[3,48,512]{2,1,0:T(8,128)(2,1)} %get-tuple-element.87), channel_id=1, source_target_pairs={{0,2},{2,4},{4,6},{6,8},{8,10},{10,12},{12,14},{14,16},{16,18},{18... | collective-permute-start | bytes 442376 | tf_op jit(solution)/shard_map/ppermute | solution.py:411
  99.4 18.6 %collective-permute-start.11 = (bf16[3,48,512]{2,1,0:T(8,128)(2,1)}, bf16[3,48,512]{2,1,0:T(8,128)(2,1)}, u32[]{:S(2)}, u32[]{:S(2)}) collective-permute-start(bf16[3,48,512]{2,1,0:T(8,128)(2,1)} %get-tuple-element.88), channel_id=1, source_target_pairs={{2,0},{4,2},{6,4},{8,6},{10,8},{12,10},{14,12},{16,14},{18,16},{20... | collective-permute-start | bytes 442376 | tf_op jit(solution)/shard_map/ppermute | solution.py:411
  134.8 6.5 %collective-permute-start.12 = (bf16[16,5120]{1,0:T(8,128)(2,1)S(1)}, bf16[16,5120]{1,0:T(8,128)(2,1)S(1)}, u32[]{:S(2)}, u32[]{:S(2)}) collective-permute-start(bf16[16,5120]{1,0:T(8,128)(2,1)S(1)} %select_convert_fusion), channel_id=1, source_target_pairs={{0,2},{2,0},{4,6},{6,4},{8,10},{10,8},{12,14},{14,12},{16,18},{18,... | collective-permute-start | bytes 491528 | tf_op jit(solution)/shard_map/ppermute | solution.py:432
  141.4 4.5 %collective-permute-start.13 = (bf16[16,5120]{1,0:T(8,128)(2,1)S(1)}, bf16[16,5120]{1,0:T(8,128)(2,1)S(1)}, u32[]{:S(2)}, u32[]{:S(2)}) collective-permute-start(bf16[16,5120]{1,0:T(8,128)(2,1)S(1)} %add_convert_fusion.6), channel_id=1, source_target_pairs={{0,32},{1,33},{2,6},{3,7},{4,36},{5,37},{6,2},{7,3},{8,40},{9,41},... | collective-permute-start | bytes 491528 | tf_op jit(solution)/shard_map/ppermute | solution.py:435
  145.9 6.0 %collective-permute-start.14 = (bf16[16,5120]{1,0:T(8,128)(2,1)S(1)}, bf16[16,5120]{1,0:T(8,128)(2,1)S(1)}, u32[]{:S(2)}, u32[]{:S(2)}) collective-permute-start(bf16[16,5120]{1,0:T(8,128)(2,1)S(1)} %add_convert_fusion.5), channel_id=1, source_target_pairs={{0,64},{1,65},{2,10},{3,11},{4,68},{5,69},{6,14},{7,15},{8,72},{9,... | collective-permute-start | bytes 491528 | tf_op jit(solution)/shard_map/ppermute | solution.py:435
  152.0 4.2 %collective-permute-start.15 = (bf16[16,5120]{1,0:T(8,128)(2,1)S(1)}, bf16[16,5120]{1,0:T(8,128)(2,1)S(1)}, u32[]{:S(2)}, u32[]{:S(2)}) collective-permute-start(bf16[16,5120]{1,0:T(8,128)(2,1)S(1)} %add_convert_fusion.4), channel_id=1, source_target_pairs={{0,4},{1,5},{2,3},{3,2},{4,0},{5,1},{6,7},{7,6},{8,12},{9,13},{10,... | collective-permute-start | bytes 491528 | tf_op jit(solution)/shard_map/ppermute | solution.py:435
  156.3 5.8 %collective-permute-start.16 = (bf16[16,5120]{1,0:T(8,128)(2,1)S(1)}, bf16[16,5120]{1,0:T(8,128)(2,1)S(1)}, u32[]{:S(2)}, u32[]{:S(2)}) collective-permute-start(bf16[16,5120]{1,0:T(8,128)(2,1)S(1)} %add_convert_fusion.3), channel_id=1, source_target_pairs={{0,8},{1,9},{2,18},{3,19},{4,12},{5,13},{6,22},{7,23},{8,0},{9,1},... | collective-permute-start | bytes 491528 | tf_op jit(solution)/shard_map/ppermute | solution.py:435
  162.1 4.2 %collective-permute-start.17 = (bf16[16,5120]{1,0:T(8,128)(2,1)S(1)}, bf16[16,5120]{1,0:T(8,128)(2,1)S(1)}, u32[]{:S(2)}, u32[]{:S(2)}) collective-permute-start(bf16[16,5120]{1,0:T(8,128)(2,1)S(1)} %add_convert_fusion.2), channel_id=1, source_target_pairs={{0,1},{1,0},{2,34},{3,35},{4,5},{5,4},{6,38},{7,39},{8,9},{9,8},{1... | collective-permute-start | bytes 491528 | tf_op jit(solution)/shard_map/ppermute | solution.py:435
  166.4 5.8 %collective-permute-start.18 = (bf16[16,5120]{1,0:T(8,128)(2,1)S(1)}, bf16[16,5120]{1,0:T(8,128)(2,1)S(1)}, u32[]{:S(2)}, u32[]{:S(2)}) collective-permute-start(bf16[16,5120]{1,0:T(8,128)(2,1)S(1)} %add_convert_fusion.1), channel_id=1, source_target_pairs={{0,16},{1,17},{2,66},{3,67},{4,20},{5,21},{6,70},{7,71},{8,24},{9,... | collective-permute-start | bytes 491528 | tf_op jit(solution)/shard_map/ppermute | solution.py:435
  172.2 7.8 %collective-permute-start.19 = (bf16[16,5120]{1,0:T(8,128)(2,1)S(1)}, bf16[16,5120]{1,0:T(8,128)(2,1)S(1)}, u32[]{:S(2)}, u32[]{:S(2)}) collective-permute-start(bf16[16,5120]{1,0:T(8,128)(2,1)S(1)} %add_convert_fusion), channel_id=1, source_target_pairs={{0,2},{2,0},{4,6},{6,4},{8,10},{10,8},{12,14},{14,12},{16,18},{18,... | collective-permute-start | bytes 491528 | tf_op jit(solution)/shard_map/ppermute | solution.py:437
  (25 other events, 57.1 us)

commit v4 on v3

--- a/solution.py
+++ b/solution.py
@@ -371,11 +371,14 @@
     return pl.BlockSpec(shape, lambda t: (place(t),) + (0,) * (len(shape) - 1))
 
 
-def call(kernel, name, grid, ins, outs, scratch, aliases={}, limit=26):
+def call(kernel, name, grid, ins, outs, scratch, aliases={}, limit=26, far=()):
     return pl.pallas_call(
         kernel,
         grid=grid if isinstance(grid, tuple) else (grid,),
-        out_shape=[jax.ShapeDtypeStruct(shape, dtype) for shape, dtype, _ in outs],
+        out_shape=[
+            pltpu.HBM(shape, dtype) if k in far else jax.ShapeDtypeStruct(shape, dtype)
+            for k, (shape, dtype, _) in enumerate(outs)
+        ],
         in_specs=[spec for _, spec in ins],
         out_specs=[spec for _, _, spec in outs],
         scratch_shapes=scratch,
@@ -557,6 +560,7 @@
         common(0, outer_place, x0, outer_place),
         kept(outer_place) + [half] + row_edges + col_edges,
         [HE, LINE, EDGE],
+        far=(0, 1, 2),
     )
     north, south = swap((top, bottom), "row")
     ins = common(0, inner_place, x0, inner_place)
@@ -568,6 +572,7 @@
         kept(inner_place) + [half] + col_edges,
         [HE, LINE, EDGE],
         {len(ins) + i: i for i in range(5)},
+        far=(0, 1, 2),
     )
     split = [[(0, 0, 8), (8, 24, 8)], [(0, 8, 16)]]
     west, east = strips([west_a, west_b, east_a, east_b], north, south)

time: 183 us -> 183 us (level)
  Pallas kernels: 77.5 us -> 80.3 us
  local copies, waits for them, and re-layouts: 33.8 us -> 31.1 us
    pallas_call x13, Pallas kernels: 77.5 us -> 80.3 us  [call(): pl.pallas_call(kernel, grid=grid if isinstance(grid, tuple) else (grid,),...]
    unnamed x74 -> x72, local copies, waits for them, and re-layouts: 32.9 us -> 30.1 us
  transfers between devices with their start and end apart: 20 -> 20, of which waited for: 8 -> 8; matrix products, arithmetic and copies ran while one was open for 0% -> 0% of each run, Pallas kernels for 28% -> 29%
where the time goes in v4:
time: 183 us; the launch traced here: 182 us
  Pallas kernels  80.3 us (44%)
  starting transfers between devices  38.2 us (21%)
  local copies, waits for them, and re-layouts  31.1 us (17%)
  waiting for transfers between devices  29 us (16%)
  other arithmetic  2.41 us (1%)
    pallas_call x13, Pallas kernels, call(): pl.pallas_call(kernel, grid=grid if isinstance(grid, tuple) else (grid,),...  80.3 us
    unnamed x72, local copies, waits for them, and re-layouts  30.1 us
    ppermute x6, waiting for transfers between devices, total(): other = lax.ppermute(part, ('row', 'col', 'rep'), pairs)  26.9 us
    ppermute x12, starting transfers between devices, swap(): return (lax.ppermute(v[1], axis, after), lax.ppermute(v[0], axis, before))  22.3 us
    ppermute x1, starting transfers between devices, total(): back = lax.ppermute(part, 'col', pair)  6.75 us
    ppermute x1, starting transfers between devices, total(): part = (mine + lax.ppermute(other, 'col', pair).astype(f32)).astype(bf16)  5.43 us
    ppermute x6, starting transfers between devices, total(): other = lax.ppermute(part, ('row', 'col', 'rep'), pairs)  3.69 us
  transfers between devices with their start and end apart: 20, of which 8 were waited for; matrix products, arithmetic and copies ran while one was open for 0% of the time, Pallas kernels for 29%

profile of v4, /device:TPU:1, one launch (start us, length us, event | category | flops | bytes accessed | tf_op | source)
XLA Modules:
  0.0 181.9 jit_solution(5861336896533042548)
XLA Ops:
  1.6 3.6 %collective-permute-start.1 = (bf16[3,32,512]{2,1,0:T(8,128)(2,1)S(1)}, bf16[3,32,512]{2,1,0:T(8,128)(2,1)S(1)}, u32[]{:S(2)}, u32[]{:S(2)}) collective-permute-start(bf16[3,32,512]{2,1,0:T(8,128)(2,1)S(1)} %get-tuple-element.101), channel_id=1, source_target_pairs={{32,0},{64,32},{96,64},{0,96},{33,1},{65,33},{97,65},{1,97},{34,2}... | collective-permute-start | bytes 294920 | tf_op jit(solution)/shard_map/ppermute | solution.py:414
  6.6 2.2 %copy-done.13 = bf16[2,512,2048]{2,1,0:T(8,128)(2,1)S(1)} copy-done((bf16[2,512,2048]{2,1,0:T(8,128)(2,1)S(1)}, bf16[2,512,2048]{2,1,0:T(8,128)(2,1)}, u32[]{:S(2)}) %copy-start.13) | copy-done | bytes 4194328
  8.8 2.2 %copy-done.14 = bf16[2,2048,512]{2,1,0:T(8,128)(2,1)S(1)} copy-done((bf16[2,2048,512]{2,1,0:T(8,128)(2,1)S(1)}, bf16[2,2048,512]{2,1,0:T(8,128)(2,1)}, u32[]{:S(2)}) %copy-start.14) | copy-done | bytes 4194328
  15.3 4.7 %fold.1 = (bf16[2,512,2048]{2,1,0:T(8,128)(2,1)S(1)}, bf16[2,2048,512]{2,1,0:T(8,128)(2,1)S(1)}, f32[2,49,8,128]{3,2,1,0:T(8,128)S(1)}) custom-call(bf16[2,512,2048]{2,1,0:T(8,128)(2,1)S(1)} %copy-done.13, bf16[2,16,512]{2,1,0:T(8,128)(2,1)S(1)} %bitcast.37, bf16[2,16,2048]{2,1,0:T(8,128)(2,1)S(1)} %copy-done.17, bf16[2,2048,512]{2,1,0:T(8,128)(2,1)S(1)} %copy-done.14, ...), custom_call_target="tpu_custom_call" | custom-call | tf_op jit(solution)/shard_map/fold/pallas_call | solution.py:375
  24.1 2.6 %collective-permute-start.2 = (bf16[3,48,512]{2,1,0:T(8,128)(2,1)S(1)}, bf16[3,48,512]{2,1,0:T(8,128)(2,1)S(1)}, u32[]{:S(2)}, u32[]{:S(2)}) collective-permute-start(bf16[3,48,512]{2,1,0:T(8,128)(2,1)S(1)} %get-tuple-element.57), channel_id=1, source_target_pairs={{0,2},{2,4},{4,6},{6,8},{8,10},{10,12},{12,14},{14,16},{16,18},{18... | collective-permute-start | bytes 442376 | tf_op jit(solution)/shard_map/ppermute | solution.py:414
  26.7 10.1 %conv.3.cv = f32[4096,128]{1,0:T(8,128)S(1)} custom-call(f32[4]{0:T(128)S(1)} %add_convert_fusion.7.flags, bf16[32,32,512]{2,1,0:T(8,128)(2,1)S(1)} %bitcast.26, bf16[3,32,512]{2,1,0:T(8,128)(2,1)S(1)} %collective-permute-done.refs_1_.refs_2_, bf16[3,32,512]{2,1,0:T(8,128)(2,1)S(1)} %collective-permute-done.1.refs_2_.refs_3_, ...), custom_call_target="tpu_custom_call" | custom-call | tf_op jit(solution)/shard_map/conv/pallas_call | solution.py:375
  36.9 2.2 %copy-done.1 = bf16[2,2048,512]{2,1,0:T(8,128)(2,1)S(1)} copy-done((bf16[2,2048,512]{2,1,0:T(8,128)(2,1)S(1)}, bf16[2,2048,512]{2,1,0:T(8,128)(2,1)}, u32[]{:S(2)}) %copy-start.1) | copy-done | bytes 4194328
  39.0 2.2 %copy-done.5 = bf16[2,512,2048]{2,1,0:T(8,128)(2,1)S(1)} copy-done((bf16[2,512,2048]{2,1,0:T(8,128)(2,1)S(1)}, bf16[2,512,2048]{2,1,0:T(8,128)(2,1)}, u32[]{:S(2)}) %copy-start.5) | copy-done | bytes 4194328
  41.2 7.6 %first_outer.1 = (bf16[1024,512]{1,0:T(8,128)(2,1)}, bf16[1024,2048]{1,0:T(8,128)(2,1)}, bf16[1024,2048]{1,0:T(8,128)(2,1)}, bf16[1024,16]{1,0:T(8,128)(2,1)S(1)...) custom-call(f32[4]{0:T(128)S(1)} %add_convert_fusion.7.flags, ...), custom_call_target="tpu_custom_call" | custom-call | tf_op jit(solution)/shard_map/first_outer/pallas_call | solution.py:375
  49.1 2.6 %collective-permute-start.5 = (bf16[3,32,512]{2,1,0:T(8,128)(2,1)S(1)}, bf16[3,32,512]{2,1,0:T(8,128)(2,1)S(1)}, u32[]{:S(2)}, u32[]{:S(2)}) collective-permute-start(bf16[3,32,512]{2,1,0:T(8,128)(2,1)S(1)} %get-tuple-element.69), channel_id=1, source_target_pairs={{32,0},{64,32},{96,64},{0,96},{33,1},{65,33},{97,65},{1,97},{34,2}... | collective-permute-start | bytes 294920 | tf_op jit(solution)/shard_map/ppermute | solution.py:414
  51.7 7.3 %first_inner.1 = (bf16[1024,512]{1,0:T(8,128)(2,1)}, bf16[1024,2048]{1,0:T(8,128)(2,1)}, bf16[1024,2048]{1,0:T(8,128)(2,1)}, bf16[1024,16]{1,0:T(8,128)(2,1)S(1)...) custom-call(f32[4]{0:T(128)S(1)} %add_convert_fusion.7.flags, ...), custom_call_target="tpu_custom_call", output_to_operand_aliasing={{0}: (14, {}), {1}: (15, {}), {2}: (16, {}), {3}: (17, {}),... | custom-call | tf_op jit(solution)/shard_map/first_inner/pallas_call | solution.py:375
  59.2 2.1 %collective-permute-start.6 = (bf16[3,48,512]{2,1,0:T(8,128)(2,1)S(1)}, bf16[3,48,512]{2,1,0:T(8,128)(2,1)S(1)}, u32[]{:S(2)}, u32[]{:S(2)}) collective-permute-start(bf16[3,48,512]{2,1,0:T(8,128)(2,1)S(1)} %get-tuple-element.74), channel_id=1, source_target_pairs={{0,2},{2,4},{4,6},{6,8},{8,10},{10,12},{12,14},{14,16},{16,18},{18... | collective-permute-start | bytes 442376 | tf_op jit(solution)/shard_map/ppermute | solution.py:414
  61.3 2.7 %collective-permute-start.7 = (bf16[3,48,512]{2,1,0:T(8,128)(2,1)S(1)}, bf16[3,48,512]{2,1,0:T(8,128)(2,1)S(1)}, u32[]{:S(2)}, u32[]{:S(2)}) collective-permute-start(bf16[3,48,512]{2,1,0:T(8,128)(2,1)S(1)} %get-tuple-element.75), channel_id=1, source_target_pairs={{2,0},{4,2},{6,4},{8,6},{10,8},{12,10},{14,12},{16,14},{18,16},{20... | collective-permute-start | bytes 442376 | tf_op jit(solution)/shard_map/ppermute | solution.py:414
  64.0 9.9 %conv.4.cv = f32[4096,128]{1,0:T(8,128)S(1)} custom-call(f32[4]{0:T(128)S(1)} %add_convert_fusion.7.flags, bf16[16,32,512]{2,1,0:T(8,128)(2,1)S(1)} %get-tuple-element.67.refs_0_.x, bf16[16,32,512]{2,1,0:T(8,128)(2,1)S(1)} %get-tuple-element.66.refs_1_.x, bf16[3,32,512]{2,1,0:T(8,128)(2,1)S(1)} %collective-permute-done.4.refs_2_.refs_4_, ...), custom_call_target="tpu_custom_call" | custom-call | tf_op jit(solution)/shard_map/conv/pallas_call | solution.py:375
  73.9 10.4 %second_outer.1 = (bf16[32,32,512]{2,1,0:T(8,128)(2,1)}, f32[16,5120]{1,0:T(8,128)S(1)}, bf16[16,32,512]{2,1,0:T(8,128)(2,1)S(1)}, bf16[3,32,512]{2,1,0:T(8,128)...) custom-call(f32[4]{0:T(128)S(1)} %add_convert_fusion.7.flags, ...), custom_call_target="tpu_custom_call" | custom-call | tf_op jit(solution)/shard_map/second_outer/pallas_call | solution.py:375
  84.3 2.7 %collective-permute-start.9 = (bf16[3,32,512]{2,1,0:T(8,128)(2,1)S(1)}, bf16[3,32,512]{2,1,0:T(8,128)(2,1)S(1)}, u32[]{:S(2)}, u32[]{:S(2)}) collective-permute-start(bf16[3,32,512]{2,1,0:T(8,128)(2,1)S(1)} %get-tuple-element.82), channel_id=1, source_target_pairs={{32,0},{64,32},{96,64},{0,96},{33,1},{65,33},{97,65},{1,97},{34,2}... | collective-permute-start | bytes 294920 | tf_op jit(solution)/shard_map/ppermute | solution.py:414
  87.0 10.2 %second_inner.1 = (bf16[32,32,512]{2,1,0:T(8,128)(2,1)}, f32[16,5120]{1,0:T(8,128)S(1)}, bf16[16,32,512]{2,1,0:T(8,128)(2,1)S(1)}, bf16[3,16,512]{2,1,0:T(8,128)(2,1)S(1)}, bf16[3,16,512]{2,1,0:T(8,128)(2,1)S(1)}) custom-call(f32[4]{0:T(128)S(1)} %add_convert_fusion.7.flags, ...), custom_call_target="tpu_custom_call", output_to_operand_aliasing={{0}: (17, {})} | custom-call | tf_op jit(solution)/shard_map/second_inner/pallas_call | solution.py:375
  99.4 5.6 %collective-permute-start.11 = (bf16[3,48,512]{2,1,0:T(8,128)(2,1)}, bf16[3,48,512]{2,1,0:T(8,128)(2,1)}, u32[]{:S(2)}, u32[]{:S(2)}) collective-permute-start(bf16[3,48,512]{2,1,0:T(8,128)(2,1)} %get-tuple-element.88), channel_id=1, source_target_pairs={{2,0},{4,2},{6,4},{8,6},{10,8},{12,10},{14,12},{16,14},{18,16},{20... | collective-permute-start | bytes 442376 | tf_op jit(solution)/shard_map/ppermute | solution.py:414
  108.9 9.9 %conv.5.cv = f32[4096,128]{1,0:T(8,128)S(1)} custom-call(f32[4]{0:T(128)S(1)} %add_convert_fusion.7.flags, bf16[16,32,512]{2,1,0:T(8,128)(2,1)S(1)} %copy-done.24, bf16[16,32,512]{2,1,0:T(8,128)(2,1)S(1)} %copy-done.26, bf16[3,32,512]{2,1,0:T(8,128)(2,1)S(1)} %copy-done.28, bf16[3,32,512]{2,1,0:T(8,128)(2,1)S(1)} %copy-done.30, ...), custom_call_target="tpu_custom_call" | custom-call | tf_op jit(solution)/shard_map/conv/pallas_call | solution.py:375
  118.9 2.2 %copy-done.3 = bf16[2,2048,512]{2,1,0:T(8,128)(2,1)S(1)} copy-done((bf16[2,2048,512]{2,1,0:T(8,128)(2,1)S(1)}, bf16[2,2048,512]{2,1,0:T(8,128)(2,1)}, u32[]{:S(2)}) %copy-start.3) | copy-done | bytes 4194328
  121.1 2.2 %copy-done.9 = bf16[1024,2048]{1,0:T(8,128)(2,1)S(1)} copy-done((bf16[1024,2048]{1,0:T(8,128)(2,1)S(1)}, bf16[1024,2048]{1,0:T(8,128)(2,1)}, u32[]{:S(2)}) %copy-start.9) | copy-done | bytes 4194328
  123.3 2.2 %copy-done.10 = bf16[1024,2048]{1,0:T(8,128)(2,1)S(1)} copy-done((bf16[1024,2048]{1,0:T(8,128)(2,1)S(1)}, bf16[1024,2048]{1,0:T(8,128)(2,1)}, u32[]{:S(2)}) %copy-start.10) | copy-done | bytes 4194328
  125.5 9.2 %third.1 = f32[16,5120]{1,0:T(8,128)S(1)} custom-call(f32[4]{0:T(128)S(1)} %add_convert_fusion.7.flags, bf16[32,32,512]{2,1,0:T(8,128)(2,1)S(1)} %bitcast.31, f32[4096,128]{1,0:T(8,128)S(1)} %conv.5.cv, bf16[3,48,512]{2,1,0:T(8,128)(2,1)} %collective-permute-done.10.w, bf16[3,48,512]{2,1,0:T(8,128)(2,1)} %collective-permute-done.11.e, ...), custom_call_target="tpu_custom_call" | custom-call | tf_op jit(solution)/shard_map/third/pallas_call | solution.py:375
  134.7 5.4 %collective-permute-start.12 = (bf16[16,5120]{1,0:T(8,128)(2,1)S(1)}, bf16[16,5120]{1,0:T(8,128)(2,1)S(1)}, u32[]{:S(2)}, u32[]{:S(2)}) collective-permute-start(bf16[16,5120]{1,0:T(8,128)(2,1)S(1)} %select_convert_fusion), channel_id=1, source_target_pairs={{0,2},{2,0},{4,6},{6,4},{8,10},{10,8},{12,14},{14,12},{16,18},{18,... | collective-permute-start | bytes 491528 | tf_op jit(solution)/shard_map/ppermute | solution.py:435
  141.4 4.5 %collective-permute-done.13 = bf16[16,5120]{1,0:T(8,128)(2,1)S(1)} collective-permute-done((bf16[16,5120]{1,0:T(8,128)(2,1)S(1)}, bf16[16,5120]{1,0:T(8,128)(2,1)S(1)}, u32[]{:S(2)}, u32[]{:S(2)}) %collective-permute-start.13) | collective-permute-done | bytes 163872 | tf_op jit(solution)/shard_map/ppermute | solution.py:438
  145.9 6.0 %collective-permute-done.14 = bf16[16,5120]{1,0:T(8,128)(2,1)S(1)} collective-permute-done((bf16[16,5120]{1,0:T(8,128)(2,1)S(1)}, bf16[16,5120]{1,0:T(8,128)(2,1)S(1)}, u32[]{:S(2)}, u32[]{:S(2)}) %collective-permute-start.14) | collective-permute-done | bytes 163872 | tf_op jit(solution)/shard_map/ppermute | solution.py:438
  152.9 3.3 %collective-permute-done.15 = bf16[16,5120]{1,0:T(8,128)(2,1)S(1)} collective-permute-done((bf16[16,5120]{1,0:T(8,128)(2,1)S(1)}, bf16[16,5120]{1,0:T(8,128)(2,1)S(1)}, u32[]{:S(2)}, u32[]{:S(2)}) %collective-permute-start.15) | collective-permute-done | bytes 163872 | tf_op jit(solution)/shard_map/ppermute | solution.py:438
  156.2 2.4 %collective-permute-start.16 = (bf16[16,5120]{1,0:T(8,128)(2,1)S(1)}, bf16[16,5120]{1,0:T(8,128)(2,1)S(1)}, u32[]{:S(2)}, u32[]{:S(2)}) collective-permute-start(bf16[16,5120]{1,0:T(8,128)(2,1)S(1)} %add_convert_fusion.3), channel_id=1, source_target_pairs={{0,8},{1,9},{2,18},{3,19},{4,12},{5,13},{6,22},{7,23},{8,0},{9,1},... | collective-permute-start | bytes 491528 | tf_op jit(solution)/shard_map/ppermute | solution.py:438
  158.7 3.3 %collective-permute-done.16 = bf16[16,5120]{1,0:T(8,128)(2,1)S(1)} collective-permute-done((bf16[16,5120]{1,0:T(8,128)(2,1)S(1)}, bf16[16,5120]{1,0:T(8,128)(2,1)S(1)}, u32[]{:S(2)}, u32[]{:S(2)}) %collective-permute-start.16) | collective-permute-done | bytes 163872 | tf_op jit(solution)/shard_map/ppermute | solution.py:438
  162.1 4.2 %collective-permute-done.17 = bf16[16,5120]{1,0:T(8,128)(2,1)S(1)} collective-permute-done((bf16[16,5120]{1,0:T(8,128)(2,1)S(1)}, bf16[16,5120]{1,0:T(8,128)(2,1)S(1)}, u32[]{:S(2)}, u32[]{:S(2)}) %collective-permute-start.17) | collective-permute-done | bytes 163872 | tf_op jit(solution)/shard_map/ppermute | solution.py:438
  166.4 5.7 %collective-permute-done.18 = bf16[16,5120]{1,0:T(8,128)(2,1)S(1)} collective-permute-done((bf16[16,5120]{1,0:T(8,128)(2,1)S(1)}, bf16[16,5120]{1,0:T(8,128)(2,1)S(1)}, u32[]{:S(2)}, u32[]{:S(2)}) %collective-permute-start.18) | collective-permute-done | bytes 163872 | tf_op jit(solution)/shard_map/ppermute | solution.py:438
  172.1 6.8 %collective-permute-start.19 = (bf16[16,5120]{1,0:T(8,128)(2,1)S(1)}, bf16[16,5120]{1,0:T(8,128)(2,1)S(1)}, u32[]{:S(2)}, u32[]{:S(2)}) collective-permute-start(bf16[16,5120]{1,0:T(8,128)(2,1)S(1)} %add_convert_fusion), channel_id=1, source_target_pairs={{0,2},{2,0},{4,6},{6,4},{8,10},{10,8},{12,14},{14,12},{16,18},{18,... | collective-permute-start | bytes 491528 | tf_op jit(solution)/shard_map/ppermute | solution.py:440
  (112 shorter events, 22.9 us)
Async XLA Ops:
  1.6 22.4 %collective-permute-start.1 = (bf16[3,32,512]{2,1,0:T(8,128)(2,1)S(1)}, bf16[3,32,512]{2,1,0:T(8,128)(2,1)S(1)}, u32[]{:S(2)}, u32[]{:S(2)}) collective-permute-start(bf16[3,32,512]{2,1,0:T(8,128)(2,1)S(1)} %get-tuple-element.101), channel_id=1, source_target_pairs={{32,0},{64,32},{96,64},{0,96},{33,1},{65,33},{97,65},{1,97},{34,2}... | collective-permute-start | bytes 294920 | tf_op jit(solution)/shard_map/ppermute | solution.py:414
  5.2 18.8 %collective-permute-start = (bf16[3,32,512]{2,1,0:T(8,128)(2,1)S(1)}, bf16[3,32,512]{2,1,0:T(8,128)(2,1)S(1)}, u32[]{:S(2)}, u32[]{:S(2)}) collective-permute-start(bf16[3,32,512]{2,1,0:T(8,128)(2,1)S(1)} %get-tuple-element.102), channel_id=1, source_target_pairs={{0,32},{32,64},{64,96},{96,0},{1,33},{33,65},{65,97},{97,1},{2,34}... | collective-permute-start | bytes 294920 | tf_op jit(solution)/shard_map/ppermute | solution.py:414
  15.3 21.5 %copy-start.32 = (f32[2,512]{1,0:T(2,128)S(1)}, f32[2,512]{1,0:T(2,128)}, u32[]{:S(2)}) copy-start(f32[2,512]{1,0:T(2,128)} %scale.9) | copy-start | bytes 12292
  15.3 21.5 %copy-start.33 = (f32[2,512]{1,0:T(2,128)S(1)}, f32[2,512]{1,0:T(2,128)}, u32[]{:S(2)}) copy-start(f32[2,512]{1,0:T(2,128)} %bias.7) | copy-start | bytes 12292
  15.3 21.5 %copy-start.34 = (f32[2,512]{1,0:T(2,128)S(1)}, f32[2,512]{1,0:T(2,128)}, u32[]{:S(2)}) copy-start(f32[2,512]{1,0:T(2,128)} %gain.7) | copy-start | bytes 12292
  15.3 21.6 %copy-start.35 = (f32[2,512]{1,0:T(2,128)S(1)}, f32[2,512]{1,0:T(2,128)}, u32[]{:S(2)}) copy-start(f32[2,512]{1,0:T(2,128)} %shift.7) | copy-start | bytes 12292
  24.0 12.9 %copy-start.20 = (bf16[2,512,16]{1,2,0:T(8,128)(2,1)S(1)}, bf16[2,512,16]{1,2,0:T(8,128)(2,1)}, u32[]{:S(2)}) copy-start(bf16[2,512,16]{1,2,0:T(8,128)(2,1)} %param.21) | copy-start | bytes 98308
  24.1 12.7 %collective-permute-start.2 = (bf16[3,48,512]{2,1,0:T(8,128)(2,1)S(1)}, bf16[3,48,512]{2,1,0:T(8,128)(2,1)S(1)}, u32[]{:S(2)}, u32[]{:S(2)}) collective-permute-start(bf16[3,48,512]{2,1,0:T(8,128)(2,1)S(1)} %get-tuple-element.57), channel_id=1, source_target_pairs={{0,2},{2,4},{4,6},{6,8},{8,10},{10,12},{12,14},{14,16},{16,18},{18... | collective-permute-start | bytes 442376 | tf_op jit(solution)/shard_map/ppermute | solution.py:414
  26.6 10.2 %collective-permute-start.3 = (bf16[3,48,512]{2,1,0:T(8,128)(2,1)S(1)}, bf16[3,48,512]{2,1,0:T(8,128)(2,1)S(1)}, u32[]{:S(2)}, u32[]{:S(2)}) collective-permute-start(bf16[3,48,512]{2,1,0:T(8,128)(2,1)S(1)} %get-tuple-element.58), channel_id=1, source_target_pairs={{2,0},{4,2},{6,4},{8,6},{10,8},{12,10},{14,12},{16,14},{18,16},{20... | collective-permute-start | bytes 442376 | tf_op jit(solution)/shard_map/ppermute | solution.py:414
  48.8 10.3 %collective-permute-start.4 = (bf16[3,32,512]{2,1,0:T(8,128)(2,1)S(1)}, bf16[3,32,512]{2,1,0:T(8,128)(2,1)S(1)}, u32[]{:S(2)}, u32[]{:S(2)}) collective-permute-start(bf16[3,32,512]{2,1,0:T(8,128)(2,1)S(1)} %get-tuple-element.68), channel_id=1, source_target_pairs={{0,32},{32,64},{64,96},{96,0},{1,33},{33,65},{65,97},{97,1},{2,34}... | collective-permute-start | bytes 294920 | tf_op jit(solution)/shard_map/ppermute | solution.py:414
  49.1 10.0 %collective-permute-start.5 = (bf16[3,32,512]{2,1,0:T(8,128)(2,1)S(1)}, bf16[3,32,512]{2,1,0:T(8,128)(2,1)S(1)}, u32[]{:S(2)}, u32[]{:S(2)}) collective-permute-start(bf16[3,32,512]{2,1,0:T(8,128)(2,1)S(1)} %get-tuple-element.69), channel_id=1, source_target_pairs={{32,0},{64,32},{96,64},{0,96},{33,1},{65,33},{97,65},{1,97},{34,2}... | collective-permute-start | bytes 294920 | tf_op jit(solution)/shard_map/ppermute | solution.py:414
  51.7 22.1 %copy-start.2 = (bf16[2,2048,512]{2,1,0:T(8,128)(2,1)S(1)}, bf16[2,2048,512]{2,1,0:T(8,128)(2,1)}, u32[]{:S(2)}) copy-start(bf16[2,2048,512]{2,1,0:T(8,128)(2,1)} %copy-done) | copy-start | bytes 12582916
  51.7 22.1 %copy-start.6 = (bf16[2,512,2048]{2,1,0:T(8,128)(2,1)S(1)}, bf16[2,512,2048]{2,1,0:T(8,128)(2,1)}, u32[]{:S(2)}) copy-start(bf16[2,512,2048]{2,1,0:T(8,128)(2,1)} %copy-done.4) | copy-start | bytes 12582916
  51.7 22.1 %copy-start.22 = (bf16[2,16,512]{2,1,0:T(8,128)(2,1)S(1)}, bf16[2,16,512]{2,1,0:T(8,128)(2,1)}, u32[]{:S(2)}) copy-start(bf16[2,16,512]{2,1,0:T(8,128)(2,1)} %bout.7) | copy-start | bytes 98308
  59.1 14.8 %copy-start.11 = (bf16[1,32,32,512]{3,2,1,0:T(8,128)(2,1)S(1)}, bf16[1,32,32,512]{3,2,1,0:T(8,128)(2,1)}, u32[]{:S(2)}) copy-start(bf16[1,32,32,512]{3,2,1,0:T(8,128)(2,1)} %param.14) | copy-start | bytes 3145732
  59.1 14.8 %copy-start.18 = (bf16[2,16,2048]{2,1,0:T(8,128)(2,1)S(1)}, bf16[2,16,2048]{2,1,0:T(8,128)(2,1)}, u32[]{:S(2)}) copy-start(bf16[2,16,2048]{2,1,0:T(8,128)(2,1)} %bin_.7) | copy-start | bytes 393220
  59.2 14.7 %collective-permute-start.6 = (bf16[3,48,512]{2,1,0:T(8,128)(2,1)S(1)}, bf16[3,48,512]{2,1,0:T(8,128)(2,1)S(1)}, u32[]{:S(2)}, u32[]{:S(2)}) collective-permute-start(bf16[3,48,512]{2,1,0:T(8,128)(2,1)S(1)} %get-tuple-element.74), channel_id=1, source_target_pairs={{0,2},{2,4},{4,6},{6,8},{8,10},{10,12},{12,14},{14,16},{16,18},{18... | collective-permute-start | bytes 442376 | tf_op jit(solution)/shard_map/ppermute | solution.py:414
  61.3 12.6 %collective-permute-start.7 = (bf16[3,48,512]{2,1,0:T(8,128)(2,1)S(1)}, bf16[3,48,512]{2,1,0:T(8,128)(2,1)S(1)}, u32[]{:S(2)}, u32[]{:S(2)}) collective-permute-start(bf16[3,48,512]{2,1,0:T(8,128)(2,1)S(1)} %get-tuple-element.75), channel_id=1, source_target_pairs={{2,0},{4,2},{6,4},{8,6},{10,8},{12,10},{14,12},{16,14},{18,16},{20... | collective-permute-start | bytes 442376 | tf_op jit(solution)/shard_map/ppermute | solution.py:414
  84.3 12.9 %copy-start.23 = (bf16[16,32,512]{2,1,0:T(8,128)(2,1)}, bf16[16,32,512]{2,1,0:T(8,128)(2,1)S(1)}, u32[]{:S(2)}) copy-start(bf16[16,32,512]{2,1,0:T(8,128)(2,1)S(1)} %get-tuple-element.79.refs_0_) | copy-start | bytes 1572868
  84.3 13.7 %collective-permute-start.8 = (bf16[3,32,512]{2,1,0:T(8,128)(2,1)S(1)}, bf16[3,32,512]{2,1,0:T(8,128)(2,1)S(1)}, u32[]{:S(2)}, u32[]{:S(2)}) collective-permute-start(bf16[3,32,512]{2,1,0:T(8,128)(2,1)S(1)} %get-tuple-element.81), channel_id=1, source_target_pairs={{0,32},{32,64},{64,96},{96,0},{1,33},{33,65},{65,97},{97,1},{2,34}... | collective-permute-start | bytes 294920 | tf_op jit(solution)/shard_map/ppermute | solution.py:414
  84.3 13.7 %collective-permute-start.9 = (bf16[3,32,512]{2,1,0:T(8,128)(2,1)S(1)}, bf16[3,32,512]{2,1,0:T(8,128)(2,1)S(1)}, u32[]{:S(2)}, u32[]{:S(2)}) collective-permute-start(bf16[3,32,512]{2,1,0:T(8,128)(2,1)S(1)} %get-tuple-element.82), channel_id=1, source_target_pairs={{32,0},{64,32},{96,64},{0,96},{33,1},{65,33},{97,65},{1,97},{34,2}... | collective-permute-start | bytes 294920 | tf_op jit(solution)/shard_map/ppermute | solution.py:414
  98.0 20.9 %copy-start.12 = (bf16[1024,512]{1,0:T(8,128)(2,1)S(1)}, bf16[1024,512]{1,0:T(8,128)(2,1)}, u32[]{:S(2)}) copy-start(bf16[1024,512]{1,0:T(8,128)(2,1)} %get-tuple-element.91.nrm_far) | copy-start | bytes 3145732
  99.4 19.5 %collective-permute-start.10 = (bf16[3,48,512]{2,1,0:T(8,128)(2,1)}, bf16[3,48,512]{2,1,0:T(8,128)(2,1)}, u32[]{:S(2)}, u32[]{:S(2)}) collective-permute-start(bf16[3,48,512]{2,1,0:T(8,128)(2,1)} %get-tuple-element.87), channel_id=1, source_target_pairs={{0,2},{2,4},{4,6},{6,8},{8,10},{10,12},{12,14},{14,16},{16,18},{18... | collective-permute-start | bytes 442376 | tf_op jit(solution)/shard_map/ppermute | solution.py:414
  99.4 19.5 %collective-permute-start.11 = (bf16[3,48,512]{2,1,0:T(8,128)(2,1)}, bf16[3,48,512]{2,1,0:T(8,128)(2,1)}, u32[]{:S(2)}, u32[]{:S(2)}) collective-permute-start(bf16[3,48,512]{2,1,0:T(8,128)(2,1)} %get-tuple-element.88), channel_id=1, source_target_pairs={{2,0},{4,2},{6,4},{8,6},{10,8},{12,10},{14,12},{16,14},{18,16},{20... | collective-permute-start | bytes 442376 | tf_op jit(solution)/shard_map/ppermute | solution.py:414
  134.7 6.5 %collective-permute-start.12 = (bf16[16,5120]{1,0:T(8,128)(2,1)S(1)}, bf16[16,5120]{1,0:T(8,128)(2,1)S(1)}, u32[]{:S(2)}, u32[]{:S(2)}) collective-permute-start(bf16[16,5120]{1,0:T(8,128)(2,1)S(1)} %select_convert_fusion), channel_id=1, source_target_pairs={{0,2},{2,0},{4,6},{6,4},{8,10},{10,8},{12,14},{14,12},{16,18},{18,... | collective-permute-start | bytes 491528 | tf_op jit(solution)/shard_map/ppermute | solution.py:435
  141.3 4.5 %collective-permute-start.13 = (bf16[16,5120]{1,0:T(8,128)(2,1)S(1)}, bf16[16,5120]{1,0:T(8,128)(2,1)S(1)}, u32[]{:S(2)}, u32[]{:S(2)}) collective-permute-start(bf16[16,5120]{1,0:T(8,128)(2,1)S(1)} %add_convert_fusion.6), channel_id=1, source_target_pairs={{0,32},{1,33},{2,6},{3,7},{4,36},{5,37},{6,2},{7,3},{8,40},{9,41},... | collective-permute-start | bytes 491528 | tf_op jit(solution)/shard_map/ppermute | solution.py:438
  145.9 6.0 %collective-permute-start.14 = (bf16[16,5120]{1,0:T(8,128)(2,1)S(1)}, bf16[16,5120]{1,0:T(8,128)(2,1)S(1)}, u32[]{:S(2)}, u32[]{:S(2)}) collective-permute-start(bf16[16,5120]{1,0:T(8,128)(2,1)S(1)} %add_convert_fusion.5), channel_id=1, source_target_pairs={{0,64},{1,65},{2,10},{3,11},{4,68},{5,69},{6,14},{7,15},{8,72},{9,... | collective-permute-start | bytes 491528 | tf_op jit(solution)/shard_map/ppermute | solution.py:438
  151.9 4.2 %collective-permute-start.15 = (bf16[16,5120]{1,0:T(8,128)(2,1)S(1)}, bf16[16,5120]{1,0:T(8,128)(2,1)S(1)}, u32[]{:S(2)}, u32[]{:S(2)}) collective-permute-start(bf16[16,5120]{1,0:T(8,128)(2,1)S(1)} %add_convert_fusion.4), channel_id=1, source_target_pairs={{0,4},{1,5},{2,3},{3,2},{4,0},{5,1},{6,7},{7,6},{8,12},{9,13},{10,... | collective-permute-start | bytes 491528 | tf_op jit(solution)/shard_map/ppermute | solution.py:438
  156.2 5.8 %collective-permute-start.16 = (bf16[16,5120]{1,0:T(8,128)(2,1)S(1)}, bf16[16,5120]{1,0:T(8,128)(2,1)S(1)}, u32[]{:S(2)}, u32[]{:S(2)}) collective-permute-start(bf16[16,5120]{1,0:T(8,128)(2,1)S(1)} %add_convert_fusion.3), channel_id=1, source_target_pairs={{0,8},{1,9},{2,18},{3,19},{4,12},{5,13},{6,22},{7,23},{8,0},{9,1},... | collective-permute-start | bytes 491528 | tf_op jit(solution)/shard_map/ppermute | solution.py:438
  162.0 4.2 %collective-permute-start.17 = (bf16[16,5120]{1,0:T(8,128)(2,1)S(1)}, bf16[16,5120]{1,0:T(8,128)(2,1)S(1)}, u32[]{:S(2)}, u32[]{:S(2)}) collective-permute-start(bf16[16,5120]{1,0:T(8,128)(2,1)S(1)} %add_convert_fusion.2), channel_id=1, source_target_pairs={{0,1},{1,0},{2,34},{3,35},{4,5},{5,4},{6,38},{7,39},{8,9},{9,8},{1... | collective-permute-start | bytes 491528 | tf_op jit(solution)/shard_map/ppermute | solution.py:438
  166.3 5.8 %collective-permute-start.18 = (bf16[16,5120]{1,0:T(8,128)(2,1)S(1)}, bf16[16,5120]{1,0:T(8,128)(2,1)S(1)}, u32[]{:S(2)}, u32[]{:S(2)}) collective-permute-start(bf16[16,5120]{1,0:T(8,128)(2,1)S(1)} %add_convert_fusion.1), channel_id=1, source_target_pairs={{0,16},{1,17},{2,66},{3,67},{4,20},{5,21},{6,70},{7,71},{8,24},{9,... | collective-permute-start | bytes 491528 | tf_op jit(solution)/shard_map/ppermute | solution.py:438
  172.1 7.8 %collective-permute-start.19 = (bf16[16,5120]{1,0:T(8,128)(2,1)S(1)}, bf16[16,5120]{1,0:T(8,128)(2,1)S(1)}, u32[]{:S(2)}, u32[]{:S(2)}) collective-permute-start(bf16[16,5120]{1,0:T(8,128)(2,1)S(1)} %add_convert_fusion), channel_id=1, source_target_pairs={{0,2},{2,0},{4,6},{6,4},{8,10},{10,8},{12,14},{14,12},{16,18},{18,... | collective-permute-start | bytes 491528 | tf_op jit(solution)/shard_map/ppermute | solution.py:440
  (24 other events, 55.2 us)

commit v5 on v4

--- a/solution.py
+++ b/solution.py
@@ -352,6 +352,7 @@
     grads[:, 4608:5120] += t_dot(mid_out[...], go)
 
 
+MICROSECONDS = {'conv': 8, 'fold': 5, 'first_outer': 7, 'first_inner': 7, 'second_outer': 10, 'second_inner': 10, 'third': 9, 'edges': 1, 'pack': 1}
 SMEM = pl.BlockSpec(memory_space=pltpu.SMEM)
 ANY = pl.BlockSpec(memory_space=pl.ANY)
 HE = pltpu.VMEM((40 * 48, 128), f32)
@@ -384,6 +385,7 @@
         scratch_shapes=scratch,
         input_output_aliases=aliases,
         name=name,
+        cost_estimate=pl.CostEstimate(flops=MICROSECONDS[name] * 10**9, bytes_accessed=10**6, transcendentals=0),
         compiler_params=pltpu.CompilerParams(vmem_limit_bytes=limit * 2**20),
     )(*[array for array, _ in ins])
 

time: 183 us -> 163 us (0.89)
  local copies, waits for them, and re-layouts: 31.1 us -> 10.9 us
    unnamed x72 -> x42, local copies, waits for them, and re-layouts: 30.1 us -> 9.9 us
  transfers between devices with their start and end apart: 20 -> 20, of which waited for: 8 -> 8; matrix products, arithmetic and copies ran while one was open for 0% -> 0% of each run, Pallas kernels for 29% -> 33%
where the time goes in v5:
time: 163 us
  Pallas kernels  81.1 us (50%)
  starting transfers between devices  38.3 us (23%)
  waiting for transfers between devices  29 us (18%)
  local copies, waits for them, and re-layouts  10.9 us (7%)
  other arithmetic  2.39 us (1%)
    pallas_call x13, Pallas kernels, call(): pl.pallas_call(kernel, grid=grid if isinstance(grid, tuple) else (grid,),...  81.1 us
    ppermute x6, waiting for transfers between devices, total(): other = lax.ppermute(part, ('row', 'col', 'rep'), pairs)  26.9 us
    ppermute x12, starting transfers between devices, swap(): return (lax.ppermute(v[1], axis, after), lax.ppermute(v[0], axis, before))  22.7 us
    unnamed x42, local copies, waits for them, and re-layouts  9.9 us
    ppermute x1, starting transfers between devices, total(): back = lax.ppermute(part, 'col', pair)  6.75 us
    ppermute x1, starting transfers between devices, total(): part = (mine + lax.ppermute(other, 'col', pair).astype(f32)).astype(bf16)  5.13 us
    ppermute x6, starting transfers between devices, total(): other = lax.ppermute(part, ('row', 'col', 'rep'), pairs)  3.69 us
  transfers between devices with their start and end apart: 20, of which 8 were waited for; matrix products, arithmetic and copies ran while one was open for 0% of the time, Pallas kernels for 33%

profile of v5, /device:TPU:1, one launch (start us, length us, event | category | flops | bytes accessed | tf_op | source)
XLA Modules:
  0.0 162.6 jit_solution(1315372433026670132)
XLA Ops:
  0.6 1.0 slice_bitcast_fusion
  1.6 3.6 %collective-permute-start.1 = (bf16[3,32,512]{2,1,0:T(8,128)(2,1)S(1)}, bf16[3,32,512]{2,1,0:T(8,128)(2,1)S(1)}, u32[]{:S(2)}, u32[]{:S(2)}) collective-permute-start(bf16[3,32,512]{2,1,0:T(8,128)(2,1)S(1)} %get-tuple-element.101), channel_id=1, source_target_pairs={{32,0},{64,32},{96,64},{0,96},{33,1},{65,33},{97,65},{1,97},{34,2}... | collective-permute-start | bytes 294920 | tf_op jit(solution)/shard_map/ppermute | solution.py:416
  5.2 1.2 copy-done
  6.6 2.2 %copy-done.2 = bf16[2,512,2048]{2,1,0:T(8,128)(2,1)S(1)} copy-done((bf16[2,512,2048]{2,1,0:T(8,128)(2,1)S(1)}, bf16[2,512,2048]{2,1,0:T(8,128)(2,1)}, u32[]{:S(2)}) %copy-start.2) | copy-done | bytes 4194328
  8.8 2.2 %copy-done.3 = bf16[2,2048,512]{2,1,0:T(8,128)(2,1)S(1)} copy-done((bf16[2,2048,512]{2,1,0:T(8,128)(2,1)S(1)}, bf16[2,2048,512]{2,1,0:T(8,128)(2,1)}, u32[]{:S(2)}) %copy-start.3) | copy-done | bytes 4194328
  11.0 0.9 copy-done.5
  15.3 4.7 %fold.1 = (bf16[2,512,2048]{2,1,0:T(8,128)(2,1)S(1)}, bf16[2,2048,512]{2,1,0:T(8,128)(2,1)S(1)}, f32[2,49,8,128]{3,2,1,0:T(8,128)S(1)}) custom-call(bf16[2,512,2048]{2,1,0:T(8,128)(2,1)S(1)} %copy-done.2, bf16[2,16,512]{2,1,0:T(8,128)(2,1)S(1)} %bitcast.38, bf16[2,16,2048]{2,1,0:T(8,128)(2,1)S(1)} %copy-done.8, bf16[2,2048,512]{2,1,0:T(8,128)(2,1)S(1)} %copy-done.3, ...), custom_call_target="tpu_custom_call" | custom-call | flops 5000000000 | bytes 1000000 | tf_op jit(solution)/shard_map/fold/pallas_call | solution.py:376
  20.1 2.5 %collective-permute-start.2 = (bf16[3,48,512]{2,1,0:T(8,128)(2,1)S(1)}, bf16[3,48,512]{2,1,0:T(8,128)(2,1)S(1)}, u32[]{:S(2)}, u32[]{:S(2)}) collective-permute-start(bf16[3,48,512]{2,1,0:T(8,128)(2,1)S(1)} %get-tuple-element.57), channel_id=1, source_target_pairs={{0,2},{2,4},{4,6},{6,8},{8,10},{10,12},{12,14},{14,16},{16,18},{18... | collective-permute-start | bytes 442376 | tf_op jit(solution)/shard_map/ppermute | solution.py:416
  22.7 10.5 %conv.3.cv = f32[4096,128]{1,0:T(8,128)S(1)} custom-call(f32[4]{0:T(128)S(1)} %add_convert_fusion.7.flags, bf16[32,32,512]{2,1,0:T(8,128)(2,1)S(1)} %bitcast.26, bf16[3,32,512]{2,1,0:T(8,128)(2,1)S(1)} %collective-permute-done.refs_1_.refs_2_, bf16[3,32,512]{2,1,0:T(8,128)(2,1)S(1)} %collective-permute-done.1.refs_2_.refs_3_, ...), custom_call_target="tpu_custom_call" | custom-call | flops 8000000000 | bytes 1000000 | tf_op jit(solution)/shard_map/conv/pallas_call | solution.py:376
  33.3 7.8 %first_outer.1 = (bf16[1024,512]{1,0:T(8,128)(2,1)}, bf16[1024,2048]{1,0:T(8,128)(2,1)}, bf16[1024,2048]{1,0:T(8,128)(2,1)}, bf16[1024,16]{1,0:T(8,128)(2,1)S(1)...) custom-call(f32[4]{0:T(128)S(1)} %add_convert_fusion.7.flags, ...), custom_call_target="tpu_custom_call" | custom-call | flops 7000000000 | bytes 1000000 | tf_op jit(solution)/shard_map/first_outer/pallas_call | solution.py:376
  41.4 2.6 %collective-permute-start.5 = (bf16[3,32,512]{2,1,0:T(8,128)(2,1)S(1)}, bf16[3,32,512]{2,1,0:T(8,128)(2,1)S(1)}, u32[]{:S(2)}, u32[]{:S(2)}) collective-permute-start(bf16[3,32,512]{2,1,0:T(8,128)(2,1)S(1)} %get-tuple-element.69), channel_id=1, source_target_pairs={{32,0},{64,32},{96,64},{0,96},{33,1},{65,33},{97,65},{1,97},{34,2}... | collective-permute-start | bytes 294920 | tf_op jit(solution)/shard_map/ppermute | solution.py:416
  44.0 7.3 %first_inner.1 = (bf16[1024,512]{1,0:T(8,128)(2,1)}, bf16[1024,2048]{1,0:T(8,128)(2,1)}, bf16[1024,2048]{1,0:T(8,128)(2,1)}, bf16[1024,16]{1,0:T(8,128)(2,1)S(1)...) custom-call(f32[4]{0:T(128)S(1)} %add_convert_fusion.7.flags, ...), custom_call_target="tpu_custom_call", output_to_operand_aliasing={{0}: (14, {}), {1}: (15, {}), {2}: (16, {}), {3}: (17, {}),... | custom-call | flops 7000000000 | bytes 1000000 | tf_op jit(solution)/shard_map/first_inner/pallas_call | solution.py:376
  51.4 2.1 %collective-permute-start.6 = (bf16[3,48,512]{2,1,0:T(8,128)(2,1)S(1)}, bf16[3,48,512]{2,1,0:T(8,128)(2,1)S(1)}, u32[]{:S(2)}, u32[]{:S(2)}) collective-permute-start(bf16[3,48,512]{2,1,0:T(8,128)(2,1)S(1)} %get-tuple-element.74), channel_id=1, source_target_pairs={{0,2},{2,4},{4,6},{6,8},{8,10},{10,12},{12,14},{14,16},{16,18},{18... | collective-permute-start | bytes 442376 | tf_op jit(solution)/shard_map/ppermute | solution.py:416
  53.5 2.7 %collective-permute-start.7 = (bf16[3,48,512]{2,1,0:T(8,128)(2,1)S(1)}, bf16[3,48,512]{2,1,0:T(8,128)(2,1)S(1)}, u32[]{:S(2)}, u32[]{:S(2)}) collective-permute-start(bf16[3,48,512]{2,1,0:T(8,128)(2,1)S(1)} %get-tuple-element.75), channel_id=1, source_target_pairs={{2,0},{4,2},{6,4},{8,6},{10,8},{12,10},{14,12},{16,14},{18,16},{20... | collective-permute-start | bytes 442376 | tf_op jit(solution)/shard_map/ppermute | solution.py:416
  56.3 10.4 %conv.4.cv = f32[4096,128]{1,0:T(8,128)S(1)} custom-call(f32[4]{0:T(128)S(1)} %add_convert_fusion.7.flags, bf16[16,32,512]{2,1,0:T(8,128)(2,1)S(1)} %get-tuple-element.67.refs_0_.x, bf16[16,32,512]{2,1,0:T(8,128)(2,1)S(1)} %get-tuple-element.66.refs_1_.x, bf16[3,32,512]{2,1,0:T(8,128)(2,1)S(1)} %collective-permute-done.4.refs_2_.refs_4_, ...), custom_call_target="tpu_custom_call" | custom-call | flops 8000000000 | bytes 1000000 | tf_op jit(solution)/shard_map/conv/pallas_call | solution.py:376
  66.8 10.4 %second_outer.1 = (bf16[32,32,512]{2,1,0:T(8,128)(2,1)}, f32[16,5120]{1,0:T(8,128)S(1)}, bf16[16,32,512]{2,1,0:T(8,128)(2,1)S(1)}, bf16[3,32,512]{2,1,0:T(8,128)...) custom-call(f32[4]{0:T(128)S(1)} %add_convert_fusion.7.flags, ...), custom_call_target="tpu_custom_call" | custom-call | flops 10000000000 | bytes 1000000 | tf_op jit(solution)/shard_map/second_outer/pallas_call | solution.py:376
  77.2 2.7 %collective-permute-start.9 = (bf16[3,32,512]{2,1,0:T(8,128)(2,1)S(1)}, bf16[3,32,512]{2,1,0:T(8,128)(2,1)S(1)}, u32[]{:S(2)}, u32[]{:S(2)}) collective-permute-start(bf16[3,32,512]{2,1,0:T(8,128)(2,1)S(1)} %get-tuple-element.82), channel_id=1, source_target_pairs={{32,0},{64,32},{96,64},{0,96},{33,1},{65,33},{97,65},{1,97},{34,2}... | collective-permute-start | bytes 294920 | tf_op jit(solution)/shard_map/ppermute | solution.py:416
  79.9 10.2 %second_inner.1 = (bf16[32,32,512]{2,1,0:T(8,128)(2,1)}, f32[16,5120]{1,0:T(8,128)S(1)}, bf16[16,32,512]{2,1,0:T(8,128)(2,1)S(1)}, bf16[3,16,512]{2,1,0:T(8,128)(2,1)S(1)}, bf16[3,16,512]{2,1,0:T(8,128)(2,1)S(1)}) custom-call(f32[4]{0:T(128)S(1)} %add_convert_fusion.7.flags, ...), custom_call_target="tpu_custom_call", output_to_operand_aliasing={{0}: (17, {})} | custom-call | flops 10000000000 | bytes 1000000 | tf_op jit(solution)/shard_map/second_inner/pallas_call | solution.py:376
  90.2 6.0 %collective-permute-start.11 = (bf16[3,48,512]{2,1,0:T(8,128)(2,1)S(1)}, bf16[3,48,512]{2,1,0:T(8,128)(2,1)S(1)}, u32[]{:S(2)}, u32[]{:S(2)}) collective-permute-start(bf16[3,48,512]{2,1,0:T(8,128)(2,1)S(1)} %get-tuple-element.88), channel_id=1, source_target_pairs={{2,0},{4,2},{6,4},{8,6},{10,8},{12,10},{14,12},{16,14},{18,16},{20... | collective-permute-start | bytes 442376 | tf_op jit(solution)/shard_map/ppermute | solution.py:416
  96.2 10.4 %conv.5.cv = f32[4096,128]{1,0:T(8,128)S(1)} custom-call(f32[4]{0:T(128)S(1)} %add_convert_fusion.7.flags, bf16[16,32,512]{2,1,0:T(8,128)(2,1)S(1)} %get-tuple-element.79.refs_0_, bf16[16,32,512]{2,1,0:T(8,128)(2,1)S(1)} %get-tuple-element.80.refs_1_, bf16[3,32,512]{2,1,0:T(8,128)(2,1)S(1)} %collective-permute-done.8.refs_2_.refs_4_, ...), custom_call_target="tpu_custom_call" | custom-call | flops 8000000000 | bytes 1000000 | tf_op jit(solution)/shard_map/conv/pallas_call | solution.py:376
  106.7 9.0 %third.1 = f32[16,5120]{1,0:T(8,128)S(1)} custom-call(f32[4]{0:T(128)S(1)} %add_convert_fusion.7.flags, bf16[32,32,512]{2,1,0:T(8,128)(2,1)S(1)} %bitcast.31, f32[4096,128]{1,0:T(8,128)S(1)} %conv.5.cv, bf16[3,48,512]{2,1,0:T(8,128)(2,1)S(1)} %collective-permute-done.10.w, bf16[3,48,512]{2,1,0:T(8,128)(2,1)S(1)} %collective-permute-done.11.e, ...), custom_call_target="tpu_custom_call" | custom-call | flops 8999999488 | bytes 1000000 | tf_op jit(solution)/shard_map/third/pallas_call | solution.py:376
  115.7 5.1 %collective-permute-start.12 = (bf16[16,5120]{1,0:T(8,128)(2,1)S(1)}, bf16[16,5120]{1,0:T(8,128)(2,1)S(1)}, u32[]{:S(2)}, u32[]{:S(2)}) collective-permute-start(bf16[16,5120]{1,0:T(8,128)(2,1)S(1)} %select_convert_fusion), channel_id=1, source_target_pairs={{0,2},{2,0},{4,6},{6,4},{8,10},{10,8},{12,14},{14,12},{16,18},{18,... | collective-permute-start | bytes 491528 | tf_op jit(solution)/shard_map/ppermute | solution.py:437
  120.9 1.0 collective-permute-done.12
  122.0 4.5 %collective-permute-done.13 = bf16[16,5120]{1,0:T(8,128)(2,1)S(1)} collective-permute-done((bf16[16,5120]{1,0:T(8,128)(2,1)S(1)}, bf16[16,5120]{1,0:T(8,128)(2,1)S(1)}, u32[]{:S(2)}, u32[]{:S(2)}) %collective-permute-start.13) | collective-permute-done | bytes 163872 | tf_op jit(solution)/shard_map/ppermute | solution.py:440
  126.6 6.0 %collective-permute-done.14 = bf16[16,5120]{1,0:T(8,128)(2,1)S(1)} collective-permute-done((bf16[16,5120]{1,0:T(8,128)(2,1)S(1)}, bf16[16,5120]{1,0:T(8,128)(2,1)S(1)}, u32[]{:S(2)}, u32[]{:S(2)}) %collective-permute-start.14) | collective-permute-done | bytes 163872 | tf_op jit(solution)/shard_map/ppermute | solution.py:440
  133.5 3.3 %collective-permute-done.15 = bf16[16,5120]{1,0:T(8,128)(2,1)S(1)} collective-permute-done((bf16[16,5120]{1,0:T(8,128)(2,1)S(1)}, bf16[16,5120]{1,0:T(8,128)(2,1)S(1)}, u32[]{:S(2)}, u32[]{:S(2)}) %collective-permute-start.15) | collective-permute-done | bytes 163872 | tf_op jit(solution)/shard_map/ppermute | solution.py:440
  136.9 2.4 %collective-permute-start.16 = (bf16[16,5120]{1,0:T(8,128)(2,1)S(1)}, bf16[16,5120]{1,0:T(8,128)(2,1)S(1)}, u32[]{:S(2)}, u32[]{:S(2)}) collective-permute-start(bf16[16,5120]{1,0:T(8,128)(2,1)S(1)} %add_convert_fusion.3), channel_id=1, source_target_pairs={{0,8},{1,9},{2,18},{3,19},{4,12},{5,13},{6,22},{7,23},{8,0},{9,1},... | collective-permute-start | bytes 491528 | tf_op jit(solution)/shard_map/ppermute | solution.py:440
  139.4 3.3 %collective-permute-done.16 = bf16[16,5120]{1,0:T(8,128)(2,1)S(1)} collective-permute-done((bf16[16,5120]{1,0:T(8,128)(2,1)S(1)}, bf16[16,5120]{1,0:T(8,128)(2,1)S(1)}, u32[]{:S(2)}, u32[]{:S(2)}) %collective-permute-start.16) | collective-permute-done | bytes 163872 | tf_op jit(solution)/shard_map/ppermute | solution.py:440
  142.8 4.2 %collective-permute-done.17 = bf16[16,5120]{1,0:T(8,128)(2,1)S(1)} collective-permute-done((bf16[16,5120]{1,0:T(8,128)(2,1)S(1)}, bf16[16,5120]{1,0:T(8,128)(2,1)S(1)}, u32[]{:S(2)}, u32[]{:S(2)}) %collective-permute-start.17) | collective-permute-done | bytes 163872 | tf_op jit(solution)/shard_map/ppermute | solution.py:440
  147.1 5.7 %collective-permute-done.18 = bf16[16,5120]{1,0:T(8,128)(2,1)S(1)} collective-permute-done((bf16[16,5120]{1,0:T(8,128)(2,1)S(1)}, bf16[16,5120]{1,0:T(8,128)(2,1)S(1)}, u32[]{:S(2)}, u32[]{:S(2)}) %collective-permute-start.18) | collective-permute-done | bytes 163872 | tf_op jit(solution)/shard_map/ppermute | solution.py:440
  152.8 6.8 %collective-permute-start.19 = (bf16[16,5120]{1,0:T(8,128)(2,1)S(1)}, bf16[16,5120]{1,0:T(8,128)(2,1)S(1)}, u32[]{:S(2)}, u32[]{:S(2)}) collective-permute-start(bf16[16,5120]{1,0:T(8,128)(2,1)S(1)} %add_convert_fusion), channel_id=1, source_target_pairs={{0,2},{2,0},{4,6},{6,4},{8,10},{10,8},{12,14},{14,12},{16,18},{18,... | collective-permute-start | bytes 491528 | tf_op jit(solution)/shard_map/ppermute | solution.py:442
  159.6 1.0 collective-permute-done.19
  (82 shorter events, 7.8 us)
Async XLA Ops:
  1.6 18.5 %collective-permute-start.1 = (bf16[3,32,512]{2,1,0:T(8,128)(2,1)S(1)}, bf16[3,32,512]{2,1,0:T(8,128)(2,1)S(1)}, u32[]{:S(2)}, u32[]{:S(2)}) collective-permute-start(bf16[3,32,512]{2,1,0:T(8,128)(2,1)S(1)} %get-tuple-element.101), channel_id=1, source_target_pairs={{32,0},{64,32},{96,64},{0,96},{33,1},{65,33},{97,65},{1,97},{34,2}... | collective-permute-start | bytes 294920 | tf_op jit(solution)/shard_map/ppermute | solution.py:416
  5.2 14.8 %collective-permute-start = (bf16[3,32,512]{2,1,0:T(8,128)(2,1)S(1)}, bf16[3,32,512]{2,1,0:T(8,128)(2,1)S(1)}, u32[]{:S(2)}, u32[]{:S(2)}) collective-permute-start(bf16[3,32,512]{2,1,0:T(8,128)(2,1)S(1)} %get-tuple-element.102), channel_id=1, source_target_pairs={{0,32},{32,64},{64,96},{96,0},{1,33},{33,65},{65,97},{97,1},{2,34}... | collective-permute-start | bytes 294920 | tf_op jit(solution)/shard_map/ppermute | solution.py:416
  20.1 13.1 %collective-permute-start.2 = (bf16[3,48,512]{2,1,0:T(8,128)(2,1)S(1)}, bf16[3,48,512]{2,1,0:T(8,128)(2,1)S(1)}, u32[]{:S(2)}, u32[]{:S(2)}) collective-permute-start(bf16[3,48,512]{2,1,0:T(8,128)(2,1)S(1)} %get-tuple-element.57), channel_id=1, source_target_pairs={{0,2},{2,4},{4,6},{6,8},{8,10},{10,12},{12,14},{14,16},{16,18},{18... | collective-permute-start | bytes 442376 | tf_op jit(solution)/shard_map/ppermute | solution.py:416
  22.7 10.6 %collective-permute-start.3 = (bf16[3,48,512]{2,1,0:T(8,128)(2,1)S(1)}, bf16[3,48,512]{2,1,0:T(8,128)(2,1)S(1)}, u32[]{:S(2)}, u32[]{:S(2)}) collective-permute-start(bf16[3,48,512]{2,1,0:T(8,128)(2,1)S(1)} %get-tuple-element.58), channel_id=1, source_target_pairs={{2,0},{4,2},{6,4},{8,6},{10,8},{12,10},{14,12},{16,14},{18,16},{20... | collective-permute-start | bytes 442376 | tf_op jit(solution)/shard_map/ppermute | solution.py:416
  22.7 10.6 %copy-start.7 = (bf16[2,2048,16]{1,2,0:T(8,128)(2,1)S(1)}, bf16[2,2048,16]{1,2,0:T(8,128)(2,1)}, u32[]{:S(2)}) copy-start(bf16[2,2048,16]{1,2,0:T(8,128)(2,1)} %param.23) | copy-start | bytes 393220
  22.7 10.6 %copy-start.11 = (bf16[2,512,16]{1,2,0:T(8,128)(2,1)S(1)}, bf16[2,512,16]{1,2,0:T(8,128)(2,1)}, u32[]{:S(2)}) copy-start(bf16[2,512,16]{1,2,0:T(8,128)(2,1)} %param.21) | copy-start | bytes 98308
  22.7 10.6 %copy-start.14 = (f32[2,512]{1,0:T(2,128)S(1)}, f32[2,512]{1,0:T(2,128)}, u32[]{:S(2)}) copy-start(f32[2,512]{1,0:T(2,128)} %bias.7) | copy-start | bytes 12292
  22.7 10.6 %copy-start.15 = (f32[2,512]{1,0:T(2,128)S(1)}, f32[2,512]{1,0:T(2,128)}, u32[]{:S(2)}) copy-start(f32[2,512]{1,0:T(2,128)} %gain.7) | copy-start | bytes 12292
  22.7 10.6 %copy-start.16 = (f32[2,512]{1,0:T(2,128)S(1)}, f32[2,512]{1,0:T(2,128)}, u32[]{:S(2)}) copy-start(f32[2,512]{1,0:T(2,128)} %shift.7) | copy-start | bytes 12292
  22.7 10.6 %copy-start.17 = (f32[2,512]{1,0:T(2,128)S(1)}, f32[2,512]{1,0:T(2,128)}, u32[]{:S(2)}) copy-start(f32[2,512]{1,0:T(2,128)} %scale.9) | copy-start | bytes 12292
  41.1 10.3 %collective-permute-start.4 = (bf16[3,32,512]{2,1,0:T(8,128)(2,1)S(1)}, bf16[3,32,512]{2,1,0:T(8,128)(2,1)S(1)}, u32[]{:S(2)}, u32[]{:S(2)}) collective-permute-start(bf16[3,32,512]{2,1,0:T(8,128)(2,1)S(1)} %get-tuple-element.68), channel_id=1, source_target_pairs={{0,32},{32,64},{64,96},{96,0},{1,33},{33,65},{65,97},{97,1},{2,34}... | collective-permute-start | bytes 294920 | tf_op jit(solution)/shard_map/ppermute | solution.py:416
  41.4 10.0 %collective-permute-start.5 = (bf16[3,32,512]{2,1,0:T(8,128)(2,1)S(1)}, bf16[3,32,512]{2,1,0:T(8,128)(2,1)S(1)}, u32[]{:S(2)}, u32[]{:S(2)}) collective-permute-start(bf16[3,32,512]{2,1,0:T(8,128)(2,1)S(1)} %get-tuple-element.69), channel_id=1, source_target_pairs={{32,0},{64,32},{96,64},{0,96},{33,1},{65,33},{97,65},{1,97},{34,2}... | collective-permute-start | bytes 294920 | tf_op jit(solution)/shard_map/ppermute | solution.py:416
  51.4 15.3 %collective-permute-start.6 = (bf16[3,48,512]{2,1,0:T(8,128)(2,1)S(1)}, bf16[3,48,512]{2,1,0:T(8,128)(2,1)S(1)}, u32[]{:S(2)}, u32[]{:S(2)}) collective-permute-start(bf16[3,48,512]{2,1,0:T(8,128)(2,1)S(1)} %get-tuple-element.74), channel_id=1, source_target_pairs={{0,2},{2,4},{4,6},{6,8},{8,10},{10,12},{12,14},{14,16},{16,18},{18... | collective-permute-start | bytes 442376 | tf_op jit(solution)/shard_map/ppermute | solution.py:416
  53.5 13.2 %collective-permute-start.7 = (bf16[3,48,512]{2,1,0:T(8,128)(2,1)S(1)}, bf16[3,48,512]{2,1,0:T(8,128)(2,1)S(1)}, u32[]{:S(2)}, u32[]{:S(2)}) collective-permute-start(bf16[3,48,512]{2,1,0:T(8,128)(2,1)S(1)} %get-tuple-element.75), channel_id=1, source_target_pairs={{2,0},{4,2},{6,4},{8,6},{10,8},{12,10},{14,12},{16,14},{18,16},{20... | collective-permute-start | bytes 442376 | tf_op jit(solution)/shard_map/ppermute | solution.py:416
  56.2 10.5 %copy-start.4 = (bf16[1,32,32,512]{3,2,1,0:T(8,128)(2,1)S(1)}, bf16[1,32,32,512]{3,2,1,0:T(8,128)(2,1)}, u32[]{:S(2)}) copy-start(bf16[1,32,32,512]{3,2,1,0:T(8,128)(2,1)} %param.14) | copy-start | bytes 3145732
  56.2 10.5 %copy-start.9 = (bf16[2,16,2048]{2,1,0:T(8,128)(2,1)S(1)}, bf16[2,16,2048]{2,1,0:T(8,128)(2,1)}, u32[]{:S(2)}) copy-start(bf16[2,16,2048]{2,1,0:T(8,128)(2,1)} %bin_.7) | copy-start | bytes 393220
  56.2 10.5 %copy-start.13 = (bf16[2,16,512]{2,1,0:T(8,128)(2,1)S(1)}, bf16[2,16,512]{2,1,0:T(8,128)(2,1)}, u32[]{:S(2)}) copy-start(bf16[2,16,512]{2,1,0:T(8,128)(2,1)} %bout.7) | copy-start | bytes 98308
  77.2 12.9 %collective-permute-start.8 = (bf16[3,32,512]{2,1,0:T(8,128)(2,1)S(1)}, bf16[3,32,512]{2,1,0:T(8,128)(2,1)S(1)}, u32[]{:S(2)}, u32[]{:S(2)}) collective-permute-start(bf16[3,32,512]{2,1,0:T(8,128)(2,1)S(1)} %get-tuple-element.81), channel_id=1, source_target_pairs={{0,32},{32,64},{64,96},{96,0},{1,33},{33,65},{65,97},{97,1},{2,34}... | collective-permute-start | bytes 294920 | tf_op jit(solution)/shard_map/ppermute | solution.py:416
  77.2 12.9 %collective-permute-start.9 = (bf16[3,32,512]{2,1,0:T(8,128)(2,1)S(1)}, bf16[3,32,512]{2,1,0:T(8,128)(2,1)S(1)}, u32[]{:S(2)}, u32[]{:S(2)}) collective-permute-start(bf16[3,32,512]{2,1,0:T(8,128)(2,1)S(1)} %get-tuple-element.82), channel_id=1, source_target_pairs={{32,0},{64,32},{96,64},{0,96},{33,1},{65,33},{97,65},{1,97},{34,2}... | collective-permute-start | bytes 294920 | tf_op jit(solution)/shard_map/ppermute | solution.py:416
  90.2 16.5 %collective-permute-start.10 = (bf16[3,48,512]{2,1,0:T(8,128)(2,1)S(1)}, bf16[3,48,512]{2,1,0:T(8,128)(2,1)S(1)}, u32[]{:S(2)}, u32[]{:S(2)}) collective-permute-start(bf16[3,48,512]{2,1,0:T(8,128)(2,1)S(1)} %get-tuple-element.87), channel_id=1, source_target_pairs={{0,2},{2,4},{4,6},{6,8},{8,10},{10,12},{12,14},{14,16},{16,18},{18... | collective-permute-start | bytes 442376 | tf_op jit(solution)/shard_map/ppermute | solution.py:416
  90.2 16.4 %collective-permute-start.11 = (bf16[3,48,512]{2,1,0:T(8,128)(2,1)S(1)}, bf16[3,48,512]{2,1,0:T(8,128)(2,1)S(1)}, u32[]{:S(2)}, u32[]{:S(2)}) collective-permute-start(bf16[3,48,512]{2,1,0:T(8,128)(2,1)S(1)} %get-tuple-element.88), channel_id=1, source_target_pairs={{2,0},{4,2},{6,4},{8,6},{10,8},{12,10},{14,12},{16,14},{18,16},{20... | collective-permute-start | bytes 442376 | tf_op jit(solution)/shard_map/ppermute | solution.py:416
  96.2 10.5 %copy-start.18 = (bf16[1024,2048]{1,0:T(8,128)(2,1)S(1)}, bf16[1024,2048]{1,0:T(8,128)(2,1)}, u32[]{:S(2)}) copy-start(bf16[1024,2048]{1,0:T(8,128)(2,1)} %get-tuple-element.92.hid_far) | copy-start | bytes 12582916
  96.2 10.5 %copy-start.19 = (bf16[1024,2048]{1,0:T(8,128)(2,1)S(1)}, bf16[1024,2048]{1,0:T(8,128)(2,1)}, u32[]{:S(2)}) copy-start(bf16[1024,2048]{1,0:T(8,128)(2,1)} %get-tuple-element.93.slope_far) | copy-start | bytes 12582916
  96.2 10.5 %copy-start.20 = (bf16[1024,512]{1,0:T(8,128)(2,1)S(1)}, bf16[1024,512]{1,0:T(8,128)(2,1)}, u32[]{:S(2)}) copy-start(bf16[1024,512]{1,0:T(8,128)(2,1)} %get-tuple-element.91.nrm_far) | copy-start | bytes 3145732
  115.7 6.2 %collective-permute-start.12 = (bf16[16,5120]{1,0:T(8,128)(2,1)S(1)}, bf16[16,5120]{1,0:T(8,128)(2,1)S(1)}, u32[]{:S(2)}, u32[]{:S(2)}) collective-permute-start(bf16[16,5120]{1,0:T(8,128)(2,1)S(1)} %select_convert_fusion), channel_id=1, source_target_pairs={{0,2},{2,0},{4,6},{6,4},{8,10},{10,8},{12,14},{14,12},{16,18},{18,... | collective-permute-start | bytes 491528 | tf_op jit(solution)/shard_map/ppermute | solution.py:437
  121.9 4.5 %collective-permute-start.13 = (bf16[16,5120]{1,0:T(8,128)(2,1)S(1)}, bf16[16,5120]{1,0:T(8,128)(2,1)S(1)}, u32[]{:S(2)}, u32[]{:S(2)}) collective-permute-start(bf16[16,5120]{1,0:T(8,128)(2,1)S(1)} %add_convert_fusion.6), channel_id=1, source_target_pairs={{0,32},{1,33},{2,6},{3,7},{4,36},{5,37},{6,2},{7,3},{8,40},{9,41},... | collective-permute-start | bytes 491528 | tf_op jit(solution)/shard_map/ppermute | solution.py:440
  126.5 6.0 %collective-permute-start.14 = (bf16[16,5120]{1,0:T(8,128)(2,1)S(1)}, bf16[16,5120]{1,0:T(8,128)(2,1)S(1)}, u32[]{:S(2)}, u32[]{:S(2)}) collective-permute-start(bf16[16,5120]{1,0:T(8,128)(2,1)S(1)} %add_convert_fusion.5), channel_id=1, source_target_pairs={{0,64},{1,65},{2,10},{3,11},{4,68},{5,69},{6,14},{7,15},{8,72},{9,... | collective-permute-start | bytes 491528 | tf_op jit(solution)/shard_map/ppermute | solution.py:440
  132.6 4.2 %collective-permute-start.15 = (bf16[16,5120]{1,0:T(8,128)(2,1)S(1)}, bf16[16,5120]{1,0:T(8,128)(2,1)S(1)}, u32[]{:S(2)}, u32[]{:S(2)}) collective-permute-start(bf16[16,5120]{1,0:T(8,128)(2,1)S(1)} %add_convert_fusion.4), channel_id=1, source_target_pairs={{0,4},{1,5},{2,3},{3,2},{4,0},{5,1},{6,7},{7,6},{8,12},{9,13},{10,... | collective-permute-start | bytes 491528 | tf_op jit(solution)/shard_map/ppermute | solution.py:440
  136.9 5.8 %collective-permute-start.16 = (bf16[16,5120]{1,0:T(8,128)(2,1)S(1)}, bf16[16,5120]{1,0:T(8,128)(2,1)S(1)}, u32[]{:S(2)}, u32[]{:S(2)}) collective-permute-start(bf16[16,5120]{1,0:T(8,128)(2,1)S(1)} %add_convert_fusion.3), channel_id=1, source_target_pairs={{0,8},{1,9},{2,18},{3,19},{4,12},{5,13},{6,22},{7,23},{8,0},{9,1},... | collective-permute-start | bytes 491528 | tf_op jit(solution)/shard_map/ppermute | solution.py:440
  142.7 4.2 %collective-permute-start.17 = (bf16[16,5120]{1,0:T(8,128)(2,1)S(1)}, bf16[16,5120]{1,0:T(8,128)(2,1)S(1)}, u32[]{:S(2)}, u32[]{:S(2)}) collective-permute-start(bf16[16,5120]{1,0:T(8,128)(2,1)S(1)} %add_convert_fusion.2), channel_id=1, source_target_pairs={{0,1},{1,0},{2,34},{3,35},{4,5},{5,4},{6,38},{7,39},{8,9},{9,8},{1... | collective-permute-start | bytes 491528 | tf_op jit(solution)/shard_map/ppermute | solution.py:440
  147.0 5.8 %collective-permute-start.18 = (bf16[16,5120]{1,0:T(8,128)(2,1)S(1)}, bf16[16,5120]{1,0:T(8,128)(2,1)S(1)}, u32[]{:S(2)}, u32[]{:S(2)}) collective-permute-start(bf16[16,5120]{1,0:T(8,128)(2,1)S(1)} %add_convert_fusion.1), channel_id=1, source_target_pairs={{0,16},{1,17},{2,66},{3,67},{4,20},{5,21},{6,70},{7,71},{8,24},{9,... | collective-permute-start | bytes 491528 | tf_op jit(solution)/shard_map/ppermute | solution.py:440
  152.8 7.8 %collective-permute-start.19 = (bf16[16,5120]{1,0:T(8,128)(2,1)S(1)}, bf16[16,5120]{1,0:T(8,128)(2,1)S(1)}, u32[]{:S(2)}, u32[]{:S(2)}) collective-permute-start(bf16[16,5120]{1,0:T(8,128)(2,1)S(1)} %add_convert_fusion), channel_id=1, source_target_pairs={{0,2},{2,0},{4,6},{6,4},{8,10},{10,8},{12,14},{14,12},{16,18},{18,... | collective-permute-start | bytes 491528 | tf_op jit(solution)/shard_map/ppermute | solution.py:442
  (9 other events, 17.3 us)

commit v6 on v5

--- a/solution.py
+++ b/solution.py
@@ -14,7 +14,6 @@
 HALF = COLS // 2
 SPAN = 32
 OFFSET = 5
-WIDE = HALF + 6
 TROWS = 8
 TILE = TROWS * COLS
 CHUNK = 2048
@@ -52,38 +51,42 @@
 
 
 def conv_kernel(sources, flip, flags, *refs):
-    xrefs, (n, s, taps, cv, held, spans, lines) = refs[: len(sources)], refs[len(sources) :]
+    xrefs, (n, s, taps, cv, xs) = refs[: len(sources)], refs[len(sources) :]
     step = pl.program_id(0)
-    zero = jnp.zeros((8, 128), f32)
-    left = lax.broadcasted_iota(jnp.int32, (8, 128), 0) < GROUPS
-
-    def take(row):
-        spread(spans, 0, held[row].astype(f32))
-        base = pl.multiple_of(row * (WIDE * 8), WIDE * 8)
-        for k in range(WIDE):
-            reg = spans[(OFFSET + k) * 8 : (OFFSET + k) * 8 + 8, :]
-            if k < 3:
-                reg = jnp.where(left, zero, reg)
-            if k >= HALF + 3:
-                reg = jnp.where(left, reg, zero)
-            lines[pl.ds(base + k * 8, 8), :] = reg
 
     @pl.when(step == 0)
     def _():
+        zero = jnp.zeros((8, 128), f32)
         for ref, pieces in zip(xrefs, sources):
             for at, row, count in pieces:
-                held[row + 3 : row + 3 + count] = ref[at : at + count]
-        held[0:3] = (n[...].astype(f32) * flags[0]).astype(bf16)
-        held[ROWS + 3 : ROWS + 6] = (s[...].astype(f32) * flags[1]).astype(bf16)
-        held[ROWS + 6 :] = jnp.zeros((2, COLS, CHANS), bf16)
-        lax.fori_loop(0, 38, lambda r, c: (take(r), c)[1], 0)
+
+                def centre(i, c, ref=ref, at=at, row=row):
+                    spread(xs, row + 3 + i, ref[at + i].astype(f32))
+                    return c
+
+                lax.fori_loop(0, count, centre, 0, unroll=4)
+        for i in range(3):
+            spread(xs, i, n[i].astype(f32) * flags[0])
+            spread(xs, ROWS + 3 + i, s[i].astype(f32) * flags[1])
+        left = lax.broadcasted_iota(jnp.int32, (8, 128), 0) < GROUPS
+
+        def edge(r, c):
+            for k in (5, 6, 7):
+                at = pl.ds(pl.multiple_of((r * SPAN + k) * 8, 8), 8)
+                xs[at, :] = jnp.where(left, zero, xs[at, :])
+            for k in (24, 25, 26):
+                at = pl.ds(pl.multiple_of((r * SPAN + k) * 8, 8), 8)
+                xs[at, :] = jnp.where(left, xs[at, :], zero)
+            return c
+
+        lax.fori_loop(0, ROWS + 6, edge, 0, unroll=2)
 
     def row(i, c):
-        at = step * TROWS + i
-        totals = [zero] * HALF
+        first = jnp.zeros((8, 128), f32)
+        totals = [first] * HALF
         for a in range(7):
-            base = pl.multiple_of((at + a) * (WIDE * 8), WIDE * 8)
-            line = [lines[pl.ds(base + k * 8, 8), :] for k in range(WIDE)]
+            base = pl.multiple_of((step * TROWS + i + a) * (SPAN * 8), SPAN * 8)
+            line = [xs[pl.ds(base + (OFFSET + k) * 8, 8), :] for k in range(HALF + 6)]
             for b in range(7):
                 tap = taps[48 - (a * 7 + b) if flip else a * 7 + b]
                 for k in range(HALF):
@@ -401,9 +404,7 @@
         + [(taps, layer(l, 49, 8, 128))],
         [((PIXELS * 4, 128), f32, tiled(lambda t: t, TILE * 4, 128))],
         [
-            pltpu.VMEM((40, COLS, CHANS), bf16),
-            pltpu.VMEM((SPAN * 8, 128), f32),
-            pltpu.VMEM((40 * WIDE * 8, 128), f32),
+            pltpu.VMEM((40 * SPAN * 8, 128), f32),
         ],
         limit=12,
     )[0]
@@ -510,7 +511,7 @@
             ((2, 49, 8, 128), f32, fixed(2, 49, 8, 128)),
         ],
         [],
-        limit=12,
+        limit=60,
     )
     west, east, win, wout = lax.optimization_barrier((west, east, win, wout))
     west, east = strips([west, east], north, south)

time: 163 us -> 159 us (0.975)
  local copies, waits for them, and re-layouts: 10.9 us -> 3.25 us
  Pallas kernels: 81.1 us -> 84.8 us
    unnamed x42 -> x36, local copies, waits for them, and re-layouts: 9.9 us -> 2.29 us
    pallas_call x13, Pallas kernels: 81.1 us -> 84.8 us  [call(): pl.pallas_call(kernel, grid=grid if isinstance(grid, tuple) else (grid,),...]
  transfers between devices with their start and end apart: 20 -> 20, of which waited for: 8 -> 8; matrix products, arithmetic and copies ran while one was open for 0% -> 0% of each run, Pallas kernels for 33% -> 36%
where the time goes in v6:
time: 159 us
  Pallas kernels  84.8 us (53%)
  starting transfers between devices  38.2 us (24%)
  waiting for transfers between devices  29 us (18%)
  local copies, waits for them, and re-layouts  3.25 us (2%)
  other arithmetic  2.39 us (2%)
    pallas_call x13, Pallas kernels, call(): pl.pallas_call(kernel, grid=grid if isinstance(grid, tuple) else (grid,),...  84.8 us
    ppermute x6, waiting for transfers between devices, total(): other = lax.ppermute(part, ('row', 'col', 'rep'), pairs)  26.9 us
    ppermute x12, starting transfers between devices, swap(): return (lax.ppermute(v[1], axis, after), lax.ppermute(v[0], axis, before))  22.7 us
    ppermute x1, starting transfers between devices, total(): back = lax.ppermute(part, 'col', pair)  6.75 us
    ppermute x1, starting transfers between devices, total(): part = (mine + lax.ppermute(other, 'col', pair).astype(f32)).astype(bf16)  5.14 us
    ppermute x6, starting transfers between devices, total(): other = lax.ppermute(part, ('row', 'col', 'rep'), pairs)  3.67 us
  transfers between devices with their start and end apart: 20, of which 8 were waited for; matrix products, arithmetic and copies ran while one was open for 0% of the time, Pallas kernels for 36%

profile of v6, /device:TPU:1, one launch (start us, length us, event | category | flops | bytes accessed | tf_op | source)
XLA Modules:
  0.0 158.7 jit_solution(14884292654726402627)
XLA Ops:
  0.6 1.0 slice_bitcast_fusion
  1.6 3.6 %collective-permute-start.1 = (bf16[3,32,512]{2,1,0:T(8,128)(2,1)S(1)}, bf16[3,32,512]{2,1,0:T(8,128)(2,1)S(1)}, u32[]{:S(2)}, u32[]{:S(2)}) collective-permute-start(bf16[3,32,512]{2,1,0:T(8,128)(2,1)S(1)} %get-tuple-element.101), channel_id=1, source_target_pairs={{32,0},{64,32},{96,64},{0,96},{33,1},{65,33},{97,65},{1,97},{34,2}... | collective-permute-start | bytes 294920 | tf_op jit(solution)/shard_map/ppermute | solution.py:417
  5.2 1.2 copy-done
  6.6 10.7 %fold.1 = (bf16[2,512,2048]{2,1,0:T(8,128)(2,1)}, bf16[2,2048,512]{2,1,0:T(8,128)(2,1)}, f32[2,49,8,128]{3,2,1,0:T(8,128)}) custom-call(bf16[2,512,2048]{2,1,0:T(8,128)(2,1)} %win.1, bf16[2,16,512]{2,1,0:T(8,128)(2,1)} %bitcast.37, bf16[2,16,2048]{2,1,0:T(8,128)(2,1)} %bin_.7, bf16[2,2048,512]{2,1,0:T(8,128)(2,1)} %wout.1, bf16[2,16,2048]{2,1,0:T(8,128)(2,1)} %bitcast.32, ...), custom_call_target="tpu_custom_call" | custom-call | flops 5000000000 | bytes 1000000 | tf_op jit(solution)/shard_map/fold/pallas_call | solution.py:379
  17.5 2.5 %collective-permute-start.2 = (bf16[3,48,512]{2,1,0:T(8,128)(2,1)S(1)}, bf16[3,48,512]{2,1,0:T(8,128)(2,1)S(1)}, u32[]{:S(2)}, u32[]{:S(2)}) collective-permute-start(bf16[3,48,512]{2,1,0:T(8,128)(2,1)S(1)} %get-tuple-element.57), channel_id=1, source_target_pairs={{0,2},{2,4},{4,6},{6,8},{8,10},{10,12},{12,14},{14,16},{16,18},{18... | collective-permute-start | bytes 442376 | tf_op jit(solution)/shard_map/ppermute | solution.py:417
  20.0 1.0 copy-done.16
  21.1 9.2 %conv.3.cv = f32[4096,128]{1,0:T(8,128)S(1)} custom-call(f32[4]{0:T(128)S(1)} %add_convert_fusion.7.flags, bf16[32,32,512]{2,1,0:T(8,128)(2,1)S(1)} %bitcast.26, bf16[3,32,512]{2,1,0:T(8,128)(2,1)S(1)} %collective-permute-done.refs_1_.refs_2_, bf16[3,32,512]{2,1,0:T(8,128)(2,1)S(1)} %collective-permute-done.1.refs_2_.refs_3_, f32[2,49,8,128]{3,2,1,0:T(8,128)S(1)} %copy-done.16), custom_call_target="tpu_custom_call" | custom-call | flops 8000000000 | bytes 1000000 | tf_op jit(solution)/shard_map/conv/pallas_call | solution.py:379
  30.4 7.8 %first_outer.1 = (bf16[1024,512]{1,0:T(8,128)(2,1)}, bf16[1024,2048]{1,0:T(8,128)(2,1)}, bf16[1024,2048]{1,0:T(8,128)(2,1)}, bf16[1024,16]{1,0:T(8,128)(2,1)S(1)...) custom-call(f32[4]{0:T(128)S(1)} %add_convert_fusion.7.flags, ...), custom_call_target="tpu_custom_call" | custom-call | flops 7000000000 | bytes 1000000 | tf_op jit(solution)/shard_map/first_outer/pallas_call | solution.py:379
  38.5 2.6 %collective-permute-start.5 = (bf16[3,32,512]{2,1,0:T(8,128)(2,1)S(1)}, bf16[3,32,512]{2,1,0:T(8,128)(2,1)S(1)}, u32[]{:S(2)}, u32[]{:S(2)}) collective-permute-start(bf16[3,32,512]{2,1,0:T(8,128)(2,1)S(1)} %get-tuple-element.69), channel_id=1, source_target_pairs={{32,0},{64,32},{96,64},{0,96},{33,1},{65,33},{97,65},{1,97},{34,2}... | collective-permute-start | bytes 294920 | tf_op jit(solution)/shard_map/ppermute | solution.py:417
  41.2 7.3 %first_inner.1 = (bf16[1024,512]{1,0:T(8,128)(2,1)}, bf16[1024,2048]{1,0:T(8,128)(2,1)}, bf16[1024,2048]{1,0:T(8,128)(2,1)}, bf16[1024,16]{1,0:T(8,128)(2,1)S(1)...) custom-call(f32[4]{0:T(128)S(1)} %add_convert_fusion.7.flags, ...), custom_call_target="tpu_custom_call", output_to_operand_aliasing={{0}: (14, {}), {1}: (15, {}), {2}: (16, {}), {3}: (17, {}),... | custom-call | flops 7000000000 | bytes 1000000 | tf_op jit(solution)/shard_map/first_inner/pallas_call | solution.py:379
  48.6 2.1 %collective-permute-start.6 = (bf16[3,48,512]{2,1,0:T(8,128)(2,1)S(1)}, bf16[3,48,512]{2,1,0:T(8,128)(2,1)S(1)}, u32[]{:S(2)}, u32[]{:S(2)}) collective-permute-start(bf16[3,48,512]{2,1,0:T(8,128)(2,1)S(1)} %get-tuple-element.74), channel_id=1, source_target_pairs={{0,2},{2,4},{4,6},{6,8},{8,10},{10,12},{12,14},{14,16},{16,18},{18... | collective-permute-start | bytes 442376 | tf_op jit(solution)/shard_map/ppermute | solution.py:417
  50.7 2.7 %collective-permute-start.7 = (bf16[3,48,512]{2,1,0:T(8,128)(2,1)S(1)}, bf16[3,48,512]{2,1,0:T(8,128)(2,1)S(1)}, u32[]{:S(2)}, u32[]{:S(2)}) collective-permute-start(bf16[3,48,512]{2,1,0:T(8,128)(2,1)S(1)} %get-tuple-element.75), channel_id=1, source_target_pairs={{2,0},{4,2},{6,4},{8,6},{10,8},{12,10},{14,12},{16,14},{18,16},{20... | collective-permute-start | bytes 442376 | tf_op jit(solution)/shard_map/ppermute | solution.py:417
  53.4 9.9 %conv.4.cv = f32[4096,128]{1,0:T(8,128)S(1)} custom-call(f32[4]{0:T(128)S(1)} %add_convert_fusion.7.flags, bf16[16,32,512]{2,1,0:T(8,128)(2,1)S(1)} %get-tuple-element.67.refs_0_.x, bf16[16,32,512]{2,1,0:T(8,128)(2,1)S(1)} %get-tuple-element.66.refs_1_.x, bf16[3,32,512]{2,1,0:T(8,128)(2,1)S(1)} %collective-permute-done.4.refs_2_.refs_4_, ...), custom_call_target="tpu_custom_call" | custom-call | flops 8000000000 | bytes 1000000 | tf_op jit(solution)/shard_map/conv/pallas_call | solution.py:379
  63.3 10.5 %second_outer.1 = (bf16[32,32,512]{2,1,0:T(8,128)(2,1)}, f32[16,5120]{1,0:T(8,128)S(1)}, bf16[16,32,512]{2,1,0:T(8,128)(2,1)S(1)}, bf16[3,32,512]{2,1,0:T(8,128)...) custom-call(f32[4]{0:T(128)S(1)} %add_convert_fusion.7.flags, ...), custom_call_target="tpu_custom_call" | custom-call | flops 10000000000 | bytes 1000000 | tf_op jit(solution)/shard_map/second_outer/pallas_call | solution.py:379
  73.8 2.7 %collective-permute-start.9 = (bf16[3,32,512]{2,1,0:T(8,128)(2,1)S(1)}, bf16[3,32,512]{2,1,0:T(8,128)(2,1)S(1)}, u32[]{:S(2)}, u32[]{:S(2)}) collective-permute-start(bf16[3,32,512]{2,1,0:T(8,128)(2,1)S(1)} %get-tuple-element.82), channel_id=1, source_target_pairs={{32,0},{64,32},{96,64},{0,96},{33,1},{65,33},{97,65},{1,97},{34,2}... | collective-permute-start | bytes 294920 | tf_op jit(solution)/shard_map/ppermute | solution.py:417
  76.5 10.2 %second_inner.1 = (bf16[32,32,512]{2,1,0:T(8,128)(2,1)}, f32[16,5120]{1,0:T(8,128)S(1)}, bf16[16,32,512]{2,1,0:T(8,128)(2,1)S(1)}, bf16[3,16,512]{2,1,0:T(8,128)(2,1)S(1)}, bf16[3,16,512]{2,1,0:T(8,128)(2,1)S(1)}) custom-call(f32[4]{0:T(128)S(1)} %add_convert_fusion.7.flags, ...), custom_call_target="tpu_custom_call", output_to_operand_aliasing={{0}: (17, {})} | custom-call | flops 10000000000 | bytes 1000000 | tf_op jit(solution)/shard_map/second_inner/pallas_call | solution.py:379
  86.9 6.0 %collective-permute-start.11 = (bf16[3,48,512]{2,1,0:T(8,128)(2,1)S(1)}, bf16[3,48,512]{2,1,0:T(8,128)(2,1)S(1)}, u32[]{:S(2)}, u32[]{:S(2)}) collective-permute-start(bf16[3,48,512]{2,1,0:T(8,128)(2,1)S(1)} %get-tuple-element.88), channel_id=1, source_target_pairs={{2,0},{4,2},{6,4},{8,6},{10,8},{12,10},{14,12},{16,14},{18,16},{20... | collective-permute-start | bytes 442376 | tf_op jit(solution)/shard_map/ppermute | solution.py:417
  92.8 9.9 %conv.5.cv = f32[4096,128]{1,0:T(8,128)S(1)} custom-call(f32[4]{0:T(128)S(1)} %add_convert_fusion.7.flags, bf16[16,32,512]{2,1,0:T(8,128)(2,1)S(1)} %get-tuple-element.79.refs_0_, bf16[16,32,512]{2,1,0:T(8,128)(2,1)S(1)} %get-tuple-element.80.refs_1_, bf16[3,32,512]{2,1,0:T(8,128)(2,1)S(1)} %collective-permute-done.8.refs_2_.refs_4_, ...), custom_call_target="tpu_custom_call" | custom-call | flops 8000000000 | bytes 1000000 | tf_op jit(solution)/shard_map/conv/pallas_call | solution.py:379
  102.8 9.0 %third.1 = f32[16,5120]{1,0:T(8,128)S(1)} custom-call(f32[4]{0:T(128)S(1)} %add_convert_fusion.7.flags, bf16[32,32,512]{2,1,0:T(8,128)(2,1)S(1)} %bitcast.31, f32[4096,128]{1,0:T(8,128)S(1)} %conv.5.cv, bf16[3,48,512]{2,1,0:T(8,128)(2,1)S(1)} %collective-permute-done.10.w, bf16[3,48,512]{2,1,0:T(8,128)(2,1)S(1)} %collective-permute-done.11.e, ...), custom_call_target="tpu_custom_call" | custom-call | flops 8999999488 | bytes 1000000 | tf_op jit(solution)/shard_map/third/pallas_call | solution.py:379
  111.9 5.1 %collective-permute-start.12 = (bf16[16,5120]{1,0:T(8,128)(2,1)S(1)}, bf16[16,5120]{1,0:T(8,128)(2,1)S(1)}, u32[]{:S(2)}, u32[]{:S(2)}) collective-permute-start(bf16[16,5120]{1,0:T(8,128)(2,1)S(1)} %select_convert_fusion), channel_id=1, source_target_pairs={{0,2},{2,0},{4,6},{6,4},{8,10},{10,8},{12,14},{14,12},{16,18},{18,... | collective-permute-start | bytes 491528 | tf_op jit(solution)/shard_map/ppermute | solution.py:438
  117.0 1.0 collective-permute-done.12
  118.2 4.5 %collective-permute-done.13 = bf16[16,5120]{1,0:T(8,128)(2,1)S(1)} collective-permute-done((bf16[16,5120]{1,0:T(8,128)(2,1)S(1)}, bf16[16,5120]{1,0:T(8,128)(2,1)S(1)}, u32[]{:S(2)}, u32[]{:S(2)}) %collective-permute-start.13) | collective-permute-done | bytes 163872 | tf_op jit(solution)/shard_map/ppermute | solution.py:441
  122.8 6.0 %collective-permute-done.14 = bf16[16,5120]{1,0:T(8,128)(2,1)S(1)} collective-permute-done((bf16[16,5120]{1,0:T(8,128)(2,1)S(1)}, bf16[16,5120]{1,0:T(8,128)(2,1)S(1)}, u32[]{:S(2)}, u32[]{:S(2)}) %collective-permute-start.14) | collective-permute-done | bytes 163872 | tf_op jit(solution)/shard_map/ppermute | solution.py:441
  128.8 0.9 collective-permute-start.15
  129.7 3.3 %collective-permute-done.15 = bf16[16,5120]{1,0:T(8,128)(2,1)S(1)} collective-permute-done((bf16[16,5120]{1,0:T(8,128)(2,1)S(1)}, bf16[16,5120]{1,0:T(8,128)(2,1)S(1)}, u32[]{:S(2)}, u32[]{:S(2)}) %collective-permute-start.15) | collective-permute-done | bytes 163872 | tf_op jit(solution)/shard_map/ppermute | solution.py:441
  133.1 2.4 %collective-permute-start.16 = (bf16[16,5120]{1,0:T(8,128)(2,1)S(1)}, bf16[16,5120]{1,0:T(8,128)(2,1)S(1)}, u32[]{:S(2)}, u32[]{:S(2)}) collective-permute-start(bf16[16,5120]{1,0:T(8,128)(2,1)S(1)} %add_convert_fusion.3), channel_id=1, source_target_pairs={{0,8},{1,9},{2,18},{3,19},{4,12},{5,13},{6,22},{7,23},{8,0},{9,1},... | collective-permute-start | bytes 491528 | tf_op jit(solution)/shard_map/ppermute | solution.py:441
  135.5 3.3 %collective-permute-done.16 = bf16[16,5120]{1,0:T(8,128)(2,1)S(1)} collective-permute-done((bf16[16,5120]{1,0:T(8,128)(2,1)S(1)}, bf16[16,5120]{1,0:T(8,128)(2,1)S(1)}, u32[]{:S(2)}, u32[]{:S(2)}) %collective-permute-start.16) | collective-permute-done | bytes 163872 | tf_op jit(solution)/shard_map/ppermute | solution.py:441
  138.9 4.2 %collective-permute-done.17 = bf16[16,5120]{1,0:T(8,128)(2,1)S(1)} collective-permute-done((bf16[16,5120]{1,0:T(8,128)(2,1)S(1)}, bf16[16,5120]{1,0:T(8,128)(2,1)S(1)}, u32[]{:S(2)}, u32[]{:S(2)}) %collective-permute-start.17) | collective-permute-done | bytes 163872 | tf_op jit(solution)/shard_map/ppermute | solution.py:441
  143.2 5.7 %collective-permute-done.18 = bf16[16,5120]{1,0:T(8,128)(2,1)S(1)} collective-permute-done((bf16[16,5120]{1,0:T(8,128)(2,1)S(1)}, bf16[16,5120]{1,0:T(8,128)(2,1)S(1)}, u32[]{:S(2)}, u32[]{:S(2)}) %collective-permute-start.18) | collective-permute-done | bytes 163872 | tf_op jit(solution)/shard_map/ppermute | solution.py:441
  148.9 6.8 %collective-permute-start.19 = (bf16[16,5120]{1,0:T(8,128)(2,1)S(1)}, bf16[16,5120]{1,0:T(8,128)(2,1)S(1)}, u32[]{:S(2)}, u32[]{:S(2)}) collective-permute-start(bf16[16,5120]{1,0:T(8,128)(2,1)S(1)} %add_convert_fusion), channel_id=1, source_target_pairs={{0,2},{2,0},{4,6},{6,4},{8,10},{10,8},{12,14},{14,12},{16,18},{18,... | collective-permute-start | bytes 491528 | tf_op jit(solution)/shard_map/ppermute | solution.py:443
  155.7 1.0 collective-permute-done.19
  157.1 0.9 multiply_bitcast_fusion
  (76 shorter events, 2.6 us)
Async XLA Ops:
  1.6 15.8 %collective-permute-start.1 = (bf16[3,32,512]{2,1,0:T(8,128)(2,1)S(1)}, bf16[3,32,512]{2,1,0:T(8,128)(2,1)S(1)}, u32[]{:S(2)}, u32[]{:S(2)}) collective-permute-start(bf16[3,32,512]{2,1,0:T(8,128)(2,1)S(1)} %get-tuple-element.101), channel_id=1, source_target_pairs={{32,0},{64,32},{96,64},{0,96},{33,1},{65,33},{97,65},{1,97},{34,2}... | collective-permute-start | bytes 294920 | tf_op jit(solution)/shard_map/ppermute | solution.py:417
  5.2 12.2 %collective-permute-start = (bf16[3,32,512]{2,1,0:T(8,128)(2,1)S(1)}, bf16[3,32,512]{2,1,0:T(8,128)(2,1)S(1)}, u32[]{:S(2)}, u32[]{:S(2)}) collective-permute-start(bf16[3,32,512]{2,1,0:T(8,128)(2,1)S(1)} %get-tuple-element.102), channel_id=1, source_target_pairs={{0,32},{32,64},{64,96},{96,0},{1,33},{33,65},{65,97},{97,1},{2,34}... | collective-permute-start | bytes 294920 | tf_op jit(solution)/shard_map/ppermute | solution.py:417
  6.6 13.4 %copy-start.1 = (bf16[1,32,32,512]{3,2,1,0:T(8,128)(2,1)S(1)}, bf16[1,32,32,512]{3,2,1,0:T(8,128)(2,1)}, u32[]{:S(2)}) copy-start(bf16[1,32,32,512]{3,2,1,0:T(8,128)(2,1)} %param.13) | copy-start | bytes 3145732
  17.5 12.8 %collective-permute-start.2 = (bf16[3,48,512]{2,1,0:T(8,128)(2,1)S(1)}, bf16[3,48,512]{2,1,0:T(8,128)(2,1)S(1)}, u32[]{:S(2)}, u32[]{:S(2)}) collective-permute-start(bf16[3,48,512]{2,1,0:T(8,128)(2,1)S(1)} %get-tuple-element.57), channel_id=1, source_target_pairs={{0,2},{2,4},{4,6},{6,8},{8,10},{10,12},{12,14},{14,16},{16,18},{18... | collective-permute-start | bytes 442376 | tf_op jit(solution)/shard_map/ppermute | solution.py:417
  20.0 10.2 %collective-permute-start.3 = (bf16[3,48,512]{2,1,0:T(8,128)(2,1)S(1)}, bf16[3,48,512]{2,1,0:T(8,128)(2,1)S(1)}, u32[]{:S(2)}, u32[]{:S(2)}) collective-permute-start(bf16[3,48,512]{2,1,0:T(8,128)(2,1)S(1)} %get-tuple-element.58), channel_id=1, source_target_pairs={{2,0},{4,2},{6,4},{8,6},{10,8},{12,10},{14,12},{16,14},{18,16},{20... | collective-permute-start | bytes 442376 | tf_op jit(solution)/shard_map/ppermute | solution.py:417
  21.0 9.3 %copy-start.9 = (f32[2,512]{1,0:T(2,128)S(1)}, f32[2,512]{1,0:T(2,128)}, u32[]{:S(2)}) copy-start(f32[2,512]{1,0:T(2,128)} %shift.7) | copy-start | bytes 12292
  21.1 9.3 %copy-start.10 = (f32[2,512]{1,0:T(2,128)S(1)}, f32[2,512]{1,0:T(2,128)}, u32[]{:S(2)}) copy-start(f32[2,512]{1,0:T(2,128)} %scale.9) | copy-start | bytes 12292
  21.1 9.3 %copy-start.11 = (bf16[2,2048,512]{2,1,0:T(8,128)(2,1)S(1)}, bf16[2,2048,512]{2,1,0:T(8,128)(2,1)}, u32[]{:S(2)}) copy-start(bf16[2,2048,512]{2,1,0:T(8,128)(2,1)} %get-tuple-element.60.wout) | copy-start | bytes 12582916
  21.1 9.3 %copy-start.12 = (bf16[2,512,2048]{2,1,0:T(8,128)(2,1)S(1)}, bf16[2,512,2048]{2,1,0:T(8,128)(2,1)}, u32[]{:S(2)}) copy-start(bf16[2,512,2048]{2,1,0:T(8,128)(2,1)} %get-tuple-element.59.win) | copy-start | bytes 12582916
  21.1 9.3 %copy-start.17 = (f32[2,49,8,128]{3,2,1,0:T(8,128)S(1)}, f32[2,49,8,128]{3,2,1,0:T(8,128)}, u32[]{:S(2)}) copy-start(f32[2,49,8,128]{3,2,1,0:T(8,128)} %get-tuple-element.50.refs_3_.taps.refs_4_) | copy-start | bytes 1204228
  38.2 10.3 %collective-permute-start.4 = (bf16[3,32,512]{2,1,0:T(8,128)(2,1)S(1)}, bf16[3,32,512]{2,1,0:T(8,128)(2,1)S(1)}, u32[]{:S(2)}, u32[]{:S(2)}) collective-permute-start(bf16[3,32,512]{2,1,0:T(8,128)(2,1)S(1)} %get-tuple-element.68), channel_id=1, source_target_pairs={{0,32},{32,64},{64,96},{96,0},{1,33},{33,65},{65,97},{97,1},{2,34}... | collective-permute-start | bytes 294920 | tf_op jit(solution)/shard_map/ppermute | solution.py:417
  38.5 10.0 %collective-permute-start.5 = (bf16[3,32,512]{2,1,0:T(8,128)(2,1)S(1)}, bf16[3,32,512]{2,1,0:T(8,128)(2,1)S(1)}, u32[]{:S(2)}, u32[]{:S(2)}) collective-permute-start(bf16[3,32,512]{2,1,0:T(8,128)(2,1)S(1)} %get-tuple-element.69), channel_id=1, source_target_pairs={{32,0},{64,32},{96,64},{0,96},{33,1},{65,33},{97,65},{1,97},{34,2}... | collective-permute-start | bytes 294920 | tf_op jit(solution)/shard_map/ppermute | solution.py:417
  48.6 14.7 %collective-permute-start.6 = (bf16[3,48,512]{2,1,0:T(8,128)(2,1)S(1)}, bf16[3,48,512]{2,1,0:T(8,128)(2,1)S(1)}, u32[]{:S(2)}, u32[]{:S(2)}) collective-permute-start(bf16[3,48,512]{2,1,0:T(8,128)(2,1)S(1)} %get-tuple-element.74), channel_id=1, source_target_pairs={{0,2},{2,4},{4,6},{6,8},{8,10},{10,12},{12,14},{14,16},{16,18},{18... | collective-permute-start | bytes 442376 | tf_op jit(solution)/shard_map/ppermute | solution.py:417
  50.7 12.6 %collective-permute-start.7 = (bf16[3,48,512]{2,1,0:T(8,128)(2,1)S(1)}, bf16[3,48,512]{2,1,0:T(8,128)(2,1)S(1)}, u32[]{:S(2)}, u32[]{:S(2)}) collective-permute-start(bf16[3,48,512]{2,1,0:T(8,128)(2,1)S(1)} %get-tuple-element.75), channel_id=1, source_target_pairs={{2,0},{4,2},{6,4},{8,6},{10,8},{12,10},{14,12},{16,14},{18,16},{20... | collective-permute-start | bytes 442376 | tf_op jit(solution)/shard_map/ppermute | solution.py:417
  53.4 9.9 %copy-start.2 = (bf16[1,32,32,512]{3,2,1,0:T(8,128)(2,1)S(1)}, bf16[1,32,32,512]{3,2,1,0:T(8,128)(2,1)}, u32[]{:S(2)}) copy-start(bf16[1,32,32,512]{3,2,1,0:T(8,128)(2,1)} %param.14) | copy-start | bytes 3145732
  53.4 9.9 %copy-start.4 = (bf16[2,16,2048]{2,1,0:T(8,128)(2,1)S(1)}, bf16[2,16,2048]{2,1,0:T(8,128)(2,1)}, u32[]{:S(2)}) copy-start(bf16[2,16,2048]{2,1,0:T(8,128)(2,1)} %bin_.7) | copy-start | bytes 393220
  53.4 9.9 %copy-start.6 = (bf16[2,16,512]{2,1,0:T(8,128)(2,1)S(1)}, bf16[2,16,512]{2,1,0:T(8,128)(2,1)}, u32[]{:S(2)}) copy-start(bf16[2,16,512]{2,1,0:T(8,128)(2,1)} %bout.7) | copy-start | bytes 98308
  73.8 12.9 %collective-permute-start.8 = (bf16[3,32,512]{2,1,0:T(8,128)(2,1)S(1)}, bf16[3,32,512]{2,1,0:T(8,128)(2,1)S(1)}, u32[]{:S(2)}, u32[]{:S(2)}) collective-permute-start(bf16[3,32,512]{2,1,0:T(8,128)(2,1)S(1)} %get-tuple-element.81), channel_id=1, source_target_pairs={{0,32},{32,64},{64,96},{96,0},{1,33},{33,65},{65,97},{97,1},{2,34}... | collective-permute-start | bytes 294920 | tf_op jit(solution)/shard_map/ppermute | solution.py:417
  73.8 12.9 %collective-permute-start.9 = (bf16[3,32,512]{2,1,0:T(8,128)(2,1)S(1)}, bf16[3,32,512]{2,1,0:T(8,128)(2,1)S(1)}, u32[]{:S(2)}, u32[]{:S(2)}) collective-permute-start(bf16[3,32,512]{2,1,0:T(8,128)(2,1)S(1)} %get-tuple-element.82), channel_id=1, source_target_pairs={{32,0},{64,32},{96,64},{0,96},{33,1},{65,33},{97,65},{1,97},{34,2}... | collective-permute-start | bytes 294920 | tf_op jit(solution)/shard_map/ppermute | solution.py:417
  86.8 16.0 %collective-permute-start.10 = (bf16[3,48,512]{2,1,0:T(8,128)(2,1)S(1)}, bf16[3,48,512]{2,1,0:T(8,128)(2,1)S(1)}, u32[]{:S(2)}, u32[]{:S(2)}) collective-permute-start(bf16[3,48,512]{2,1,0:T(8,128)(2,1)S(1)} %get-tuple-element.87), channel_id=1, source_target_pairs={{0,2},{2,4},{4,6},{6,8},{8,10},{10,12},{12,14},{14,16},{16,18},{18... | collective-permute-start | bytes 442376 | tf_op jit(solution)/shard_map/ppermute | solution.py:417
  86.9 15.9 %collective-permute-start.11 = (bf16[3,48,512]{2,1,0:T(8,128)(2,1)S(1)}, bf16[3,48,512]{2,1,0:T(8,128)(2,1)S(1)}, u32[]{:S(2)}, u32[]{:S(2)}) collective-permute-start(bf16[3,48,512]{2,1,0:T(8,128)(2,1)S(1)} %get-tuple-element.88), channel_id=1, source_target_pairs={{2,0},{4,2},{6,4},{8,6},{10,8},{12,10},{14,12},{16,14},{18,16},{20... | collective-permute-start | bytes 442376 | tf_op jit(solution)/shard_map/ppermute | solution.py:417
  92.8 10.0 %copy-start.13 = (bf16[1024,2048]{1,0:T(8,128)(2,1)S(1)}, bf16[1024,2048]{1,0:T(8,128)(2,1)}, u32[]{:S(2)}) copy-start(bf16[1024,2048]{1,0:T(8,128)(2,1)} %get-tuple-element.92.hid_far) | copy-start | bytes 12582916
  92.8 10.0 %copy-start.14 = (bf16[1024,2048]{1,0:T(8,128)(2,1)S(1)}, bf16[1024,2048]{1,0:T(8,128)(2,1)}, u32[]{:S(2)}) copy-start(bf16[1024,2048]{1,0:T(8,128)(2,1)} %get-tuple-element.93.slope_far) | copy-start | bytes 12582916
  92.8 10.0 %copy-start.15 = (bf16[1024,512]{1,0:T(8,128)(2,1)S(1)}, bf16[1024,512]{1,0:T(8,128)(2,1)}, u32[]{:S(2)}) copy-start(bf16[1024,512]{1,0:T(8,128)(2,1)} %get-tuple-element.91.nrm_far) | copy-start | bytes 3145732
  111.9 6.2 %collective-permute-start.12 = (bf16[16,5120]{1,0:T(8,128)(2,1)S(1)}, bf16[16,5120]{1,0:T(8,128)(2,1)S(1)}, u32[]{:S(2)}, u32[]{:S(2)}) collective-permute-start(bf16[16,5120]{1,0:T(8,128)(2,1)S(1)} %select_convert_fusion), channel_id=1, source_target_pairs={{0,2},{2,0},{4,6},{6,4},{8,10},{10,8},{12,14},{14,12},{16,18},{18,... | collective-permute-start | bytes 491528 | tf_op jit(solution)/shard_map/ppermute | solution.py:438
  118.1 4.5 %collective-permute-start.13 = (bf16[16,5120]{1,0:T(8,128)(2,1)S(1)}, bf16[16,5120]{1,0:T(8,128)(2,1)S(1)}, u32[]{:S(2)}, u32[]{:S(2)}) collective-permute-start(bf16[16,5120]{1,0:T(8,128)(2,1)S(1)} %add_convert_fusion.6), channel_id=1, source_target_pairs={{0,32},{1,33},{2,6},{3,7},{4,36},{5,37},{6,2},{7,3},{8,40},{9,41},... | collective-permute-start | bytes 491528 | tf_op jit(solution)/shard_map/ppermute | solution.py:441
  122.7 6.0 %collective-permute-start.14 = (bf16[16,5120]{1,0:T(8,128)(2,1)S(1)}, bf16[16,5120]{1,0:T(8,128)(2,1)S(1)}, u32[]{:S(2)}, u32[]{:S(2)}) collective-permute-start(bf16[16,5120]{1,0:T(8,128)(2,1)S(1)} %add_convert_fusion.5), channel_id=1, source_target_pairs={{0,64},{1,65},{2,10},{3,11},{4,68},{5,69},{6,14},{7,15},{8,72},{9,... | collective-permute-start | bytes 491528 | tf_op jit(solution)/shard_map/ppermute | solution.py:441
  128.8 4.2 %collective-permute-start.15 = (bf16[16,5120]{1,0:T(8,128)(2,1)S(1)}, bf16[16,5120]{1,0:T(8,128)(2,1)S(1)}, u32[]{:S(2)}, u32[]{:S(2)}) collective-permute-start(bf16[16,5120]{1,0:T(8,128)(2,1)S(1)} %add_convert_fusion.4), channel_id=1, source_target_pairs={{0,4},{1,5},{2,3},{3,2},{4,0},{5,1},{6,7},{7,6},{8,12},{9,13},{10,... | collective-permute-start | bytes 491528 | tf_op jit(solution)/shard_map/ppermute | solution.py:441
  133.1 5.8 %collective-permute-start.16 = (bf16[16,5120]{1,0:T(8,128)(2,1)S(1)}, bf16[16,5120]{1,0:T(8,128)(2,1)S(1)}, u32[]{:S(2)}, u32[]{:S(2)}) collective-permute-start(bf16[16,5120]{1,0:T(8,128)(2,1)S(1)} %add_convert_fusion.3), channel_id=1, source_target_pairs={{0,8},{1,9},{2,18},{3,19},{4,12},{5,13},{6,22},{7,23},{8,0},{9,1},... | collective-permute-start | bytes 491528 | tf_op jit(solution)/shard_map/ppermute | solution.py:441
  138.8 4.2 %collective-permute-start.17 = (bf16[16,5120]{1,0:T(8,128)(2,1)S(1)}, bf16[16,5120]{1,0:T(8,128)(2,1)S(1)}, u32[]{:S(2)}, u32[]{:S(2)}) collective-permute-start(bf16[16,5120]{1,0:T(8,128)(2,1)S(1)} %add_convert_fusion.2), channel_id=1, source_target_pairs={{0,1},{1,0},{2,34},{3,35},{4,5},{5,4},{6,38},{7,39},{8,9},{9,8},{1... | collective-permute-start | bytes 491528 | tf_op jit(solution)/shard_map/ppermute | solution.py:441
  143.1 5.8 %collective-permute-start.18 = (bf16[16,5120]{1,0:T(8,128)(2,1)S(1)}, bf16[16,5120]{1,0:T(8,128)(2,1)S(1)}, u32[]{:S(2)}, u32[]{:S(2)}) collective-permute-start(bf16[16,5120]{1,0:T(8,128)(2,1)S(1)} %add_convert_fusion.1), channel_id=1, source_target_pairs={{0,16},{1,17},{2,66},{3,67},{4,20},{5,21},{6,70},{7,71},{8,24},{9,... | collective-permute-start | bytes 491528 | tf_op jit(solution)/shard_map/ppermute | solution.py:441
  148.9 7.8 %collective-permute-start.19 = (bf16[16,5120]{1,0:T(8,128)(2,1)S(1)}, bf16[16,5120]{1,0:T(8,128)(2,1)S(1)}, u32[]{:S(2)}, u32[]{:S(2)}) collective-permute-start(bf16[16,5120]{1,0:T(8,128)(2,1)S(1)} %add_convert_fusion), channel_id=1, source_target_pairs={{0,2},{2,0},{4,6},{6,4},{8,10},{10,8},{12,14},{14,12},{16,18},{18,... | collective-permute-start | bytes 491528 | tf_op jit(solution)/shard_map/ppermute | solution.py:443
  (6 other events, 39.3 us)

commit v7 on v6

--- a/solution.py
+++ b/solution.py
@@ -563,7 +563,7 @@
         common(0, outer_place, x0, outer_place),
         kept(outer_place) + [half] + row_edges + col_edges,
         [HE, LINE, EDGE],
-        far=(0, 1, 2),
+        far=(1,),
     )
     north, south = swap((top, bottom), "row")
     ins = common(0, inner_place, x0, inner_place)
@@ -575,7 +575,7 @@
         kept(inner_place) + [half] + col_edges,
         [HE, LINE, EDGE],
         {len(ins) + i: i for i in range(5)},
-        far=(0, 1, 2),
+        far=(1,),
     )
     split = [[(0, 0, 8), (8, 24, 8)], [(0, 8, 16)]]
     west, east = strips([west_a, west_b, east_a, east_b], north, south)

time: 159 us -> 158 us (level)
  no operation moved by 1% of the time
where the time goes in v7:
time: 158 us
  Pallas kernels  83.8 us (53%)
  starting transfers between devices  38.2 us (24%)
  waiting for transfers between devices  29 us (18%)
  local copies, waits for them, and re-layouts  3.24 us (2%)
  other arithmetic  2.39 us (2%)
    pallas_call x13, Pallas kernels, call(): pl.pallas_call(kernel, grid=grid if isinstance(grid, tuple) else (grid,),...  83.8 us
    ppermute x6, waiting for transfers between devices, total(): other = lax.ppermute(part, ('row', 'col', 'rep'), pairs)  26.9 us
    ppermute x12, starting transfers between devices, swap(): return (lax.ppermute(v[1], axis, after), lax.ppermute(v[0], axis, before))  22.7 us
    ppermute x1, starting transfers between devices, total(): back = lax.ppermute(part, 'col', pair)  6.75 us
    ppermute x1, starting transfers between devices, total(): part = (mine + lax.ppermute(other, 'col', pair).astype(f32)).astype(bf16)  5.14 us
    ppermute x6, starting transfers between devices, total(): other = lax.ppermute(part, ('row', 'col', 'rep'), pairs)  3.69 us
  transfers between devices with their start and end apart: 20, of which 8 were waited for; matrix products, arithmetic and copies ran while one was open for 0% of the time, Pallas kernels for 36%

profile of v7, /device:TPU:1, one launch (start us, length us, event | category | flops | bytes accessed | tf_op | source)
XLA Modules:
  0.0 157.6 jit_solution(10798846528794490809)
XLA Ops:
  0.6 1.0 slice_bitcast_fusion
  1.6 3.6 %collective-permute-start.1 = (bf16[3,32,512]{2,1,0:T(8,128)(2,1)S(1)}, bf16[3,32,512]{2,1,0:T(8,128)(2,1)S(1)}, u32[]{:S(2)}, u32[]{:S(2)}) collective-permute-start(bf16[3,32,512]{2,1,0:T(8,128)(2,1)S(1)} %get-tuple-element.101), channel_id=1, source_target_pairs={{32,0},{64,32},{96,64},{0,96},{33,1},{65,33},{97,65},{1,97},{34,2}... | collective-permute-start | bytes 294920 | tf_op jit(solution)/shard_map/ppermute | solution.py:417
  5.2 1.2 copy-done
  6.6 10.7 %fold.1 = (bf16[2,512,2048]{2,1,0:T(8,128)(2,1)}, bf16[2,2048,512]{2,1,0:T(8,128)(2,1)}, f32[2,49,8,128]{3,2,1,0:T(8,128)}) custom-call(bf16[2,512,2048]{2,1,0:T(8,128)(2,1)} %win.1, bf16[2,16,512]{2,1,0:T(8,128)(2,1)} %bitcast.37, bf16[2,16,2048]{2,1,0:T(8,128)(2,1)} %bin_.7, bf16[2,2048,512]{2,1,0:T(8,128)(2,1)} %wout.1, bf16[2,16,2048]{2,1,0:T(8,128)(2,1)} %bitcast.32, ...), custom_call_target="tpu_custom_call" | custom-call | flops 5000000000 | bytes 1000000 | tf_op jit(solution)/shard_map/fold/pallas_call | solution.py:379
  17.5 2.5 %collective-permute-start.2 = (bf16[3,48,512]{2,1,0:T(8,128)(2,1)S(1)}, bf16[3,48,512]{2,1,0:T(8,128)(2,1)S(1)}, u32[]{:S(2)}, u32[]{:S(2)}) collective-permute-start(bf16[3,48,512]{2,1,0:T(8,128)(2,1)S(1)} %get-tuple-element.57), channel_id=1, source_target_pairs={{0,2},{2,4},{4,6},{6,8},{8,10},{10,12},{12,14},{14,16},{16,18},{18... | collective-permute-start | bytes 442376 | tf_op jit(solution)/shard_map/ppermute | solution.py:417
  20.0 1.0 copy-done.14
  21.1 9.2 %conv.3.cv = f32[4096,128]{1,0:T(8,128)S(1)} custom-call(f32[4]{0:T(128)S(1)} %add_convert_fusion.7.flags, bf16[32,32,512]{2,1,0:T(8,128)(2,1)S(1)} %bitcast.26, bf16[3,32,512]{2,1,0:T(8,128)(2,1)S(1)} %collective-permute-done.refs_1_.refs_2_, bf16[3,32,512]{2,1,0:T(8,128)(2,1)S(1)} %collective-permute-done.1.refs_2_.refs_3_, f32[2,49,8,128]{3,2,1,0:T(8,128)S(1)} %copy-done.14), custom_call_target="tpu_custom_call" | custom-call | flops 8000000000 | bytes 1000000 | tf_op jit(solution)/shard_map/conv/pallas_call | solution.py:379
  30.4 7.2 %first_outer.1 = (bf16[1024,512]{1,0:T(8,128)(2,1)S(1)}, bf16[1024,2048]{1,0:T(8,128)(2,1)}, bf16[1024,2048]{1,0:T(8,128)(2,1)S(1)}, bf16[1024,16]{1,0:T(8,128)(...) custom-call(f32[4]{0:T(128)S(1)} %add_convert_fusion.7.flags, ...), custom_call_target="tpu_custom_call" | custom-call | flops 7000000000 | bytes 1000000 | tf_op jit(solution)/shard_map/first_outer/pallas_call | solution.py:379
  37.9 2.6 %collective-permute-start.5 = (bf16[3,32,512]{2,1,0:T(8,128)(2,1)S(1)}, bf16[3,32,512]{2,1,0:T(8,128)(2,1)S(1)}, u32[]{:S(2)}, u32[]{:S(2)}) collective-permute-start(bf16[3,32,512]{2,1,0:T(8,128)(2,1)S(1)} %get-tuple-element.69), channel_id=1, source_target_pairs={{32,0},{64,32},{96,64},{0,96},{33,1},{65,33},{97,65},{1,97},{34,2}... | collective-permute-start | bytes 294920 | tf_op jit(solution)/shard_map/ppermute | solution.py:417
  40.5 6.9 %first_inner.1 = (bf16[1024,512]{1,0:T(8,128)(2,1)S(1)}, bf16[1024,2048]{1,0:T(8,128)(2,1)}, bf16[1024,2048]{1,0:T(8,128)(2,1)S(1)}, bf16[1024,16]{1,0:T(8,128)(...) custom-call(f32[4]{0:T(128)S(1)} %add_convert_fusion.7.flags, ...), custom_call_target="tpu_custom_call", output_to_operand_aliasing={{0}: (14, {}), {1}: (15, {}), {2}: (16, {}), {3}: (17, {}),... | custom-call | flops 7000000000 | bytes 1000000 | tf_op jit(solution)/shard_map/first_inner/pallas_call | solution.py:379
  47.5 2.1 %collective-permute-start.6 = (bf16[3,48,512]{2,1,0:T(8,128)(2,1)S(1)}, bf16[3,48,512]{2,1,0:T(8,128)(2,1)S(1)}, u32[]{:S(2)}, u32[]{:S(2)}) collective-permute-start(bf16[3,48,512]{2,1,0:T(8,128)(2,1)S(1)} %get-tuple-element.74), channel_id=1, source_target_pairs={{0,2},{2,4},{4,6},{6,8},{8,10},{10,12},{12,14},{14,16},{16,18},{18... | collective-permute-start | bytes 442376 | tf_op jit(solution)/shard_map/ppermute | solution.py:417
  49.6 2.7 %collective-permute-start.7 = (bf16[3,48,512]{2,1,0:T(8,128)(2,1)S(1)}, bf16[3,48,512]{2,1,0:T(8,128)(2,1)S(1)}, u32[]{:S(2)}, u32[]{:S(2)}) collective-permute-start(bf16[3,48,512]{2,1,0:T(8,128)(2,1)S(1)} %get-tuple-element.75), channel_id=1, source_target_pairs={{2,0},{4,2},{6,4},{8,6},{10,8},{12,10},{14,12},{16,14},{18,16},{20... | collective-permute-start | bytes 442376 | tf_op jit(solution)/shard_map/ppermute | solution.py:417
  52.4 9.9 %conv.4.cv = f32[4096,128]{1,0:T(8,128)S(1)} custom-call(f32[4]{0:T(128)S(1)} %add_convert_fusion.7.flags, bf16[16,32,512]{2,1,0:T(8,128)(2,1)S(1)} %get-tuple-element.67.refs_0_.x, bf16[16,32,512]{2,1,0:T(8,128)(2,1)S(1)} %get-tuple-element.66.refs_1_.x, bf16[3,32,512]{2,1,0:T(8,128)(2,1)S(1)} %collective-permute-done.4.refs_2_.refs_4_, ...), custom_call_target="tpu_custom_call" | custom-call | flops 8000000000 | bytes 1000000 | tf_op jit(solution)/shard_map/conv/pallas_call | solution.py:379
  62.3 10.5 %second_outer.1 = (bf16[32,32,512]{2,1,0:T(8,128)(2,1)}, f32[16,5120]{1,0:T(8,128)S(1)}, bf16[16,32,512]{2,1,0:T(8,128)(2,1)S(1)}, bf16[3,32,512]{2,1,0:T(8,128)...) custom-call(f32[4]{0:T(128)S(1)} %add_convert_fusion.7.flags, ...), custom_call_target="tpu_custom_call" | custom-call | flops 10000000000 | bytes 1000000 | tf_op jit(solution)/shard_map/second_outer/pallas_call | solution.py:379
  72.7 2.7 %collective-permute-start.9 = (bf16[3,32,512]{2,1,0:T(8,128)(2,1)S(1)}, bf16[3,32,512]{2,1,0:T(8,128)(2,1)S(1)}, u32[]{:S(2)}, u32[]{:S(2)}) collective-permute-start(bf16[3,32,512]{2,1,0:T(8,128)(2,1)S(1)} %get-tuple-element.82), channel_id=1, source_target_pairs={{32,0},{64,32},{96,64},{0,96},{33,1},{65,33},{97,65},{1,97},{34,2}... | collective-permute-start | bytes 294920 | tf_op jit(solution)/shard_map/ppermute | solution.py:417
  75.4 10.2 %second_inner.1 = (bf16[32,32,512]{2,1,0:T(8,128)(2,1)}, f32[16,5120]{1,0:T(8,128)S(1)}, bf16[16,32,512]{2,1,0:T(8,128)(2,1)S(1)}, bf16[3,16,512]{2,1,0:T(8,128)(2,1)S(1)}, bf16[3,16,512]{2,1,0:T(8,128)(2,1)S(1)}) custom-call(f32[4]{0:T(128)S(1)} %add_convert_fusion.7.flags, ...), custom_call_target="tpu_custom_call", output_to_operand_aliasing={{0}: (17, {})} | custom-call | flops 10000000000 | bytes 1000000 | tf_op jit(solution)/shard_map/second_inner/pallas_call | solution.py:379
  85.8 5.9 %collective-permute-start.11 = (bf16[3,48,512]{2,1,0:T(8,128)(2,1)S(1)}, bf16[3,48,512]{2,1,0:T(8,128)(2,1)S(1)}, u32[]{:S(2)}, u32[]{:S(2)}) collective-permute-start(bf16[3,48,512]{2,1,0:T(8,128)(2,1)S(1)} %get-tuple-element.88), channel_id=1, source_target_pairs={{2,0},{4,2},{6,4},{8,6},{10,8},{12,10},{14,12},{16,14},{18,16},{20... | collective-permute-start | bytes 442376 | tf_op jit(solution)/shard_map/ppermute | solution.py:417
  91.7 9.9 %conv.5.cv = f32[4096,128]{1,0:T(8,128)S(1)} custom-call(f32[4]{0:T(128)S(1)} %add_convert_fusion.7.flags, bf16[16,32,512]{2,1,0:T(8,128)(2,1)S(1)} %get-tuple-element.79.refs_0_, bf16[16,32,512]{2,1,0:T(8,128)(2,1)S(1)} %get-tuple-element.80.refs_1_, bf16[3,32,512]{2,1,0:T(8,128)(2,1)S(1)} %collective-permute-done.8.refs_2_.refs_4_, ...), custom_call_target="tpu_custom_call" | custom-call | flops 8000000000 | bytes 1000000 | tf_op jit(solution)/shard_map/conv/pallas_call | solution.py:379
  101.7 9.0 %third.1 = f32[16,5120]{1,0:T(8,128)S(1)} custom-call(f32[4]{0:T(128)S(1)} %add_convert_fusion.7.flags, bf16[32,32,512]{2,1,0:T(8,128)(2,1)S(1)} %bitcast.31, f32[4096,128]{1,0:T(8,128)S(1)} %conv.5.cv, bf16[3,48,512]{2,1,0:T(8,128)(2,1)S(1)} %collective-permute-done.10.w, bf16[3,48,512]{2,1,0:T(8,128)(2,1)S(1)} %collective-permute-done.11.e, ...), custom_call_target="tpu_custom_call" | custom-call | flops 8999999488 | bytes 1000000 | tf_op jit(solution)/shard_map/third/pallas_call | solution.py:379
  110.7 5.1 %collective-permute-start.12 = (bf16[16,5120]{1,0:T(8,128)(2,1)S(1)}, bf16[16,5120]{1,0:T(8,128)(2,1)S(1)}, u32[]{:S(2)}, u32[]{:S(2)}) collective-permute-start(bf16[16,5120]{1,0:T(8,128)(2,1)S(1)} %select_convert_fusion), channel_id=1, source_target_pairs={{0,2},{2,0},{4,6},{6,4},{8,10},{10,8},{12,14},{14,12},{16,18},{18,... | collective-permute-start | bytes 491528 | tf_op jit(solution)/shard_map/ppermute | solution.py:438
  115.9 1.0 collective-permute-done.12
  117.1 4.5 %collective-permute-done.13 = bf16[16,5120]{1,0:T(8,128)(2,1)S(1)} collective-permute-done((bf16[16,5120]{1,0:T(8,128)(2,1)S(1)}, bf16[16,5120]{1,0:T(8,128)(2,1)S(1)}, u32[]{:S(2)}, u32[]{:S(2)}) %collective-permute-start.13) | collective-permute-done | bytes 163872 | tf_op jit(solution)/shard_map/ppermute | solution.py:441
  121.6 6.0 %collective-permute-done.14 = bf16[16,5120]{1,0:T(8,128)(2,1)S(1)} collective-permute-done((bf16[16,5120]{1,0:T(8,128)(2,1)S(1)}, bf16[16,5120]{1,0:T(8,128)(2,1)S(1)}, u32[]{:S(2)}, u32[]{:S(2)}) %collective-permute-start.14) | collective-permute-done | bytes 163872 | tf_op jit(solution)/shard_map/ppermute | solution.py:441
  127.6 0.9 collective-permute-start.15
  128.6 3.3 %collective-permute-done.15 = bf16[16,5120]{1,0:T(8,128)(2,1)S(1)} collective-permute-done((bf16[16,5120]{1,0:T(8,128)(2,1)S(1)}, bf16[16,5120]{1,0:T(8,128)(2,1)S(1)}, u32[]{:S(2)}, u32[]{:S(2)}) %collective-permute-start.15) | collective-permute-done | bytes 163872 | tf_op jit(solution)/shard_map/ppermute | solution.py:441
  131.9 2.4 %collective-permute-start.16 = (bf16[16,5120]{1,0:T(8,128)(2,1)S(1)}, bf16[16,5120]{1,0:T(8,128)(2,1)S(1)}, u32[]{:S(2)}, u32[]{:S(2)}) collective-permute-start(bf16[16,5120]{1,0:T(8,128)(2,1)S(1)} %add_convert_fusion.3), channel_id=1, source_target_pairs={{0,8},{1,9},{2,18},{3,19},{4,12},{5,13},{6,22},{7,23},{8,0},{9,1},... | collective-permute-start | bytes 491528 | tf_op jit(solution)/shard_map/ppermute | solution.py:441
  134.4 3.3 %collective-permute-done.16 = bf16[16,5120]{1,0:T(8,128)(2,1)S(1)} collective-permute-done((bf16[16,5120]{1,0:T(8,128)(2,1)S(1)}, bf16[16,5120]{1,0:T(8,128)(2,1)S(1)}, u32[]{:S(2)}, u32[]{:S(2)}) %collective-permute-start.16) | collective-permute-done | bytes 163872 | tf_op jit(solution)/shard_map/ppermute | solution.py:441
  137.8 4.2 %collective-permute-done.17 = bf16[16,5120]{1,0:T(8,128)(2,1)S(1)} collective-permute-done((bf16[16,5120]{1,0:T(8,128)(2,1)S(1)}, bf16[16,5120]{1,0:T(8,128)(2,1)S(1)}, u32[]{:S(2)}, u32[]{:S(2)}) %collective-permute-start.17) | collective-permute-done | bytes 163872 | tf_op jit(solution)/shard_map/ppermute | solution.py:441
  142.1 5.7 %collective-permute-done.18 = bf16[16,5120]{1,0:T(8,128)(2,1)S(1)} collective-permute-done((bf16[16,5120]{1,0:T(8,128)(2,1)S(1)}, bf16[16,5120]{1,0:T(8,128)(2,1)S(1)}, u32[]{:S(2)}, u32[]{:S(2)}) %collective-permute-start.18) | collective-permute-done | bytes 163872 | tf_op jit(solution)/shard_map/ppermute | solution.py:441
  147.8 6.8 %collective-permute-start.19 = (bf16[16,5120]{1,0:T(8,128)(2,1)S(1)}, bf16[16,5120]{1,0:T(8,128)(2,1)S(1)}, u32[]{:S(2)}, u32[]{:S(2)}) collective-permute-start(bf16[16,5120]{1,0:T(8,128)(2,1)S(1)} %add_convert_fusion), channel_id=1, source_target_pairs={{0,2},{2,0},{4,6},{6,4},{8,10},{10,8},{12,14},{14,12},{16,18},{18,... | collective-permute-start | bytes 491528 | tf_op jit(solution)/shard_map/ppermute | solution.py:443
  154.6 1.0 collective-permute-done.19
  156.0 0.9 multiply_bitcast_fusion
  (72 shorter events, 2.6 us)
Async XLA Ops:
  1.6 15.8 %collective-permute-start.1 = (bf16[3,32,512]{2,1,0:T(8,128)(2,1)S(1)}, bf16[3,32,512]{2,1,0:T(8,128)(2,1)S(1)}, u32[]{:S(2)}, u32[]{:S(2)}) collective-permute-start(bf16[3,32,512]{2,1,0:T(8,128)(2,1)S(1)} %get-tuple-element.101), channel_id=1, source_target_pairs={{32,0},{64,32},{96,64},{0,96},{33,1},{65,33},{97,65},{1,97},{34,2}... | collective-permute-start | bytes 294920 | tf_op jit(solution)/shard_map/ppermute | solution.py:417
  5.2 12.2 %collective-permute-start = (bf16[3,32,512]{2,1,0:T(8,128)(2,1)S(1)}, bf16[3,32,512]{2,1,0:T(8,128)(2,1)S(1)}, u32[]{:S(2)}, u32[]{:S(2)}) collective-permute-start(bf16[3,32,512]{2,1,0:T(8,128)(2,1)S(1)} %get-tuple-element.102), channel_id=1, source_target_pairs={{0,32},{32,64},{64,96},{96,0},{1,33},{33,65},{65,97},{97,1},{2,34}... | collective-permute-start | bytes 294920 | tf_op jit(solution)/shard_map/ppermute | solution.py:417
  6.6 13.4 %copy-start.1 = (bf16[1,32,32,512]{3,2,1,0:T(8,128)(2,1)S(1)}, bf16[1,32,32,512]{3,2,1,0:T(8,128)(2,1)}, u32[]{:S(2)}) copy-start(bf16[1,32,32,512]{3,2,1,0:T(8,128)(2,1)} %param.13) | copy-start | bytes 3145732
  17.5 12.8 %collective-permute-start.2 = (bf16[3,48,512]{2,1,0:T(8,128)(2,1)S(1)}, bf16[3,48,512]{2,1,0:T(8,128)(2,1)S(1)}, u32[]{:S(2)}, u32[]{:S(2)}) collective-permute-start(bf16[3,48,512]{2,1,0:T(8,128)(2,1)S(1)} %get-tuple-element.57), channel_id=1, source_target_pairs={{0,2},{2,4},{4,6},{6,8},{8,10},{10,12},{12,14},{14,16},{16,18},{18... | collective-permute-start | bytes 442376 | tf_op jit(solution)/shard_map/ppermute | solution.py:417
  20.0 10.2 %collective-permute-start.3 = (bf16[3,48,512]{2,1,0:T(8,128)(2,1)S(1)}, bf16[3,48,512]{2,1,0:T(8,128)(2,1)S(1)}, u32[]{:S(2)}, u32[]{:S(2)}) collective-permute-start(bf16[3,48,512]{2,1,0:T(8,128)(2,1)S(1)} %get-tuple-element.58), channel_id=1, source_target_pairs={{2,0},{4,2},{6,4},{8,6},{10,8},{12,10},{14,12},{16,14},{18,16},{20... | collective-permute-start | bytes 442376 | tf_op jit(solution)/shard_map/ppermute | solution.py:417
  21.0 9.3 %copy-start.7 = (f32[2,512]{1,0:T(2,128)S(1)}, f32[2,512]{1,0:T(2,128)}, u32[]{:S(2)}) copy-start(f32[2,512]{1,0:T(2,128)} %bias.7) | copy-start | bytes 12292
  21.0 9.3 %copy-start.8 = (f32[2,512]{1,0:T(2,128)S(1)}, f32[2,512]{1,0:T(2,128)}, u32[]{:S(2)}) copy-start(f32[2,512]{1,0:T(2,128)} %gain.7) | copy-start | bytes 12292
  21.0 9.3 %copy-start.9 = (f32[2,512]{1,0:T(2,128)S(1)}, f32[2,512]{1,0:T(2,128)}, u32[]{:S(2)}) copy-start(f32[2,512]{1,0:T(2,128)} %shift.7) | copy-start | bytes 12292
  21.0 9.3 %copy-start.10 = (f32[2,512]{1,0:T(2,128)S(1)}, f32[2,512]{1,0:T(2,128)}, u32[]{:S(2)}) copy-start(f32[2,512]{1,0:T(2,128)} %scale.9) | copy-start | bytes 12292
  21.1 9.3 %copy-start.11 = (bf16[2,2048,512]{2,1,0:T(8,128)(2,1)S(1)}, bf16[2,2048,512]{2,1,0:T(8,128)(2,1)}, u32[]{:S(2)}) copy-start(bf16[2,2048,512]{2,1,0:T(8,128)(2,1)} %get-tuple-element.60.wout) | copy-start | bytes 12582916
  21.1 9.3 %copy-start.12 = (bf16[2,512,2048]{2,1,0:T(8,128)(2,1)S(1)}, bf16[2,512,2048]{2,1,0:T(8,128)(2,1)}, u32[]{:S(2)}) copy-start(bf16[2,512,2048]{2,1,0:T(8,128)(2,1)} %get-tuple-element.59.win) | copy-start | bytes 12582916
  21.1 9.3 %copy-start.15 = (f32[2,49,8,128]{3,2,1,0:T(8,128)S(1)}, f32[2,49,8,128]{3,2,1,0:T(8,128)}, u32[]{:S(2)}) copy-start(f32[2,49,8,128]{3,2,1,0:T(8,128)} %get-tuple-element.50.refs_3_.taps.refs_4_) | copy-start | bytes 1204228
  37.6 9.9 %collective-permute-start.4 = (bf16[3,32,512]{2,1,0:T(8,128)(2,1)S(1)}, bf16[3,32,512]{2,1,0:T(8,128)(2,1)S(1)}, u32[]{:S(2)}, u32[]{:S(2)}) collective-permute-start(bf16[3,32,512]{2,1,0:T(8,128)(2,1)S(1)} %get-tuple-element.68), channel_id=1, source_target_pairs={{0,32},{32,64},{64,96},{96,0},{1,33},{33,65},{65,97},{97,1},{2,34}... | collective-permute-start | bytes 294920 | tf_op jit(solution)/shard_map/ppermute | solution.py:417
  37.9 9.6 %collective-permute-start.5 = (bf16[3,32,512]{2,1,0:T(8,128)(2,1)S(1)}, bf16[3,32,512]{2,1,0:T(8,128)(2,1)S(1)}, u32[]{:S(2)}, u32[]{:S(2)}) collective-permute-start(bf16[3,32,512]{2,1,0:T(8,128)(2,1)S(1)} %get-tuple-element.69), channel_id=1, source_target_pairs={{32,0},{64,32},{96,64},{0,96},{33,1},{65,33},{97,65},{1,97},{34,2}... | collective-permute-start | bytes 294920 | tf_op jit(solution)/shard_map/ppermute | solution.py:417
  47.5 14.7 %collective-permute-start.6 = (bf16[3,48,512]{2,1,0:T(8,128)(2,1)S(1)}, bf16[3,48,512]{2,1,0:T(8,128)(2,1)S(1)}, u32[]{:S(2)}, u32[]{:S(2)}) collective-permute-start(bf16[3,48,512]{2,1,0:T(8,128)(2,1)S(1)} %get-tuple-element.74), channel_id=1, source_target_pairs={{0,2},{2,4},{4,6},{6,8},{8,10},{10,12},{12,14},{14,16},{16,18},{18... | collective-permute-start | bytes 442376 | tf_op jit(solution)/shard_map/ppermute | solution.py:417
  49.6 12.6 %collective-permute-start.7 = (bf16[3,48,512]{2,1,0:T(8,128)(2,1)S(1)}, bf16[3,48,512]{2,1,0:T(8,128)(2,1)S(1)}, u32[]{:S(2)}, u32[]{:S(2)}) collective-permute-start(bf16[3,48,512]{2,1,0:T(8,128)(2,1)S(1)} %get-tuple-element.75), channel_id=1, source_target_pairs={{2,0},{4,2},{6,4},{8,6},{10,8},{12,10},{14,12},{16,14},{18,16},{20... | collective-permute-start | bytes 442376 | tf_op jit(solution)/shard_map/ppermute | solution.py:417
  52.4 9.9 %copy-start.2 = (bf16[1,32,32,512]{3,2,1,0:T(8,128)(2,1)S(1)}, bf16[1,32,32,512]{3,2,1,0:T(8,128)(2,1)}, u32[]{:S(2)}) copy-start(bf16[1,32,32,512]{3,2,1,0:T(8,128)(2,1)} %param.14) | copy-start | bytes 3145732
  52.4 9.9 %copy-start.4 = (bf16[2,16,2048]{2,1,0:T(8,128)(2,1)S(1)}, bf16[2,16,2048]{2,1,0:T(8,128)(2,1)}, u32[]{:S(2)}) copy-start(bf16[2,16,2048]{2,1,0:T(8,128)(2,1)} %bin_.7) | copy-start | bytes 393220
  52.4 9.9 %copy-start.6 = (bf16[2,16,512]{2,1,0:T(8,128)(2,1)S(1)}, bf16[2,16,512]{2,1,0:T(8,128)(2,1)}, u32[]{:S(2)}) copy-start(bf16[2,16,512]{2,1,0:T(8,128)(2,1)} %bout.7) | copy-start | bytes 98308
  72.7 12.9 %collective-permute-start.8 = (bf16[3,32,512]{2,1,0:T(8,128)(2,1)S(1)}, bf16[3,32,512]{2,1,0:T(8,128)(2,1)S(1)}, u32[]{:S(2)}, u32[]{:S(2)}) collective-permute-start(bf16[3,32,512]{2,1,0:T(8,128)(2,1)S(1)} %get-tuple-element.81), channel_id=1, source_target_pairs={{0,32},{32,64},{64,96},{96,0},{1,33},{33,65},{65,97},{97,1},{2,34}... | collective-permute-start | bytes 294920 | tf_op jit(solution)/shard_map/ppermute | solution.py:417
  72.7 12.9 %collective-permute-start.9 = (bf16[3,32,512]{2,1,0:T(8,128)(2,1)S(1)}, bf16[3,32,512]{2,1,0:T(8,128)(2,1)S(1)}, u32[]{:S(2)}, u32[]{:S(2)}) collective-permute-start(bf16[3,32,512]{2,1,0:T(8,128)(2,1)S(1)} %get-tuple-element.82), channel_id=1, source_target_pairs={{32,0},{64,32},{96,64},{0,96},{33,1},{65,33},{97,65},{1,97},{34,2}... | collective-permute-start | bytes 294920 | tf_op jit(solution)/shard_map/ppermute | solution.py:417
  85.7 16.0 %collective-permute-start.10 = (bf16[3,48,512]{2,1,0:T(8,128)(2,1)S(1)}, bf16[3,48,512]{2,1,0:T(8,128)(2,1)S(1)}, u32[]{:S(2)}, u32[]{:S(2)}) collective-permute-start(bf16[3,48,512]{2,1,0:T(8,128)(2,1)S(1)} %get-tuple-element.87), channel_id=1, source_target_pairs={{0,2},{2,4},{4,6},{6,8},{8,10},{10,12},{12,14},{14,16},{16,18},{18... | collective-permute-start | bytes 442376 | tf_op jit(solution)/shard_map/ppermute | solution.py:417
  85.8 15.9 %collective-permute-start.11 = (bf16[3,48,512]{2,1,0:T(8,128)(2,1)S(1)}, bf16[3,48,512]{2,1,0:T(8,128)(2,1)S(1)}, u32[]{:S(2)}, u32[]{:S(2)}) collective-permute-start(bf16[3,48,512]{2,1,0:T(8,128)(2,1)S(1)} %get-tuple-element.88), channel_id=1, source_target_pairs={{2,0},{4,2},{6,4},{8,6},{10,8},{12,10},{14,12},{16,14},{18,16},{20... | collective-permute-start | bytes 442376 | tf_op jit(solution)/shard_map/ppermute | solution.py:417
  91.7 10.0 %copy-start.13 = (bf16[1024,2048]{1,0:T(8,128)(2,1)S(1)}, bf16[1024,2048]{1,0:T(8,128)(2,1)}, u32[]{:S(2)}) copy-start(bf16[1024,2048]{1,0:T(8,128)(2,1)} %get-tuple-element.92.hid_far) | copy-start | bytes 12582916
  110.7 6.2 %collective-permute-start.12 = (bf16[16,5120]{1,0:T(8,128)(2,1)S(1)}, bf16[16,5120]{1,0:T(8,128)(2,1)S(1)}, u32[]{:S(2)}, u32[]{:S(2)}) collective-permute-start(bf16[16,5120]{1,0:T(8,128)(2,1)S(1)} %select_convert_fusion), channel_id=1, source_target_pairs={{0,2},{2,0},{4,6},{6,4},{8,10},{10,8},{12,14},{14,12},{16,18},{18,... | collective-permute-start | bytes 491528 | tf_op jit(solution)/shard_map/ppermute | solution.py:438
  117.0 4.5 %collective-permute-start.13 = (bf16[16,5120]{1,0:T(8,128)(2,1)S(1)}, bf16[16,5120]{1,0:T(8,128)(2,1)S(1)}, u32[]{:S(2)}, u32[]{:S(2)}) collective-permute-start(bf16[16,5120]{1,0:T(8,128)(2,1)S(1)} %add_convert_fusion.6), channel_id=1, source_target_pairs={{0,32},{1,33},{2,6},{3,7},{4,36},{5,37},{6,2},{7,3},{8,40},{9,41},... | collective-permute-start | bytes 491528 | tf_op jit(solution)/shard_map/ppermute | solution.py:441
  121.6 6.0 %collective-permute-start.14 = (bf16[16,5120]{1,0:T(8,128)(2,1)S(1)}, bf16[16,5120]{1,0:T(8,128)(2,1)S(1)}, u32[]{:S(2)}, u32[]{:S(2)}) collective-permute-start(bf16[16,5120]{1,0:T(8,128)(2,1)S(1)} %add_convert_fusion.5), channel_id=1, source_target_pairs={{0,64},{1,65},{2,10},{3,11},{4,68},{5,69},{6,14},{7,15},{8,72},{9,... | collective-permute-start | bytes 491528 | tf_op jit(solution)/shard_map/ppermute | solution.py:441
  127.6 4.2 %collective-permute-start.15 = (bf16[16,5120]{1,0:T(8,128)(2,1)S(1)}, bf16[16,5120]{1,0:T(8,128)(2,1)S(1)}, u32[]{:S(2)}, u32[]{:S(2)}) collective-permute-start(bf16[16,5120]{1,0:T(8,128)(2,1)S(1)} %add_convert_fusion.4), channel_id=1, source_target_pairs={{0,4},{1,5},{2,3},{3,2},{4,0},{5,1},{6,7},{7,6},{8,12},{9,13},{10,... | collective-permute-start | bytes 491528 | tf_op jit(solution)/shard_map/ppermute | solution.py:441
  131.9 5.8 %collective-permute-start.16 = (bf16[16,5120]{1,0:T(8,128)(2,1)S(1)}, bf16[16,5120]{1,0:T(8,128)(2,1)S(1)}, u32[]{:S(2)}, u32[]{:S(2)}) collective-permute-start(bf16[16,5120]{1,0:T(8,128)(2,1)S(1)} %add_convert_fusion.3), channel_id=1, source_target_pairs={{0,8},{1,9},{2,18},{3,19},{4,12},{5,13},{6,22},{7,23},{8,0},{9,1},... | collective-permute-start | bytes 491528 | tf_op jit(solution)/shard_map/ppermute | solution.py:441
  137.7 4.2 %collective-permute-start.17 = (bf16[16,5120]{1,0:T(8,128)(2,1)S(1)}, bf16[16,5120]{1,0:T(8,128)(2,1)S(1)}, u32[]{:S(2)}, u32[]{:S(2)}) collective-permute-start(bf16[16,5120]{1,0:T(8,128)(2,1)S(1)} %add_convert_fusion.2), channel_id=1, source_target_pairs={{0,1},{1,0},{2,34},{3,35},{4,5},{5,4},{6,38},{7,39},{8,9},{9,8},{1... | collective-permute-start | bytes 491528 | tf_op jit(solution)/shard_map/ppermute | solution.py:441
  142.0 5.8 %collective-permute-start.18 = (bf16[16,5120]{1,0:T(8,128)(2,1)S(1)}, bf16[16,5120]{1,0:T(8,128)(2,1)S(1)}, u32[]{:S(2)}, u32[]{:S(2)}) collective-permute-start(bf16[16,5120]{1,0:T(8,128)(2,1)S(1)} %add_convert_fusion.1), channel_id=1, source_target_pairs={{0,16},{1,17},{2,66},{3,67},{4,20},{5,21},{6,70},{7,71},{8,24},{9,... | collective-permute-start | bytes 491528 | tf_op jit(solution)/shard_map/ppermute | solution.py:441
  147.8 7.8 %collective-permute-start.19 = (bf16[16,5120]{1,0:T(8,128)(2,1)S(1)}, bf16[16,5120]{1,0:T(8,128)(2,1)S(1)}, u32[]{:S(2)}, u32[]{:S(2)}) collective-permute-start(bf16[16,5120]{1,0:T(8,128)(2,1)S(1)} %add_convert_fusion), channel_id=1, source_target_pairs={{0,2},{2,0},{4,6},{6,4},{8,10},{10,8},{12,14},{14,12},{16,18},{18,... | collective-permute-start | bytes 491528 | tf_op jit(solution)/shard_map/ppermute | solution.py:443
  (4 other events, 20.7 us)
